TPU v7x, 128 devices: a whole 4x4x4 slice. The times are simulated.
128 devices in a mesh: row: 16 (over z, y), col: 8 (over x, core).
Axes of the slice: x: 4, y: 4, z: 4, core: 2. Of those that a mesh axis runs over, the one named last changes fastest.
Arguments:
- patches: bfloat16 [128, 128, 384], P('row', 'col'), may hold values from -10 to 10
- tissue: int32 [128, 128], P('row', 'col'), may hold values from 0 to 1
- in_weight: bfloat16 [384, 1536], replicated, may hold values from -0.3125 to 0.3125
- conv_weight: float32 [3, 3, 768], replicated, may hold values from -2 to 2
- conv_bias: float32 [768], replicated, may hold values from -3 to 3
- x_weight: bfloat16 [768, 224], replicated, may hold values from -0.21875 to 0.21875
- dt_weight: bfloat16 [4, 24, 768], replicated, may hold values from -1.25 to 1.25
- dt_bias: float32 [4, 768], replicated, may hold values from -5.5 to -3.5
- decay_rate: float32 [4, 768, 16], replicated, may hold values from 0.0001 to 4
- skip_gain: float32 [768], replicated, may hold values from 0.5 to 2
- norm_gain: float32 [768], replicated, may hold values from 0.1 to 1.9
- out_weight: bfloat16 [768, 384], replicated, may hold values from -0.21875 to 0.21875
Outputs:
- result: bfloat16 [128, 128, 384], P('row', 'col')
All inputs are finite; a program needn't handle non-finite values.
Results may differ from a plain program's by a relative error of at most 0.0076.
Values may be sent and summed in bfloat16 or wider, within the bound.
No kernel may reach another device: no remote copies, remote signals or barrier semaphores. Data moves between devices by JAX's collectives and lax.ppermute only.
A program may use at most 256 MiB of HBM per device.

v0:
```python
import jax
import jax.numpy as jnp
from jax import lax
from jax.sharding import PartitionSpec as P


def entering(part, axis, combine, identity, reverse):
    count = lax.axis_size(axis)
    place = lax.axis_index(axis)
    ahead = count - 1 - place if reverse else place
    gathered = jax.tree.map(lambda a: lax.all_gather(a, axis), part)
    state = jax.tree.map(lambda a, e: jnp.zeros_like(a) + jnp.asarray(e, a.dtype), part, identity)

    def one(step, state):
        source = count - 1 - step if reverse else step
        return combine(
            state, jax.tree.map(lambda a: lax.dynamic_index_in_dim(a, source, 0, False), gathered)
        )

    return lax.fori_loop(0, ahead, one, state)


def spread(block, axis, holder):
    block = jnp.where(lax.axis_index(axis) == holder, block, jnp.zeros_like(block))
    return lax.psum(block, axis)


def padded(cells, sides, width):
    for axis, dim in sides:
        count = lax.axis_size(axis)
        ends = count - 1
        head = lax.slice_in_dim(cells, 0, width, axis=dim)
        tail = lax.slice_in_dim(cells, cells.shape[dim] - width, cells.shape[dim], axis=dim)
        cells = jnp.concatenate(
            [
                lax.ppermute(tail, axis, [(i, (i + 1) % count) for i in range(ends)]),
                cells,
                lax.ppermute(head, axis, [((i + 1) % count, i) for i in range(ends)]),
            ],
            axis=dim,
        )
    return cells


def make_combine(decays):

    def combine(earlier, following):
        return (
            earlier[0] + following[0],
            jnp.exp(-decays * following[0][..., None, :]) * earlier[1] + following[1],
        )

    return combine


def ordered_prefix(combine, parts, backward):
    if backward:
        parts = tuple((member[::-1] for member in parts))
    inclusive = lax.associative_scan(combine, parts)
    exclusive = tuple(
        (jnp.concatenate([jnp.zeros_like(member[:1]), member[:-1]], axis=0) for member in inclusive)
    )
    whole = tuple((member[-1] for member in inclusive))
    if backward:
        exclusive = tuple((member[::-1] for member in exclusive))
    return (exclusive, whole)


def row_chain(segment, combine, backward):
    neutral = tuple((jnp.zeros_like(member) for member in segment))
    inner_prefix = entering(segment, "col", combine, neutral, backward)
    root_index = 0 if backward else lax.axis_size("col") - 1
    whole = jax.tree.map(
        lambda part: spread(part, "col", root_index), combine(inner_prefix, segment)
    )
    local_prefix, device_total = ordered_prefix(combine, whole, backward)
    neutral_total = tuple((jnp.zeros_like(member) for member in device_total))
    outer_prefix = entering(device_total, "row", combine, neutral_total, backward)
    lifted = (outer_prefix[0][None], outer_prefix[1][None])
    return combine(combine(lifted, local_prefix), inner_prefix)


def col_chain(segment, combine, backward):
    neutral = tuple((jnp.zeros_like(member) for member in segment))
    inner_prefix = entering(segment, "row", combine, neutral, backward)
    root_index = 0 if backward else lax.axis_size("row") - 1
    whole = jax.tree.map(
        lambda part: spread(part, "row", root_index), combine(inner_prefix, segment)
    )
    local_prefix, device_total = ordered_prefix(combine, whole, backward)
    neutral_total = tuple((jnp.zeros_like(member) for member in device_total))
    outer_prefix = entering(device_total, "col", combine, neutral_total, backward)
    lifted = (outer_prefix[0][None], outer_prefix[1][None])
    return combine(combine(lifted, local_prefix), inner_prefix)


def local_layout(values, columns_first, backward):
    arranged = values if columns_first else jnp.transpose(values, (1, 0, 2))
    if backward:
        arranged = arranged[::-1]
    return arranged


def tile_layout(arranged, columns_first, backward):
    if backward:
        arranged = arranged[::-1]
    return arranged if columns_first else jnp.transpose(arranged, (1, 0, 2))


def segment_totals(steps_dt, inputs_du, b_coeffs, decays):

    def advance(carried, inputs):
        delta, driven, b_row = inputs
        sums, states = carried
        states = (
            jnp.exp(-decays * delta[:, None, :]) * states + driven[:, None, :] * b_row[:, :, None]
        )
        return ((sums + delta, states), None)

    width_seg = steps_dt.shape[1]
    start = (
        jnp.zeros((width_seg, decays.shape[1]), jnp.float32),
        jnp.zeros((width_seg,) + decays.shape, jnp.float32),
    )
    totals, unused = lax.scan(advance, start, (steps_dt, inputs_du, b_coeffs))
    return totals


def segment_outputs(entry, steps_dt, inputs_du, b_coeffs, c_coeffs, decays):

    def advance(states, inputs):
        delta, driven, b_row, c_row = inputs
        states = (
            jnp.exp(-decays * delta[:, None, :]) * states + driven[:, None, :] * b_row[:, :, None]
        )
        return (states, jnp.sum(states * c_row[:, :, None], axis=1))

    final_states, outputs = lax.scan(advance, entry, (steps_dt, inputs_du, b_coeffs, c_coeffs))
    return outputs


def per_device(
    patches,
    tissue,
    in_weight,
    conv_weight,
    conv_bias,
    x_weight,
    dt_weight,
    dt_bias,
    decay_rate,
    skip_gain,
    norm_gain,
    out_weight,
):
    tile_rows, tile_cols, channels = patches.shape
    inner_width = out_weight.shape[0]
    state_width = decay_rate.shape[2]
    rank_width = dt_weight.shape[1]
    token_count = tile_rows * tile_cols
    flattened = patches.reshape(token_count, channels)
    projected = jnp.dot(flattened, in_weight, preferred_element_type=jnp.float32)
    x_inner = (
        projected[:, :inner_width].astype(jnp.bfloat16).reshape(tile_rows, tile_cols, inner_width)
    )
    gate_half = projected[:, inner_width:].astype(jnp.bfloat16)
    framed = padded(x_inner, (("row", 0), ("col", 1)), 1).astype(jnp.float32)
    conv_sum = jnp.zeros((tile_rows, tile_cols, inner_width), jnp.float32) + conv_bias
    for offset_row in range(3):
        for offset_col in range(3):
            conv_sum = (
                conv_sum
                + framed[offset_row : offset_row + tile_rows, offset_col : offset_col + tile_cols]
                * conv_weight[offset_row, offset_col]
            )
    activated = jax.nn.silu(conv_sum).astype(jnp.bfloat16).reshape(token_count, inner_width)
    scan_proj = jnp.dot(activated, x_weight, preferred_element_type=jnp.float32)
    tissue_live = tissue.reshape(token_count, 1).astype(jnp.float32)
    activated_wide = activated.astype(jnp.float32)
    width_each = rank_width + 2 * state_width
    combined = jnp.zeros((token_count, inner_width), jnp.float32)
    for direction in range(4):
        section = scan_proj[:, direction * width_each : (direction + 1) * width_each]
        low_rank = section[:, :rank_width].astype(jnp.bfloat16)
        steps_dt = (
            jax.nn.softplus(
                jnp.dot(low_rank, dt_weight[direction], preferred_element_type=jnp.float32)
                + dt_bias[direction]
            )
            * tissue_live
        )
        inputs_du = steps_dt * activated_wide
        b_coeffs = section[:, rank_width : rank_width + state_width]
        c_coeffs = section[:, rank_width + state_width :]
        columns_first = direction >= 2
        backward = direction % 2 == 1
        layout = [
            local_layout(member.reshape(tile_rows, tile_cols, -1), columns_first, backward)
            for member in (steps_dt, inputs_du, b_coeffs, c_coeffs)
        ]
        decays = jnp.transpose(decay_rate[direction], (1, 0))
        combine = make_combine(decays)
        segment = segment_totals(layout[0], layout[1], layout[2], decays)
        if columns_first:
            entry = col_chain(segment, combine, backward)
        else:
            entry = row_chain(segment, combine, backward)
        outputs = segment_outputs(entry[1], layout[0], layout[1], layout[2], layout[3], decays)
        combined = combined + tile_layout(outputs, columns_first, backward).reshape(
            token_count, inner_width
        )
    combined = combined + skip_gain * activated_wide
    mean_value = jnp.mean(combined, axis=1, keepdims=True)
    centered = combined - mean_value
    variance = jnp.mean(centered * centered, axis=1, keepdims=True)
    normed = centered * lax.rsqrt(variance + 1e-05) * norm_gain
    mixed = (normed * jax.nn.silu(gate_half.astype(jnp.float32))).astype(jnp.bfloat16)
    result = jnp.dot(mixed, out_weight, preferred_element_type=jnp.float32) * tissue_live
    return result.astype(jnp.bfloat16).reshape(tile_rows, tile_cols, channels)


def solution(mesh):
    in_specs = (
        P("row", "col", None),
        P("row", "col"),
        P(),
        P(),
        P(),
        P(),
        P(),
        P(),
        P(),
        P(),
        P(),
        P(),
    )
    out_specs = P("row", "col", None)
    return jax.shard_map(
        per_device, mesh=mesh, in_specs=in_specs, out_specs=out_specs, check_vma=False
    )
```

profile of v0, /device:TPU:120, one launch (start us, length us, event | category | flops | bytes accessed | tf_op | source)
XLA Modules:
  0.0 946.8 jit_solution(16673459941629093007)
XLA Ops:
  33.2 14.3 %while.241 = (s32[]{:T(128)}, f32[8,768]{1,0:T(8,128)S(1)}, f32[8,16,768]{2,1,0:T(8,128)S(1)}, f32[16,8,768]{2,1,0:T(8,128)}, f32[1,16,768]{2,1,0:T(8,128)S(1)},...) while((s32[]{:T(128)}, f32[8,768]{1,0:T(8,128)S(1)}, ...), condition=%wide.region_12.13_spmd.clone, body=%wide.region_11.12_spmd.clone.sunk | while | flops 503811 | bytes 1033844 | solution.py:125
  53.9 14.2 %all-gather.2 = f32[64,768]{1,0:T(8,128)S(1)} all-gather(f32[8,768]{1,0:T(8,128)S(1)} %get-tuple-element.1473), channel_id=4, replica_groups=mesh['row'=16,'col'=8] {'col'}, dimensions={0}, use_global_device_ids=true | all-gather | bytes 221184 | tf_op jit(solution)/shard_map/all_gather | solution.py:11
  68.1 14.1 %all-gather = f32[64,768]{1,0:T(8,128)} all-gather(f32[8,768]{1,0:T(8,128)S(1)} %get-tuple-element.1467), channel_id=2, replica_groups=mesh['row'=16,'col'=8] {'col'}, dimensions={0}, use_global_device_ids=true | all-gather | bytes 221184 | tf_op jit(solution)/shard_map/all_gather | solution.py:11
  91.2 20.4 %all-gather.17.cloned.1.call-done = f32[64,16,768]{2,1,0:T(8,128)} async-done(((f32[8,16,768]{2,1,0:T(8,128)}), f32[64,16,768]{2,1,0:T(8,128)}) %all-gather.17.cloned.1.call-update) | async-done | bytes 3145744 | tf_op jit(solution)/shard_map/all_gather | solution.py:11
  114.5 21.0 %while.242 = (s32[]{:T(128)}, f32[16,768]{1,0:T(8,128)S(1)}, f32[16,16,768]{2,1,0:T(8,128)S(1)}, f32[8,16,768]{2,1,0:T(8,128)}, f32[1,16,768]{2,1,0:T(8,128)S(1)...) while((s32[]{:T(128)}, f32[16,768]{1,0:T(8,128)S(1)}, ...), condition=%wide.region_23.24_spmd.clone, body=%wide.region_22.23_spmd.clone.sunk | while | flops 1007619 | bytes 2018420 | solution.py:125
  146.4 23.7 %all-gather.4 = f32[256,768]{1,0:T(8,128)S(1)} all-gather(f32[16,768]{1,0:T(8,128)S(1)} %get-tuple-element.1479), channel_id=6, replica_groups=mesh['row'=16,'col'=8] {'row'}, dimensions={0}, use_global_device_ids=true | all-gather | bytes 835584 | tf_op jit(solution)/shard_map/all_gather | solution.py:11
  170.2 27.2 %all-gather.6 = f32[256,768]{1,0:T(8,128)} all-gather(f32[16,768]{1,0:T(8,128)S(1)} %get-tuple-element.1485), channel_id=8, replica_groups=mesh['row'=16,'col'=8] {'row'}, dimensions={0}, use_global_device_ids=true | all-gather | bytes 835584 | tf_op jit(solution)/shard_map/all_gather | solution.py:11
  197.5 35.3 %all-reduce.66 = (f32[8,768]{1,0:T(8,128)S(1)}, f32[8,768]{1,0:T(8,128)S(1)}) all-reduce(f32[8,768]{1,0:T(8,128)S(1)} %add_select_fusion.7, f32[8,768]{1,0:T(8,128)S(1)} %add_select_fusion.6), channel_id=1, replica_groups=mesh['row'=16,'col'=8] {'col'}, use_global_device_ids=true, to_apply=%region_4.5 | all-reduce | flops 12288 | bytes 98304 | tf_op jit(solution)/shard_map/psum | solution.py:25
  249.0 25.1 %while.234 = (s32[]{:T(128)}, f32[16,768]{1,0:T(8,128)S(1)}, f32[16,16,768]{2,1,0:T(8,128)S(1)}, s32[]{:T(128)}, f32[16,16,768]{2,1,0:T(8,128)S(1)}, /*index=5*/...) while((s32[]{:T(128)}, f32[16,768]{1,0:T(8,128)S(1)}, ...), condition=%wide.region_25.26_spmd, body=%wide.region_24.25_spmd.sunk | while | flops 602117 | bytes 2654351 | solution.py:20
  274.1 61.3 %all-gather.23.cloned.1.call-done = f32[256,16,768]{2,1,0:T(8,128)} async-done(((f32[16,16,768]{2,1,0:T(8,128)}), f32[256,16,768]{2,1,0:T(8,128)}) %all-gather.23.cloned.1.call-update) | async-done | bytes 12582928 | tf_op jit(solution)/shard_map/all_gather | solution.py:11
  343.2 120.4 %all-reduce.72.cloned.1.call-done = (f32[16,768]{1,0:T(8,128)}, f32[16,768]{1,0:T(8,128)}) async-done(((f32[16,768]{1,0:T(8,128)}, f32[16,768]{1,0:T(8,128)}), (f32[16,768]{1,0:T(8,128)}, f32[16,768]{1,0:T(8,128)})) %all-reduce.72.cloned.1.call-update) | async-done | bytes 98320 | tf_op jit(solution)/shard_map/psum | solution.py:25
  473.6 21.5 %all-gather.9 = f32[16,1,768]{2,1,0:T(1,128)S(1)} all-gather(f32[1,1,768]{2,1,0:T(1,128)S(1)} %get-tuple-element.1970), channel_id=1, replica_groups=mesh['row'=16,'col'=8] {'row'}, dimensions={0}, use_global_device_ids=true | all-gather | bytes 52224 | tf_op jit(solution)/shard_map/all_gather | solution.py:11
  495.7 22.5 %all-gather.8 = f32[16,1,768]{2,1,0:T(1,128)S(1)} all-gather(f32[1,1,768]{2,1,0:T(1,128)S(1)} %get-tuple-element.1971), channel_id=1, replica_groups=mesh['row'=16,'col'=8] {'row'}, dimensions={0}, use_global_device_ids=true | all-gather | bytes 52224 | tf_op jit(solution)/shard_map/all_gather | solution.py:11
  518.9 13.0 %all-gather.10 = f32[8,1,768]{2,1,0:T(1,128)S(1)} all-gather(f32[1,1,768]{2,1,0:T(1,128)S(1)} %get-tuple-element.1973), channel_id=1, replica_groups=mesh['row'=16,'col'=8] {'col'}, dimensions={0}, use_global_device_ids=true | all-gather | bytes 27648 | tf_op jit(solution)/shard_map/all_gather | solution.py:11
  534.6 12.7 %all-gather.11 = f32[8,1,768]{2,1,0:T(1,128)S(1)} all-gather(f32[1,1,768]{2,1,0:T(1,128)S(1)} %get-tuple-element.1972), channel_id=1, replica_groups=mesh['row'=16,'col'=8] {'col'}, dimensions={0}, use_global_device_ids=true | all-gather | bytes 27648 | tf_op jit(solution)/shard_map/all_gather | solution.py:11
  598.9 25.4 %all_gather.83 = f32[16,16,768]{2,1,0:T(8,128)} all-gather(f32[1,16,768]{2,1,0:T(8,128)S(1)} %slice_add_fusion.14), channel_id=1, replica_groups=mesh['row'=16,'col'=8] {'row'}, dimensions={0}, use_global_device_ids=true | all-gather | bytes 835584 | tf_op jit(solution)/shard_map/all_gather | solution.py:11
  628.4 54.2 %while.233 = (s32[]{:T(128)}, f32[8,16,768]{2,1,0:T(8,128)S(1)}, f32[16,8,768]{2,0,1:T(8,128)}, f32[1,16,768]{2,1,0:T(8,128)S(1)}, f32[16,8,768]{2,1,0:T(8,128)}...) while((s32[]{:T(128)}, f32[8,16,768]{2,1,0:T(8,128)S(1)}, ...), condition=%wide.region_21.22_spmd, body=%wide.region_19.21_spmd.sunk | while | flops 583682 | bytes 1109105 | solution.py:138
  691.9 48.1 %all_gather.77 = f32[16,16,768]{2,1,0:T(8,128)} all-gather(f32[1,16,768]{2,1,0:T(8,128)S(1)} %slice_add_fusion.16), channel_id=1, replica_groups=mesh['row'=16,'col'=8] {'row'}, dimensions={0}, use_global_device_ids=true | all-gather | bytes 835584 | tf_op jit(solution)/shard_map/all_gather | solution.py:11
  740.0 24.3 %while.229 = (s32[]{:T(128)}, f32[16,768]{1,0:T(8,128)S(1)}, s32[]{:T(128)}, f32[16,768]{1,0:T(8,128)}, f32[16,768]{1,0:T(8,128)S(1)}, /*index=5*/f32[16,16,768]{2,1,0:T(8,128)}, s32[]{:T(128)}, s32[]{:T(128)}, s32[]{:T(128)}) while((s32[]{:T(128)}, f32[16,768]{1,0:T(8,128)S(1)}, s32[]{:T(128)}, f32[16,768]{1,0:T(8,128)}, ...), condition=%wide.region_7.8_spmd, body=%wide.region_6.7_spmd.sunk | while | flops 36869 | bytes 205959 | solution.py:20
  769.0 54.1 %while.230 = (s32[]{:T(128)}, f32[8,16,768]{2,1,0:T(8,128)S(1)}, f32[16,8,768]{2,0,1:T(8,128)}, f32[1,16,768]{2,1,0:T(8,128)S(1)}, f32[16,8,768]{2,1,0:T(8,128)}...) while((s32[]{:T(128)}, f32[8,16,768]{2,1,0:T(8,128)S(1)}, ...), condition=%wide.region_10.11_spmd, body=%wide.region_8.10_spmd.sunk | while | flops 583682 | bytes 1109105 | solution.py:138
  831.8 14.5 %all_gather.89 = f32[8,16,768]{2,1,0:T(8,128)} all-gather(f32[1,16,768]{2,1,0:T(8,128)S(1)} %slice_add_fusion.11), channel_id=1, replica_groups=mesh['row'=16,'col'=8] {'col'}, dimensions={0}, use_global_device_ids=true | all-gather | bytes 442368 | tf_op jit(solution)/shard_map/all_gather | solution.py:11
  851.5 16.8 %while.236 = (s32[]{:T(128)}, f32[16,16,768]{2,1,0:T(8,128)S(1)}, f32[8,16,768]{2,1,0:T(8,128)S(1)}, f32[1,16,768]{2,1,0:T(8,128)S(1)}, f32[8,16,768]{2,1,0:T(8,...) while((s32[]{:T(128)}, f32[16,16,768]{2,1,0:T(8,128)S(1)}, ...), condition=%wide.region_32.33_spmd, body=%wide.region_30.32_spmd.sunk | while | flops 1167362 | bytes 2070633 | solution.py:138
  881.9 23.7 %all_gather.95 = f32[8,16,768]{2,1,0:T(8,128)S(1)} all-gather(f32[1,16,768]{2,1,0:T(8,128)S(1)} %slice_add_fusion.8), channel_id=1, replica_groups=mesh['row'=16,'col'=8] {'col'}, dimensions={0}, use_global_device_ids=true | all-gather | bytes 442368 | tf_op jit(solution)/shard_map/all_gather | solution.py:11
  917.4 16.7 %while.239 = (s32[]{:T(128)}, f32[16,16,768]{2,1,0:T(8,128)S(1)}, f32[8,16,768]{2,1,0:T(8,128)S(1)}, f32[1,16,768]{2,1,0:T(8,128)S(1)}, f32[8,16,768]{2,1,0:T(8,...) while((s32[]{:T(128)}, f32[16,16,768]{2,1,0:T(8,128)S(1)}, ...), condition=%wide.region_43.44_spmd, body=%wide.region_41.43_spmd.sunk | while | flops 1167362 | bytes 2070633 | solution.py:138
  (1086 shorter events, 448.3 us)
Async XLA Ops:
  7.4 74.8 %all-gather.19.cloned.1.call-start = ((), (), s32[]{:S(2)}) async-start(), calls=%async_computation.1 | async-start | bytes 3538944 | tf_op jit(solution)/shard_map/all_gather | solution.py:11
  9.9 8.6 collective-permute-start
  11.4 7.2 collective-permute-start.1
  17.5 229.9 %copy-start.21 = (f32[16,768]{1,0:T(8,128)}, f32[16,768]{1,0:T(8,128)S(1)}, u32[]{:S(2)}) copy-start(f32[16,768]{1,0:T(8,128)S(1)} %get-tuple-element.3112) | copy-start | bytes 147460
  17.5 230.7 %copy-start.23 = (f32[16,768]{1,0:T(8,128)}, f32[16,768]{1,0:T(8,128)S(1)}, u32[]{:S(2)}) copy-start(f32[16,768]{1,0:T(8,128)S(1)} %get-tuple-element.3169) | copy-start | bytes 147460
  18.6 3.6 collective-permute-start.2
  19.9 4.8 collective-permute-start.3
  48.4 63.2 %all-gather.17.cloned.1.call-start = ((), (), s32[]{:S(2)}) async-start(), calls=%async_computation | async-start | bytes 3538944 | tf_op jit(solution)/shard_map/all_gather | solution.py:11
  53.1 187.6 %all-reduce.76.cloned.1.call-start = ((), (), s32[]{:S(2)}) async-start(), calls=%async_computation.6 | async-start | bytes 1572864 | tf_op jit(solution)/shard_map/psum | solution.py:25
  114.5 134.4 %all-gather.21.cloned.1.call-start = ((), (), s32[]{:S(2)}) async-start(), calls=%async_computation.2 | async-start | bytes 13369344 | tf_op jit(solution)/shard_map/all_gather | solution.py:11
  136.5 198.8 %all-gather.23.cloned.1.call-start = ((), (), s32[]{:S(2)}) async-start(), calls=%async_computation.3 | async-start | bytes 13369344 | tf_op jit(solution)/shard_map/all_gather | solution.py:11
  142.4 103.7 %copy-start.68 = (f32[8,16,16]{2,1,0:T(8,128)}, f32[8,16,16]{2,1,0:T(8,128)S(1)}, u32[]{:S(2)}) copy-start(f32[8,16,16]{2,1,0:T(8,128)S(1)} %get-tuple-element.3286) | copy-start | bytes 24580
  142.4 104.9 %copy-start.28 = (f32[16,768]{1,0:T(8,128)}, f32[16,768]{1,0:T(8,128)S(1)}, u32[]{:S(2)}) copy-start(f32[16,768]{1,0:T(8,128)S(1)} %get-tuple-element.1485) | copy-start | bytes 147460
  142.4 104.9 %copy-start.34 = (f32[8,16,768]{2,1,0:T(8,128)}, f32[8,16,768]{2,1,0:T(8,128)S(1)}, u32[]{:S(2)}) copy-start(f32[8,16,768]{2,1,0:T(8,128)S(1)} %get-tuple-element.3266) | copy-start | bytes 1179652
  142.4 104.9 %copy-start.35 = (f32[8,16,768]{2,1,0:T(8,128)}, f32[8,16,768]{2,1,0:T(8,128)S(1)}, u32[]{:S(2)}) copy-start(f32[8,16,768]{2,1,0:T(8,128)S(1)} %get-tuple-element.3267) | copy-start | bytes 1179652
  143.3 320.3 %all-reduce.72.cloned.1.call-start = ((), (), s32[]{:S(2)}) async-start(), calls=%async_computation.4 | async-start | bytes 196608 | tf_op jit(solution)/shard_map/psum | solution.py:25
  274.0 62.0 %copy-start.11 = (f32[1,16,768]{2,1,0:T(8,128)}, f32[1,16,768]{2,1,0:T(8,128)S(1)}, u32[]{:S(2)}) copy-start(f32[1,16,768]{2,1,0:T(8,128)S(1)} %get-tuple-element.3252) | copy-start | bytes 147460
  274.1 62.0 %copy-start.29 = (f32[16,768]{1,0:T(8,128)}, f32[16,768]{1,0:T(8,128)S(1)}, u32[]{:S(2)}) copy-start(f32[16,768]{1,0:T(8,128)S(1)} %get-tuple-element.1481) | copy-start | bytes 147460
  339.0 215.5 %all-reduce.74.cloned.1.call-start = ((), (), s32[]{:S(2)}) async-start(), calls=%async_computation.5 | async-start | bytes 3145728 | tf_op jit(solution)/shard_map/psum | solution.py:25
  343.2 211.4 %copy-start.19 = (f32[16,768]{1,0:T(8,128)S(1)}, f32[16,768]{1,0:T(8,128)}, u32[]{:S(2)}) copy-start(f32[16,768]{1,0:T(8,128)} %get-tuple-element.3058) | copy-start | bytes 147460
  464.4 92.9 %copy-start.17 = (f32[16,768]{1,0:T(8,128)S(1)}, f32[16,768]{1,0:T(8,128)}, u32[]{:S(2)}) copy-start(f32[16,768]{1,0:T(8,128)} %get-tuple-element.3001) | copy-start | bytes 147460
  470.3 77.6 %copy-start.71 = (f32[7,768]{1,0:T(8,128)}, f32[7,768]{1,0:T(8,128)S(1)}, u32[]{:S(2)}) copy-start(f32[7,768]{1,0:T(8,128)S(1)} %slice.762) | copy-start | bytes 64516
  682.5 84.8 %copy-start.6 = (f32[8,16,768]{2,1,0:T(8,128)S(1)}, f32[8,16,768]{2,1,0:T(8,128)}, u32[]{:S(2)}) copy-start(f32[8,16,768]{2,1,0:T(8,128)} %copy-done.5) | copy-start | bytes 1179652
  689.1 79.9 %copy-start.14 = (f32[1,16,768]{2,1,0:T(8,128)S(1)}, f32[1,16,768]{2,1,0:T(8,128)}, u32[]{:S(2)}) copy-start(f32[1,16,768]{2,1,0:T(8,128)} %copy-done.13) | copy-start | bytes 147460
  (118 other events, 1226.9 us)
Sparse Core Ops, SparseCore 0:
  48.5 33.5 all-gather.18
  83.8 27.6 all-gather.16
  114.6 74.8 all-reduce.75
Sparse Core Ops, SparseCore 1:
  136.6 104.9 all-gather.20
  243.6 91.7 all-gather.22
  339.1 124.4 all-reduce.71
  467.0 87.5 all-reduce.73
where the time goes:
time: 963 us; the launch traced here: 947 us
  blocking collectives  296 us (31%)
  local copies, waits for them, and re-layouts  255 us (26%)
  waiting for transfers between devices  211 us (22%)
  other arithmetic  147 us (15%)
  between operations  17.4 us (2%)
    all_gather x12, blocking collectives, entering(): gathered = jax.tree.map(lambda a: lax.all_gather(a, axis), part)  261 us
    psum x3, waiting for transfers between devices, spread(): return lax.psum(block, axis)  126 us
    all_gather x4, waiting for transfers between devices, entering(): gathered = jax.tree.map(lambda a: lax.all_gather(a, axis), part)  81.6 us
    add x63, other arithmetic, combine(): jnp.exp(-decays * following[0][..., None, :]) * earlier[1] + following[1]  61.6 us
    dynamic_update_slice x80, local copies, waits for them, and re-layouts, segment_outputs(): lax.scan(advance, entry, (steps_dt, inputs_du, b_coeffs, c_coeffs))  55.4 us
    mul x144, local copies, waits for them, and re-layouts, advance(): driven[:, None, :] * b_row[:, :, None]  50.4 us
    psum x1, blocking collectives, spread(): return lax.psum(block, axis)  35.3 us
    mul x48, local copies, waits for them, and re-layouts, advance(): return (states, jnp.sum(states * c_row[:, :, None], axis=1))  33.4 us
  transfers between devices with their start and end apart: 11, of which 5 were waited for; matrix products, arithmetic and copies ran while one was open for 11% of the time, Pallas kernels for 0%

commit v1 on v0

v1 whole, which is shorter than its diff:
```python
import functools
import math

import jax
import jax.numpy as jnp
from jax import lax
from jax.experimental import pallas as pl
from jax.experimental.pallas import tpu as pltpu
from jax.sharding import PartitionSpec as P

F32 = jnp.float32
BF16 = jnp.bfloat16
LANES = 128
SLICE = 96
STATE = 16
RANK = 24
EACH = RANK + 2 * STATE
OFF_LANE = 2 * EACH
TOT = 24
LOG2E = math.log2(math.e)


def vmem(count):
    return [pl.BlockSpec(memory_space=pltpu.VMEM)] * count


def call(kernel, out_shape, in_specs, scratch=(), flops=10**7, name=None):
    return pl.pallas_call(
        kernel,
        out_shape=out_shape,
        in_specs=in_specs,
        out_specs=jax.tree.map(lambda _: pl.BlockSpec(memory_space=pltpu.VMEM), out_shape),
        scratch_shapes=list(scratch),
        compiler_params=pltpu.CompilerParams(vmem_limit_bytes=48 << 20),
        cost_estimate=pl.CostEstimate(flops=flops, bytes_accessed=4 * 10**6, transcendentals=0),
        name=name,
    )


def lane_iota(shape):
    return lax.broadcasted_iota(jnp.int32, shape, len(shape) - 1)


def softplus(x):
    return jnp.maximum(x, 0.0) + jnp.log1p(jnp.exp(-jnp.abs(x)))


def silu(x):
    return x * jax.nn.sigmoid(x)


def cut_slice(values, k):
    j0, off = divmod(SLICE * k, LANES)
    first = values[:, j0 * LANES : (j0 + 1) * LANES]
    if off == 0:
        return first
    shift = LANES - off
    head = pltpu.roll(first, shift, 1)
    if shift >= SLICE:
        return head
    second = values[:, (j0 + 1) * LANES : (j0 + 2) * LANES]
    tail = pltpu.roll(second, shift, 1)
    return jnp.where(lane_iota(head.shape) < shift, head, tail)


def join_slices(parts):
    tiles = []
    lane = lane_iota(parts[0].shape)
    for m in range(2):
        y0, y1, y2, y3 = parts[4 * m : 4 * m + 4]
        r1 = pltpu.roll(y1, 96, 1)
        r2 = pltpu.roll(y2, 64, 1)
        r3 = pltpu.roll(y3, 32, 1)
        tiles.append(jnp.where(lane < 96, y0, r1))
        tiles.append(jnp.where(lane < 64, r1, r2))
        tiles.append(jnp.where(lane < 32, r2, r3))
    return tiles


def order_matrix(to_columns):
    q = lax.broadcasted_iota(jnp.int32, (LANES, LANES), 0 if to_columns else 1)
    p = lax.broadcasted_iota(jnp.int32, (LANES, LANES), 1 if to_columns else 0)
    return (p == (q % 8) * 16 + q // 8).astype(F32).astype(BF16)


def local_kernel(
    x_ref, top_ref, bottom_ref, left_ref, right_ref, w_ref, cw_ref, cb_ref, xw_ref, off_ref,
    act_ref, recr_ref, recc_ref, frame_ref,
):
    inner = x_ref.shape[1]
    weight = w_ref[...]

    def project(v):
        return jnp.dot(v, weight, preferred_element_type=F32).astype(BF16).astype(F32)

    frame_ref[1:9, 8:24, :] = x_ref[...].astype(F32).reshape(8, 16, inner)
    frame_ref[0:1, 8:24, :] = project(top_ref[...]).reshape(1, 16, inner)
    frame_ref[9:10, 8:24, :] = project(bottom_ref[...]).reshape(1, 16, inner)
    left = project(left_ref[...])
    right = project(right_ref[...])
    for i in range(10):
        frame_ref[i, 7:8, :] = left[i : i + 1]
        frame_ref[i, 24:25, :] = right[i : i + 1]
    total = jnp.zeros((8, 16, inner), F32) + cb_ref[...].reshape(1, 1, inner)
    for dc in range(3):
        for dr in range(3):
            k = dr * 3 + dc
            total = total + frame_ref[dr : dr + 8, 7 + dc : 23 + dc, :] * cw_ref[
                k : k + 1, :
            ].reshape(1, 1, inner)
    act = silu(total).reshape(LANES, inner).astype(BF16)
    act_ref[...] = act
    coef = jnp.dot(act, xw_ref[...], preferred_element_type=F32)
    lane = lane_iota((LANES, LANES))
    off = jnp.broadcast_to(off_ref[...], (LANES, LANES))
    coef_r = jnp.where(lane == OFF_LANE, off, coef[:, :LANES]).astype(BF16)
    coef_c = jnp.where(lane == OFF_LANE, off, coef[:, LANES:]).astype(BF16)
    turn = order_matrix(True)
    act_r = jnp.dot(turn, act, preferred_element_type=F32)
    coef_r = jnp.dot(turn, coef_r, preferred_element_type=F32).astype(BF16)
    wide = act.astype(F32)
    half = coef_c.astype(F32).reshape(8, 16, LANES)
    halves = [
        half[:, 8 * h : 8 * h + 8, :].reshape(64, LANES).astype(BF16) for h in range(2)
    ]
    for k in range(8):
        recr_ref[k, :, :LANES] = cut_slice(act_r, k).astype(BF16)
        recr_ref[k, :, LANES:] = coef_r
        piece = cut_slice(wide, k).reshape(8, 16, LANES)
        for h in range(2):
            recc_ref[2 * k + h, :, :LANES] = (
                piece[:, 8 * h : 8 * h + 8, :].reshape(64, LANES).astype(BF16)
            )
            recc_ref[2 * k + h, :, LANES:] = halves[h]


def unpack(rec_ref, du_ref, coef_ref, dt_ref):
    act = rec_ref[:, :LANES].astype(F32)
    for o in range(2):
        du_ref[o] = dt_ref[o] * act
    coef_ref[...] = rec_ref[:, LANES:].astype(F32)


def totals_kernel(copies, rec_ref, dtw_ref, bias_ref, decay_ref, dt_ref, excl_ref, tot_ref, du_ref, coef_ref):
    steps = rec_ref.shape[0] // 8
    coef_bf = rec_ref[:, LANES:]
    for o in range(2):
        z = jnp.dot(coef_bf, dtw_ref[o], preferred_element_type=F32) + bias_ref[o]
        dt_ref[o] = softplus(z)
    unpack(rec_ref, du_ref, coef_ref, dt_ref)
    sub = lax.broadcasted_iota(jnp.int32, (8, LANES), 0)
    for o in range(2):
        decay = [jnp.broadcast_to(decay_ref[o, n : n + 1, :], (8, LANES)) for n in range(STATE)]

        def advance(t, carry):
            span, states = carry
            t = steps - 1 - t if o == 1 else t
            at = pl.ds(pl.multiple_of(t * 8, 8), 8)
            dt = dt_ref[o, at, :]
            du = du_ref[o, at, :]
            coef = coef_ref[at, :]
            new = []
            for n in range(STATE):
                lane = o * EACH + RANK + n
                b = jnp.broadcast_to(coef[:, lane : lane + 1], (8, LANES))
                new.append(jnp.exp2(decay[n] * dt) * states[n] + du * b)
            return span + dt, tuple(new)

        zero = jnp.zeros((8, LANES), F32)
        span, states = lax.fori_loop(0, steps, advance, (zero, (zero,) * STATE), unroll=2)
        states = list(states)
        for k in (1, 2, 4):
            shift = k if o == 0 else 8 - k
            keep = sub >= k if o == 0 else sub < 8 - k
            for n in range(STATE):
                moved = jnp.where(keep, pltpu.roll(states[n], shift, 0), 0.0)
                states[n] = jnp.exp2(decay[n] * span) * moved + states[n]
            span = span + jnp.where(keep, pltpu.roll(span, shift, 0), 0.0)
        shift = 1 if o == 0 else 7
        keep = sub >= 1 if o == 0 else sub < 7
        last = 7 if o == 0 else 0
        for n in range(STATE):
            excl_ref[o, n] = jnp.where(keep, pltpu.roll(states[n], shift, 0), 0.0)
            for k in range(copies):
                tot_ref[k, o * TOT + n : o * TOT + n + 1, :] = states[n][last : last + 1]
        excl_ref[o, STATE] = jnp.where(keep, pltpu.roll(span, shift, 0), 0.0)
        for k in range(copies):
            tot_ref[k, o * TOT + STATE : (o + 1) * TOT, :] = jnp.broadcast_to(
                span[last : last + 1], (TOT - STATE, LANES)
            )


def outputs_kernel(place_ref, rec_ref, dt_ref, excl_ref, tot_ref, decay_ref, y_ref, du_ref, coef_ref, sum_ref):
    steps = rec_ref.shape[0] // 8
    chunks = tot_ref.shape[0]
    place = place_ref[0]
    unpack(rec_ref, du_ref, coef_ref, dt_ref)
    for o in range(2):
        rates = decay_ref[o]
        entry = jnp.zeros((STATE, LANES), F32)
        for k in range(chunks) if o == 0 else range(chunks - 1, -1, -1):
            ahead = k < place if o == 0 else k > place
            base = o * TOT
            following = (
                jnp.exp2(rates * tot_ref[k, base + STATE : base + STATE + 1, :]) * entry
                + tot_ref[k, base : base + STATE, :]
            )
            entry = jnp.where(ahead, following, entry)
        decay = [jnp.broadcast_to(decay_ref[o, n : n + 1, :], (8, LANES)) for n in range(STATE)]
        states = tuple(
            jnp.exp2(decay[n] * excl_ref[o, STATE]) * entry[n : n + 1] + excl_ref[o, n]
            for n in range(STATE)
        )

        def advance(t, states):
            t = steps - 1 - t if o == 1 else t
            at = pl.ds(pl.multiple_of(t * 8, 8), 8)
            dt = dt_ref[o, at, :]
            du = du_ref[o, at, :]
            coef = coef_ref[at, :]
            new = []
            parts = []
            for n in range(STATE):
                lane = o * EACH + RANK + n
                b = jnp.broadcast_to(coef[:, lane : lane + 1], (8, LANES))
                c = jnp.broadcast_to(coef[:, lane + STATE : lane + STATE + 1], (8, LANES))
                h = jnp.exp2(decay[n] * dt) * states[n] + du * b
                new.append(h)
                parts.append(h * c)
            while len(parts) > 1:
                parts = [a + b for a, b in zip(parts[::2], parts[1::2])]
            if o == 0:
                sum_ref[at, :] = parts[0]
            else:
                sum_ref[at, :] = sum_ref[at, :] + parts[0]
            return tuple(new)

        lax.fori_loop(0, steps, advance, states, unroll=2)
    y_ref[...] = sum_ref[...].astype(BF16)


def final_kernel(yr_ref, yc_ref, act_ref, gate_ref, skip_ref, gain_ref, w_ref, live_ref, out_ref):
    turn = order_matrix(False)
    parts = []
    for k in range(8):
        first = jnp.dot(turn, yr_ref[k], preferred_element_type=F32)
        second = jnp.concatenate(
            [yc_ref[2 * k + h].astype(F32).reshape(8, 8, LANES) for h in range(2)], axis=1
        ).reshape(LANES, LANES)
        parts.append(first + second)
    combined = jnp.concatenate(join_slices(parts), axis=1)
    combined = combined + skip_ref[...] * act_ref[...].astype(F32)
    mean = jnp.mean(combined, axis=1, keepdims=True)
    centered = combined - mean
    variance = jnp.mean(centered * centered, axis=1, keepdims=True)
    normed = centered * lax.rsqrt(variance + 1e-05) * gain_ref[...]
    mixed = (normed * silu(gate_ref[...].astype(F32))).astype(BF16)
    out_ref[...] = (
        jnp.dot(mixed, w_ref[...], preferred_element_type=F32) * live_ref[...]
    ).astype(BF16)


def shifted(values, axis, step):
    count = lax.axis_size(axis)
    pairs = [(i, i + step) for i in range(count) if 0 <= i + step < count]
    return lax.ppermute(values, axis, pairs)


def padded_lanes(values, fill):
    pad = LANES - values.shape[-1]
    return jnp.pad(values, [(0, 0)] * (values.ndim - 1) + [(0, pad)], constant_values=fill)


def slice_params(dt_weight, dt_bias, decay_rate, first, piece):
    at = piece * SLICE
    dtw = lax.dynamic_slice_in_dim(dt_weight[first : first + 2], at, SLICE, 2)
    bias = lax.dynamic_slice_in_dim(dt_bias[first : first + 2], at, SLICE, 1)
    rates = lax.dynamic_slice_in_dim(decay_rate[first : first + 2], at, SLICE, 1)
    dtw = padded_lanes(dtw, 0)
    rows = jnp.zeros((2, LANES, LANES), BF16)
    for o in range(2):
        rows = lax.dynamic_update_slice(rows, dtw[o : o + 1], (o, o * EACH, 0))
    rows = rows.at[:, OFF_LANE, :].set(jnp.asarray(-1e30, BF16))
    bias = padded_lanes(bias, -1e30)[:, None, :]
    rates = padded_lanes(jnp.swapaxes(rates, 1, 2) * -LOG2E, 0)
    return rows, bias, rates


def per_device(
    patches, tissue, in_weight, conv_weight, conv_bias, x_weight, dt_weight, dt_bias,
    decay_rate, skip_gain, norm_gain, out_weight,
):
    tile_rows, tile_cols, channels = patches.shape
    inner = out_weight.shape[0]
    tokens = tile_rows * tile_cols
    row = lax.axis_index("row")
    col = lax.axis_index("col")
    top = shifted(patches[-1], "row", 1)
    bottom = shifted(patches[0], "row", -1)

    def edge(j):
        return jnp.concatenate([top[j : j + 1], patches[:, j], bottom[j : j + 1]], axis=0)

    left = shifted(edge(tile_cols - 1), "col", 1)
    right = shifted(edge(0), "col", -1)
    projected = jnp.dot(
        patches.reshape(tokens, channels), in_weight, preferred_element_type=F32
    ).astype(BF16)
    x_inner = projected[:, :inner]
    gate = projected[:, inner:]
    live = tissue.reshape(tokens, 1).astype(F32)
    half_width = x_weight.shape[1] // 2
    x_wide = jnp.concatenate(
        [padded_lanes(x_weight[:, :half_width], 0), padded_lanes(x_weight[:, half_width:], 0)], axis=1
    )
    params_r = slice_params(dt_weight, dt_bias, decay_rate, 0, col)
    params_c = slice_params(dt_weight, dt_bias, decay_rate, 2, row // 2)

    act, rec_r, rec_c = call(
        local_kernel,
        (
            jax.ShapeDtypeStruct((tokens, inner), BF16),
            jax.ShapeDtypeStruct((8, tokens, 2 * LANES), BF16),
            jax.ShapeDtypeStruct((16, tokens // 2, 2 * LANES), BF16),
        ),
        vmem(10),
        [pltpu.VMEM((10, 32, inner), F32)],
        name="local",
    )(
        x_inner, top, bottom, left, right, in_weight[:, :inner],
        conv_weight.reshape(9, inner), conv_bias.reshape(1, inner), x_wide, 1.0 - live,
    )

    length = 8 * tokens
    pair_scratch = [pltpu.VMEM((2, length, LANES), F32), pltpu.VMEM((length, LANES), F32)]

    def totals(rec, params, copies, name):
        return call(
            functools.partial(totals_kernel, copies),
            (
                jax.ShapeDtypeStruct((2, length, LANES), F32),
                jax.ShapeDtypeStruct((2, STATE + 1, 8, LANES), F32),
                jax.ShapeDtypeStruct((copies, 2 * TOT, LANES), F32),
            ),
            vmem(4),
            pair_scratch,
            flops=10**9,
            name=name,
        )(rec, *params)

    def outputs(place, rec, dt, excl, tot, rates, name):
        return call(
            outputs_kernel,
            jax.ShapeDtypeStruct((length, LANES), BF16),
            [pl.BlockSpec(memory_space=pltpu.SMEM)] + vmem(5),
            pair_scratch + [pltpu.VMEM((length, LANES), F32)],
            flops=10**9,
            name=name,
        )(place.reshape(1).astype(jnp.int32), rec, dt, excl, tot, rates)

    rec_r = lax.all_to_all(rec_r, "col", 0, 0).reshape(length, 2 * LANES)
    rec_c = lax.all_to_all(rec_c, "row", 0, 0).reshape(length, 2 * LANES)

    dt_r, excl_r, tot_r = totals(rec_r, params_r, 16, "totals_rows")
    dt_c, excl_c, tot_c = totals(rec_c, params_c, 1, "totals_cols")

    tot_r = lax.all_to_all(tot_r, "row", 0, 0)
    side = row % 2
    mate = lax.ppermute(tot_c, "row", [(i, i ^ 1) for i in range(16)])
    both = jnp.concatenate([jnp.where(side == 0, tot_c, mate), jnp.where(side == 0, mate, tot_c)])
    both = lax.all_to_all(jnp.broadcast_to(both[None], (8,) + both.shape), "col", 0, 0)
    tot_c = both.reshape(16, 2 * TOT, LANES)

    y_r = outputs(row, rec_r, dt_r, excl_r, tot_r, params_r[2], "outputs_rows")
    y_c = outputs(col * 2 + side, rec_c, dt_c, excl_c, tot_c, params_c[2], "outputs_cols")
    y_r = lax.all_to_all(y_r.reshape(8, tokens, LANES), "col", 0, 0)
    y_c = lax.all_to_all(y_c.reshape(16, tokens // 2, LANES), "row", 0, 0)

    result = call(
        final_kernel, jax.ShapeDtypeStruct((tokens, channels), BF16), vmem(8), name="final"
    )(
        y_r, y_c, act, gate, skip_gain.reshape(1, inner), norm_gain.reshape(1, inner), out_weight, live
    )
    return result.reshape(tile_rows, tile_cols, channels)


def solution(mesh):
    in_specs = (P("row", "col", None), P("row", "col")) + (P(),) * 10
    return jax.shard_map(
        per_device, mesh=mesh, in_specs=in_specs, out_specs=P("row", "col", None), check_vma=False
    )
```

time: 963 us -> 174 us (0.18)
  the two profiles are of different devices: /device:TPU:120 before, /device:TPU:1 now
where the time goes in v1:
time: 174 us; the launch traced here: 173 us
  Pallas kernels  87.5 us (50%)
  starting transfers between devices  52 us (30%)
  waiting for transfers between devices  21.9 us (13%)
  local copies, waits for them, and re-layouts  9.78 us (6%)
    pallas_call x2, Pallas kernels, outputs(): call(outputs_kernel, jax.ShapeDtypeStruct((length, LANES), BF16), [pl.Blo...  48.9 us
    pallas_call x2, Pallas kernels, totals(): call(functools.partial(totals_kernel, copies), (jax.ShapeDtypeStruct((2,...  35 us
    ppermute x4, starting transfers between devices, shifted(): return lax.ppermute(values, axis, pairs)  12.3 us
    all_to_all x1, starting transfers between devices, per_device(): rec_c = lax.all_to_all(rec_c, 'row', 0, 0).reshape(length, 2 * LANES)  9.54 us
    all_to_all x1, waiting for transfers between devices, per_device(): rec_r = lax.all_to_all(rec_r, 'col', 0, 0).reshape(length, 2 * LANES)  9.22 us
    all_to_all x1, waiting for transfers between devices, per_device(): y_c = lax.all_to_all(y_c.reshape(16, tokens // 2, LANES), 'row', 0, 0)  8.49 us
    all_to_all x1, starting transfers between devices, per_device(): y_c = lax.all_to_all(y_c.reshape(16, tokens // 2, LANES), 'row', 0, 0)  6.93 us
    all_to_all x1, starting transfers between devices, per_device(): tot_r = lax.all_to_all(tot_r, 'row', 0, 0)  6.66 us
  transfers between devices with their start and end apart: 11, of which 4 were waited for; matrix products, arithmetic and copies ran while one was open for 3% of the time, Pallas kernels for 48%

profile of v1, /device:TPU:1, one launch (start us, length us, event | category | flops | bytes accessed | tf_op | source)
XLA Modules:
  0.0 173.0 jit_solution(16571680532193051659)
XLA Ops:
  0.9 1.3 collective-permute-start.1
  2.2 4.7 %collective-permute-start = (bf16[16,384]{1,0:T(8,128)(2,1)S(1)}, bf16[16,384]{1,0:T(8,128)(2,1)S(1)}, u32[]{:S(2)}, u32[]{:S(2)}) collective-permute-start(bf16[16,384]{1,0:T(8,128)(2,1)S(1)} %get-tuple-element.56), channel_id=1, source_target_pairs={{0,8},{8,16},{16,24},{24,32},{32,40},{40,48},{48,56},{56,64},{64,7... | collective-permute-start | bytes 36872 | tf_op jit(solution)/shard_map/ppermute | solution.py:266
  11.5 4.4 %collective-permute-start.2 = (bf16[10,384]{1,0:T(8,128)(2,1)S(1)}, bf16[10,384]{1,0:T(8,128)(2,1)S(1)}, u32[]{:S(2)}, u32[]{:S(2)}) collective-permute-start(bf16[10,384]{1,0:T(8,128)(2,1)S(1)} %pad_maximum_fusion.1), channel_id=1, source_target_pairs={{0,1},{1,2},{2,3},{3,4},{4,5},{5,6},{6,7},{8,9},{9,10},{10,11},{11... | collective-permute-start | bytes 23048 | tf_op jit(solution)/shard_map/ppermute | solution.py:266
  15.9 1.9 %collective-permute-start.3 = (bf16[10,384]{1,0:T(8,128)(2,1)S(1)}, bf16[10,384]{1,0:T(8,128)(2,1)S(1)}, u32[]{:S(2)}, u32[]{:S(2)}) collective-permute-start(bf16[10,384]{1,0:T(8,128)(2,1)S(1)} %pad_maximum_fusion.2), channel_id=1, source_target_pairs={{1,0},{2,1},{3,2},{4,3},{5,4},{6,5},{7,6},{9,8},{10,9},{11,10},{12... | collective-permute-start | bytes 23048 | tf_op jit(solution)/shard_map/ppermute | solution.py:266
  18.0 2.9 %collective-permute-done.3.right_ref = bf16[10,384]{1,0:T(8,128)(2,1)S(1)} collective-permute-done((bf16[10,384]{1,0:T(8,128)(2,1)S(1)}, bf16[10,384]{1,0:T(8,128)(2,1)S(1)}, u32[]{:S(2)}, u32[]{:S(2)}) %collective-permute-start.3) | collective-permute-done | bytes 7712 | tf_op jit(solution)/shard_map/ppermute | solution.py:266
  20.9 2.3 %local.1 = (bf16[128,768]{1,0:T(8,128)(2,1)S(1)}, bf16[8,128,256]{2,1,0:T(8,128)(2,1)}, bf16[16,64,256]{2,1,0:T(8,128)(2,1)}) custom-call(bf16[128,768]{1,0:T(8,128)(2,1)S(1)} %get-tuple-element.48.x_ref, bf16[16,384]{1,0:T(8,128)(2,1)S(1)} %collective-permute-done.top_ref, bf16[16,384]{1,0:T(8,128)(2,1)S(1)} %collective-permute-done.1.bottom_ref, ...), custom_call_target="tpu_custom_call" | custom-call | flops 10000000 | bytes 4000000 | tf_op jit(solution)/shard_map/local/pallas_call | solution.py:319
  23.2 4.2 %all-to-all-start = ((bf16[8,128,256]{2,1,0:T(8,128)(2,1)}), bf16[8,128,256]{2,1,0:T(8,128)(2,1)S(1)}, u32[]{:S(2)}, u32[]{:S(2)}) async-start(bf16[8,128,256]{2,1,0:T(8,128)(2,1)} %get-tuple-element.38), calls=%async_computation | async-start | bytes 1048576 | tf_op jit(solution)/shard_map/all_to_all | solution.py:361
  27.7 9.2 %all-to-all-done = bf16[8,128,256]{2,1,0:T(8,128)(2,1)S(1)} async-done(((bf16[8,128,256]{2,1,0:T(8,128)(2,1)}), bf16[8,128,256]{2,1,0:T(8,128)(2,1)S(1)}, u32[]{:S(2)}, u32[]{:S(2)}) %all-to-all-start) | async-done | bytes 524320 | tf_op jit(solution)/shard_map/all_to_all | solution.py:361
  36.9 9.5 %all-to-all-start.3 = ((bf16[16,64,256]{2,1,0:T(8,128)(2,1)}), bf16[16,64,256]{2,1,0:T(8,128)(2,1)S(1)}, u32[]{:S(2)}, u32[]{:S(2)}) async-start(bf16[16,64,256]{2,1,0:T(8,128)(2,1)} %get-tuple-element.42), calls=%async_computation.3 | async-start | bytes 1048576 | tf_op jit(solution)/shard_map/all_to_all | solution.py:362
  46.7 17.9 %totals_rows.1 = (f32[2,1024,128]{2,1,0:T(8,128)S(1)}, f32[2,17,8,128]{3,2,1,0:T(8,128)S(1)}, f32[16,48,128]{2,1,0:T(8,128)}) custom-call(bf16[1024,256]{1,0:T(8,128)(2,1)S(1)} %bitcast.27, bf16[2,128,128]{2,1,0:T(8,128)(2,1)S(1)} %scatter.6.dtw_ref, f32[2,1,128]{2,1,0:T(1,128)S(1)} %bitcast.33, f32[2,16,128]{2,1,0:T(8,128)S(1)} %pad.38.decay_ref), custom_call_target="tpu_custom_call" | custom-call | flops 1000000000 | bytes 4000000 | tf_op jit(solution)/shard_map/totals_rows/pallas_call | solution.py:338
  65.6 6.7 %all-to-all-start.1 = ((f32[16,48,128]{2,1,0:T(8,128)}), f32[16,48,128]{2,1,0:T(8,128)S(1)}, u32[]{:S(2)}, u32[]{:S(2)}) async-start(f32[16,48,128]{2,1,0:T(8,128)} %get-tuple-element.41), calls=%async_computation.1 | async-start | bytes 786432 | tf_op jit(solution)/shard_map/all_to_all | solution.py:367
  72.2 17.1 %totals_cols.1 = (f32[2,1024,128]{2,1,0:T(8,128)S(1)}, f32[2,17,8,128]{3,2,1,0:T(8,128)S(1)}, f32[1,48,128]{2,1,0:T(8,128)S(1)}) custom-call(bf16[1024,256]{1,0:T(8,128)(2,1)S(1)} %bitcast.29, bf16[2,128,128]{2,1,0:T(8,128)(2,1)S(1)} %scatter.9.dtw_ref, f32[2,1,128]{2,1,0:T(1,128)S(1)} %bitcast.32, f32[2,16,128]{2,1,0:T(8,128)S(1)} %pad.41.decay_ref), custom_call_target="tpu_custom_call" | custom-call | flops 1000000000 | bytes 4000000 | tf_op jit(solution)/shard_map/totals_cols/pallas_call | solution.py:338
  89.3 1.0 copy-done.1
  90.3 1.4 collective-permute-start.4
  91.7 1.3 collective-permute-done.4
  93.8 6.2 %all-to-all-start.4 = ((f32[8,2,48,128]{3,2,1,0:T(8,128)}), f32[8,2,48,128]{3,2,1,0:T(8,128)S(1)}, u32[]{:S(2)}, u32[]{:S(2)}) async-start(f32[8,2,48,128]{3,2,1,0:T(8,128)} %broadcast_in_dim.14), calls=%async_computation.4 | async-start | bytes 786432 | tf_op jit(solution)/shard_map/all_to_all | solution.py:371
  100.0 1.2 copy-done.4
  101.2 24.4 %outputs_rows.1 = bf16[1024,128]{1,0:T(8,128)(2,1)} custom-call(s32[1]{0:T(128)} %bitcast.place_ref, bf16[1024,256]{1,0:T(8,128)(2,1)S(1)} %bitcast.28, f32[2,1024,128]{2,1,0:T(8,128)S(1)} %copy-done.4, f32[2,17,8,128]{3,2,1,0:T(8,128)S(1)} %get-tuple-element.40.excl_ref, f32[16,48,128]{2,1,0:T(8,128)S(1)} %all-to-all-done.1.tot_ref, ...), custom_call_target="tpu_custom_call" | custom-call | flops 1000000000 | bytes 4000000 | tf_op jit(solution)/shard_map/outputs_rows/pallas_call | solution.py:352
  125.7 4.8 %all-to-all-start.2 = ((bf16[8,128,128]{2,1,0:T(8,128)(2,1)}), bf16[8,128,128]{2,1,0:T(8,128)(2,1)S(1)}, u32[]{:S(2)}, u32[]{:S(2)}) async-start(bf16[8,128,128]{2,1,0:T(8,128)(2,1)} %bitcast.9), calls=%async_computation.2 | async-start | bytes 524288 | tf_op jit(solution)/shard_map/all_to_all | solution.py:376
  130.5 1.2 copy-done.2
  131.7 24.4 %outputs_cols.1 = bf16[1024,128]{1,0:T(8,128)(2,1)} custom-call(s32[1]{0:T(128)} %bitcast.10.place_ref, bf16[1024,256]{1,0:T(8,128)(2,1)S(1)} %bitcast.30, f32[2,1024,128]{2,1,0:T(8,128)S(1)} %copy-done.2, f32[2,17,8,128]{3,2,1,0:T(8,128)S(1)} %get-tuple-element.44.excl_ref, f32[16,48,128]{2,1,0:T(8,128)S(1)} %bitcast.31, f32[2,16,128]{2,1,0:T(8,128)S(1)} %pad.41.decay_ref), custom_call_target="tpu_custom_call" | custom-call | flops 1000000000 | bytes 4000000 | tf_op jit(solution)/shard_map/outputs_cols/pallas_call | solution.py:352
  156.2 6.9 %all-to-all-start.5 = ((bf16[16,64,128]{2,1,0:T(8,128)(2,1)}), bf16[16,64,128]{2,1,0:T(8,128)(2,1)S(1)}, u32[]{:S(2)}, u32[]{:S(2)}) async-start(bf16[16,64,128]{2,1,0:T(8,128)(2,1)} %bitcast.15), calls=%async_computation.5 | async-start | bytes 524288 | tf_op jit(solution)/shard_map/all_to_all | solution.py:377
  163.2 8.5 %all-to-all-done.5.yc_ref = bf16[16,64,128]{2,1,0:T(8,128)(2,1)S(1)} async-done(((bf16[16,64,128]{2,1,0:T(8,128)(2,1)}), bf16[16,64,128]{2,1,0:T(8,128)(2,1)S(1)}, u32[]{:S(2)}, u32[]{:S(2)}) %all-to-all-start.5) | async-done | bytes 262176 | tf_op jit(solution)/shard_map/all_to_all | solution.py:377
  171.7 1.4 final.1
  (79 shorter events, 7.7 us)
Async XLA Ops:
  0.0 10.6 %copy-start.6 = (bf16[8,16,384]{2,1,0:T(8,128)(2,1)S(1)}, bf16[8,16,384]{2,1,0:T(8,128)(2,1)}, u32[]{:S(2)}) copy-start(bf16[8,16,384]{2,1,0:T(8,128)(2,1)} %param.16) | copy-start | bytes 294916
  0.0 10.2 %slice-start = ((bf16[768,224]{0,1:T(8,128)(2,1)}), bf16[768,112]{0,1:T(8,128)(2,1)S(1)}, s32[]{:S(2)}) async-start(bf16[768,224]{0,1:T(8,128)(2,1)} %param.21), calls=%async_computation.6 | async-start | bytes 344064 | tf_op jit(solution)/shard_map/slice | solution.py:314
  0.0 10.4 %slice-start.1 = ((bf16[768,224]{0,1:T(8,128)(2,1)}), bf16[768,128]{0,1:T(8,128)(2,1)S(1)}, s32[]{:S(2)}) async-start(bf16[768,224]{0,1:T(8,128)(2,1)} %param.21), calls=%async_computation.7 | async-start | bytes 393216 | tf_op jit(solution)/shard_map/slice.61
  0.0 10.6 %copy-start.5 = (bf16[384,1536]{1,0:T(8,128)(2,1)S(1)}, bf16[384,1536]{1,0:T(8,128)(2,1)}, u32[]{:S(2)}) copy-start(bf16[384,1536]{1,0:T(8,128)(2,1)} %param.18) | copy-start | bytes 3538948
  0.9 10.5 %collective-permute-start.1 = (bf16[16,384]{1,0:T(8,128)(2,1)S(1)}, bf16[16,384]{1,0:T(8,128)(2,1)S(1)}, u32[]{:S(2)}, u32[]{:S(2)}) collective-permute-start(bf16[16,384]{1,0:T(8,128)(2,1)S(1)} %get-tuple-element.55), channel_id=1, source_target_pairs={{8,0},{16,8},{24,16},{32,24},{40,32},{48,40},{56,48},{64,56},{72,6... | collective-permute-start | bytes 36872 | tf_op jit(solution)/shard_map/ppermute | solution.py:266
  2.2 9.3 %collective-permute-start = (bf16[16,384]{1,0:T(8,128)(2,1)S(1)}, bf16[16,384]{1,0:T(8,128)(2,1)S(1)}, u32[]{:S(2)}, u32[]{:S(2)}) collective-permute-start(bf16[16,384]{1,0:T(8,128)(2,1)S(1)} %get-tuple-element.56), channel_id=1, source_target_pairs={{0,8},{8,16},{16,24},{24,32},{32,40},{40,48},{48,56},{56,64},{64,7... | collective-permute-start | bytes 36872 | tf_op jit(solution)/shard_map/ppermute | solution.py:266
  11.2 6.7 %copy-start.9 = (f32[768]{0:T(1024)S(1)}, f32[768]{0:T(1024)}, u32[]{:S(2)}) copy-start(f32[768]{0:T(1024)} %param.20) | copy-start | bytes 9220
  11.3 6.7 %copy-start.8 = (f32[3,3,768]{2,1,0:T(4,128)S(1)}, f32[3,3,768]{2,1,0:T(4,128)}, u32[]{:S(2)}) copy-start(f32[3,3,768]{2,1,0:T(4,128)} %param.19) | copy-start | bytes 82948
  11.5 6.6 %collective-permute-start.2 = (bf16[10,384]{1,0:T(8,128)(2,1)S(1)}, bf16[10,384]{1,0:T(8,128)(2,1)S(1)}, u32[]{:S(2)}, u32[]{:S(2)}) collective-permute-start(bf16[10,384]{1,0:T(8,128)(2,1)S(1)} %pad_maximum_fusion.1), channel_id=1, source_target_pairs={{0,1},{1,2},{2,3},{3,4},{4,5},{5,6},{6,7},{8,9},{9,10},{10,11},{11... | collective-permute-start | bytes 23048 | tf_op jit(solution)/shard_map/ppermute | solution.py:266
  15.9 5.0 %collective-permute-start.3 = (bf16[10,384]{1,0:T(8,128)(2,1)S(1)}, bf16[10,384]{1,0:T(8,128)(2,1)S(1)}, u32[]{:S(2)}, u32[]{:S(2)}) collective-permute-start(bf16[10,384]{1,0:T(8,128)(2,1)S(1)} %pad_maximum_fusion.2), channel_id=1, source_target_pairs={{1,0},{2,1},{3,2},{4,3},{5,4},{6,5},{7,6},{9,8},{10,9},{11,10},{12... | collective-permute-start | bytes 23048 | tf_op jit(solution)/shard_map/ppermute | solution.py:266
  23.2 23.3 %copy-start.7 = (f32[4,768,16]{1,2,0:T(8,128)S(1)}, f32[4,768,16]{1,2,0:T(8,128)}, u32[]{:S(2)}) copy-start(f32[4,768,16]{1,2,0:T(8,128)} %param.24) | copy-start | bytes 589828
  23.2 13.7 %all-to-all-start = ((bf16[8,128,256]{2,1,0:T(8,128)(2,1)}), bf16[8,128,256]{2,1,0:T(8,128)(2,1)S(1)}, u32[]{:S(2)}, u32[]{:S(2)}) async-start(bf16[8,128,256]{2,1,0:T(8,128)(2,1)} %get-tuple-element.38), calls=%async_computation | async-start | bytes 1048576 | tf_op jit(solution)/shard_map/all_to_all | solution.py:361
  36.9 28.7 %all-to-all-start.3 = ((bf16[16,64,256]{2,1,0:T(8,128)(2,1)}), bf16[16,64,256]{2,1,0:T(8,128)(2,1)S(1)}, u32[]{:S(2)}, u32[]{:S(2)}) async-start(bf16[16,64,256]{2,1,0:T(8,128)(2,1)} %get-tuple-element.42), calls=%async_computation.3 | async-start | bytes 1048576 | tf_op jit(solution)/shard_map/all_to_all | solution.py:362
  65.6 27.4 %all-to-all-start.1 = ((f32[16,48,128]{2,1,0:T(8,128)}), f32[16,48,128]{2,1,0:T(8,128)S(1)}, u32[]{:S(2)}, u32[]{:S(2)}) async-start(f32[16,48,128]{2,1,0:T(8,128)} %get-tuple-element.41), calls=%async_computation.1 | async-start | bytes 786432 | tf_op jit(solution)/shard_map/all_to_all | solution.py:367
  89.3 1.0 copy-start.1
  90.3 2.7 %collective-permute-start.4 = (f32[1,48,128]{2,1,0:T(8,128)S(1)}, f32[1,48,128]{2,1,0:T(8,128)S(1)}, u32[]{:S(2)}, u32[]{:S(2)}) collective-permute-start(f32[1,48,128]{2,1,0:T(8,128)S(1)} %get-tuple-element.45), channel_id=1, source_target_pairs={{0,8},{8,0},{16,24},{24,16},{32,40},{40,32},{48,56},{56,48},{64,72... | collective-permute-start | bytes 73736 | tf_op jit(solution)/shard_map/ppermute | solution.py:369
  93.8 31.9 %all-to-all-start.4 = ((f32[8,2,48,128]{3,2,1,0:T(8,128)}), f32[8,2,48,128]{3,2,1,0:T(8,128)S(1)}, u32[]{:S(2)}, u32[]{:S(2)}) async-start(f32[8,2,48,128]{3,2,1,0:T(8,128)} %broadcast_in_dim.14), calls=%async_computation.4 | async-start | bytes 786432 | tf_op jit(solution)/shard_map/all_to_all | solution.py:371
  100.0 1.2 copy-start.4
  125.7 30.5 %all-to-all-start.2 = ((bf16[8,128,128]{2,1,0:T(8,128)(2,1)}), bf16[8,128,128]{2,1,0:T(8,128)(2,1)S(1)}, u32[]{:S(2)}, u32[]{:S(2)}) async-start(bf16[8,128,128]{2,1,0:T(8,128)(2,1)} %bitcast.9), calls=%async_computation.2 | async-start | bytes 524288 | tf_op jit(solution)/shard_map/all_to_all | solution.py:376
  130.5 1.2 copy-start.2
  131.7 31.4 %copy-start.10 = (f32[768]{0:T(1024)S(1)}, f32[768]{0:T(1024)}, u32[]{:S(2)}) copy-start(f32[768]{0:T(1024)} %param.25) | copy-start | bytes 9220
  131.7 31.4 %copy-start.11 = (f32[768]{0:T(1024)S(1)}, f32[768]{0:T(1024)}, u32[]{:S(2)}) copy-start(f32[768]{0:T(1024)} %param.26) | copy-start | bytes 9220
  131.7 39.9 %copy-start = (bf16[768,384]{1,0:T(8,128)(2,1)S(1)}, bf16[768,384]{1,0:T(8,128)(2,1)}, u32[]{:S(2)}) copy-start(bf16[768,384]{1,0:T(8,128)(2,1)} %w_ref.1) | copy-start | bytes 1769476
  156.2 15.5 %all-to-all-start.5 = ((bf16[16,64,128]{2,1,0:T(8,128)(2,1)}), bf16[16,64,128]{2,1,0:T(8,128)(2,1)S(1)}, u32[]{:S(2)}, u32[]{:S(2)}) async-start(bf16[16,64,128]{2,1,0:T(8,128)(2,1)} %bitcast.15), calls=%async_computation.5 | async-start | bytes 524288 | tf_op jit(solution)/shard_map/all_to_all | solution.py:377
  (2 other events, 1.6 us)

commit v2 on v1

v2 whole, which is shorter than its diff:
```python
import functools
import math

import jax
import jax.numpy as jnp
from jax import lax
from jax.experimental import pallas as pl
from jax.experimental.pallas import tpu as pltpu
from jax.sharding import PartitionSpec as P

F32 = jnp.float32
BF16 = jnp.bfloat16
LANES = 128
SLICE = 96
STATE = 16
RANK = 24
EACH = RANK + 2 * STATE
OFF_LANE = 2 * EACH
TOT = 24
TURN = OFF_LANE
BLOCK = 16
LOG2E = math.log2(math.e)


def vmem(count):
    return [pl.BlockSpec(memory_space=pltpu.VMEM)] * count


def call(kernel, out_shape, in_specs, scratch=(), flops=10**7, name=None):
    return pl.pallas_call(
        kernel,
        out_shape=out_shape,
        in_specs=in_specs,
        out_specs=jax.tree.map(lambda _: pl.BlockSpec(memory_space=pltpu.VMEM), out_shape),
        scratch_shapes=list(scratch),
        compiler_params=pltpu.CompilerParams(vmem_limit_bytes=48 << 20),
        cost_estimate=pl.CostEstimate(flops=flops, bytes_accessed=4 * 10**6, transcendentals=0),
        name=name,
    )


def lane_iota(shape):
    return lax.broadcasted_iota(jnp.int32, shape, len(shape) - 1)


def softplus(x):
    return jnp.maximum(x, 0.0) + jnp.log1p(jnp.exp(-jnp.abs(x)))


def silu(x):
    return x * jax.nn.sigmoid(x)


def cut_slice(values, k):
    j0, off = divmod(SLICE * k, LANES)
    first = values[:, j0 * LANES : (j0 + 1) * LANES]
    if off == 0:
        return first
    shift = LANES - off
    head = pltpu.roll(first, shift, 1)
    if shift >= SLICE:
        return head
    second = values[:, (j0 + 1) * LANES : (j0 + 2) * LANES]
    tail = pltpu.roll(second, shift, 1)
    return jnp.where(lane_iota(head.shape) < shift, head, tail)


def join_slices(parts):
    tiles = []
    lane = lane_iota(parts[0].shape)
    for m in range(2):
        y0, y1, y2, y3 = parts[4 * m : 4 * m + 4]
        r1 = pltpu.roll(y1, 96, 1)
        r2 = pltpu.roll(y2, 64, 1)
        r3 = pltpu.roll(y3, 32, 1)
        tiles.append(jnp.where(lane < 96, y0, r1))
        tiles.append(jnp.where(lane < 64, r1, r2))
        tiles.append(jnp.where(lane < 32, r2, r3))
    return tiles


def order_matrix(to_columns):
    q = lax.broadcasted_iota(jnp.int32, (LANES, LANES), 0 if to_columns else 1)
    p = lax.broadcasted_iota(jnp.int32, (LANES, LANES), 1 if to_columns else 0)
    return (p == (q % 8) * 16 + q // 8).astype(F32).astype(BF16)


def local_kernel(
    place_ref, x_ref, top_ref, bottom_ref, left_ref, right_ref, w_ref, cw_ref, cb_ref, xw_ref, off_ref,
    *rest,
):
    act_ref, recr_refs, recc_ref = rest[0], rest[1:9], rest[9]
    frame_ref, xwide_ref, slices_ref = rest[10:]
    inner = x_ref.shape[1]
    weight = w_ref[:, :inner]

    def project(v):
        return jnp.dot(v, weight, preferred_element_type=F32).astype(BF16).astype(F32)

    frame_ref[1:9, 8:24, :] = x_ref[...].astype(F32).reshape(8, 16, inner)
    frame_ref[0:1, 8:24, :] = project(top_ref[...]).reshape(1, 16, inner)
    frame_ref[9:10, 8:24, :] = project(bottom_ref[...]).reshape(1, 16, inner)
    left = project(left_ref[...])
    right = project(right_ref[...])
    for i in range(10):
        frame_ref[i, 7:8, :] = left[i : i + 1]
        frame_ref[i, 24:25, :] = right[i : i + 1]
    total = jnp.zeros((8, 16, inner), F32) + cb_ref[...].reshape(1, 1, inner)
    for dc in range(3):
        for dr in range(3):
            k = dr * 3 + dc
            total = total + frame_ref[dr : dr + 8, 7 + dc : 23 + dc, :] * cw_ref[
                k : k + 1, :
            ].reshape(1, 1, inner)
    act = silu(total).reshape(LANES, inner).astype(BF16)
    act_ref[...] = act
    xwide_ref[:, LANES:] = jnp.zeros((inner, LANES), BF16)
    xwide_ref[:, : xw_ref.shape[1]] = xw_ref[...]
    coef = jnp.dot(act, xwide_ref[...], preferred_element_type=F32)
    lane = lane_iota((LANES, LANES))
    off = jnp.broadcast_to(off_ref[...], (LANES, LANES))
    coef_r = jnp.where(lane == OFF_LANE, off, jnp.where(lane < OFF_LANE, coef[:, :LANES], 0.0)).astype(BF16)
    coef_c = jnp.where(
        lane == (OFF_LANE + TURN) % LANES,
        off,
        jnp.where(lane >= TURN, coef[:, :LANES], coef[:, LANES:]),
    ).astype(BF16)
    turn = order_matrix(True)
    act_r = jnp.dot(turn, act, preferred_element_type=F32)
    coef_r = jnp.dot(turn, coef_r, preferred_element_type=F32).astype(BF16)
    wide = act.astype(F32)
    half = coef_c.astype(F32).reshape(8, 16, LANES)
    halves = [
        half[:, 8 * h : 8 * h + 8, :].reshape(64, LANES).astype(BF16) for h in range(2)
    ]
    for k in range(8):
        slices_ref[k] = cut_slice(act_r, k).astype(BF16)
        piece = cut_slice(wide, k).reshape(8, 16, LANES)
        for h in range(2):
            recc_ref[2 * k + h, :, :LANES] = (
                piece[:, 8 * h : 8 * h + 8, :].reshape(64, LANES).astype(BF16)
            )
            recc_ref[2 * k + h, :, LANES:] = halves[h]
    for j in range(8):
        recr_refs[j][:, :LANES] = slices_ref[(place_ref[0] + j) & 7]
        recr_refs[j][:, LANES:] = coef_r


def spread_matrix(spread_ref, turn, width):
    shape = (LANES, width * LANES)
    source = lax.broadcasted_iota(jnp.int32, shape, 0)
    tile = lax.broadcasted_iota(jnp.int32, shape, 1) // LANES
    for o in range(2):
        wanted = (tile + (o * EACH + RANK + turn)) & (LANES - 1)
        spread_ref[o] = (source == wanted).astype(F32).astype(BF16)


def drive(du_ref, dt_ref, act_ref):
    act = act_ref[...].astype(F32)
    for o in range(2):
        du_ref[o] = dt_ref[o] * act


def block_at(i, o, length):
    size = BLOCK * 8
    i = length // size - 1 - i if o == 1 else i
    return pl.multiple_of(i * size, size)


def totals_kernel(pieces, copies, first, turn, place_ref, *refs):
    recs, (dtw_ref, bias_ref, rates_ref) = refs[:pieces], refs[pieces : pieces + 3]
    dt_ref, act_ref, coef_ref, excl_ref, tot_ref, decay_ref = refs[pieces + 3 : pieces + 9]
    du_ref, rows_ref, spread_ref, bx_ref = refs[pieces + 9 :]
    length = act_ref.shape[0]
    step = length // pieces
    for j in range(pieces):
        at = pl.ds(pl.multiple_of(((place_ref[0] - j) & (pieces - 1)) * step, step), step)
        act_ref[at, :] = recs[j][:, :LANES]
        coef_ref[at, :] = recs[j][:, LANES:]
    inner = dtw_ref.shape[2]
    shift = jnp.where(place_ref[1] == 0, 0, inner - SLICE * place_ref[1])
    used = lane_iota((1, LANES)) < SLICE
    rows_ref[...] = jnp.zeros_like(rows_ref)
    coef = coef_ref[...]
    for o in range(2):
        dtw = pltpu.roll(dtw_ref[first + o].astype(F32), shift, 1)[:, :LANES]
        base = (o * EACH + turn) % LANES
        head = min(RANK, LANES - base)
        rows_ref[o, base : base + head, :] = dtw[:head]
        if head < RANK:
            rows_ref[o, : RANK - head, :] = dtw[head:]
        mark = (OFF_LANE + turn) % LANES
        rows_ref[o, mark : mark + 1, :] = jnp.full((1, LANES), -1e30, F32)
        bias = pltpu.roll(bias_ref[...], shift, 1)[first + o : first + o + 1, :LANES]
        bias = jnp.where(used, bias, -1e30)
        rates = pltpu.roll(rates_ref[first + o], shift, 1)[:, :LANES]
        decay_ref[o] = jnp.where(used, rates * -LOG2E, 0.0)
        z = jnp.dot(coef, rows_ref[o].astype(BF16), preferred_element_type=F32) + bias
        dt_ref[o] = softplus(z)
    drive(du_ref, dt_ref, act_ref)
    spread_matrix(spread_ref, turn, STATE)
    sub = lax.broadcasted_iota(jnp.int32, (8, LANES), 0)
    for o in range(2):
        decay = [jnp.broadcast_to(decay_ref[o, n : n + 1, :], (8, LANES)) for n in range(STATE)]

        def advance(i, carry):
            span, states = carry
            states = list(states)
            base = block_at(i, o, length)
            bx_ref[...] = jnp.dot(
                coef_ref[pl.ds(base, BLOCK * 8), :], spread_ref[o], preferred_element_type=F32
            )
            for t in range(BLOCK) if o == 0 else range(BLOCK - 1, -1, -1):
                dt = dt_ref[o, pl.ds(base + t * 8, 8), :]
                du = du_ref[o, pl.ds(base + t * 8, 8), :]
                for n in range(STATE):
                    b = bx_ref[t * 8 : t * 8 + 8, n * LANES : (n + 1) * LANES]
                    states[n] = jnp.exp2(decay[n] * dt) * states[n] + du * b
                span = span + dt
            return span, tuple(states)

        zero = jnp.zeros((8, LANES), F32)
        span, states = lax.fori_loop(0, length // (8 * BLOCK), advance, (zero, (zero,) * STATE))
        states = list(states)
        for k in (1, 2, 4):
            shift_k = k if o == 0 else 8 - k
            keep = sub >= k if o == 0 else sub < 8 - k
            for n in range(STATE):
                moved = jnp.where(keep, pltpu.roll(states[n], shift_k, 0), 0.0)
                states[n] = jnp.exp2(decay[n] * span) * moved + states[n]
            span = span + jnp.where(keep, pltpu.roll(span, shift_k, 0), 0.0)
        shift_k = 1 if o == 0 else 7
        keep = sub >= 1 if o == 0 else sub < 7
        last = 7 if o == 0 else 0
        for n in range(STATE):
            excl_ref[o, n] = jnp.where(keep, pltpu.roll(states[n], shift_k, 0), 0.0)
            for k in range(copies):
                tot_ref[k, o * TOT + n : o * TOT + n + 1, :] = states[n][last : last + 1]
        excl_ref[o, STATE] = jnp.where(keep, pltpu.roll(span, shift_k, 0), 0.0)
        for k in range(copies):
            tot_ref[k, o * TOT + STATE : (o + 1) * TOT, :] = jnp.broadcast_to(
                span[last : last + 1], (TOT - STATE, LANES)
            )


def outputs_kernel(pieces, parts_out, turn, place_ref, dt_ref, act_ref, coef_ref, excl_ref, decay_ref, *refs):
    tots, outs = refs[:pieces], refs[pieces : pieces + parts_out]
    du_ref, spread_ref, bx_ref, sum_ref, gathered_ref = refs[pieces + parts_out :]
    length = act_ref.shape[0]
    chunks = gathered_ref.shape[0]
    place = place_ref[2]
    per = chunks // pieces
    for j in range(pieces):
        at = pl.ds(((place_ref[0] - j) & (pieces - 1)) * per, per)
        gathered_ref[at] = tots[j][...]
    drive(du_ref, dt_ref, act_ref)
    spread_matrix(spread_ref, turn, 2 * STATE)
    for o in range(2):
        rates = decay_ref[o]
        entry = jnp.zeros((STATE, LANES), F32)
        for k in range(chunks) if o == 0 else range(chunks - 1, -1, -1):
            ahead = k < place if o == 0 else k > place
            base = o * TOT
            following = (
                jnp.exp2(rates * gathered_ref[k, base + STATE : base + STATE + 1, :]) * entry
                + gathered_ref[k, base : base + STATE, :]
            )
            entry = jnp.where(ahead, following, entry)
        decay = [jnp.broadcast_to(decay_ref[o, n : n + 1, :], (8, LANES)) for n in range(STATE)]
        states = tuple(
            jnp.exp2(decay[n] * excl_ref[o, STATE]) * entry[n : n + 1] + excl_ref[o, n]
            for n in range(STATE)
        )

        def advance(i, states):
            states = list(states)
            base = block_at(i, o, length)
            bx_ref[...] = jnp.dot(
                coef_ref[pl.ds(base, BLOCK * 8), :], spread_ref[o], preferred_element_type=F32
            )
            for t in range(BLOCK) if o == 0 else range(BLOCK - 1, -1, -1):
                at = pl.ds(base + t * 8, 8)
                dt = dt_ref[o, at, :]
                du = du_ref[o, at, :]
                parts = []
                for n in range(STATE):
                    b = bx_ref[t * 8 : t * 8 + 8, n * LANES : (n + 1) * LANES]
                    c = bx_ref[t * 8 : t * 8 + 8, (STATE + n) * LANES : (STATE + n + 1) * LANES]
                    states[n] = jnp.exp2(decay[n] * dt) * states[n] + du * b
                    parts.append(states[n] * c)
                while len(parts) > 1:
                    parts = [a + b for a, b in zip(parts[::2], parts[1::2])]
                if o == 0:
                    sum_ref[at, :] = parts[0]
                else:
                    sum_ref[at, :] = sum_ref[at, :] + parts[0]
            return tuple(states)

        lax.fori_loop(0, length // (8 * BLOCK), advance, states)
    if parts_out == 1:
        outs[0][...] = sum_ref[...].astype(BF16)
    else:
        step = length // parts_out
        for j in range(parts_out):
            at = pl.multiple_of(((place_ref[0] + j) & (parts_out - 1)) * step, step)
            outs[j][...] = sum_ref[pl.ds(at, step), :].astype(BF16)


def final_kernel(
    place_ref, yc_ref, act_ref, gate_ref, skip_ref, gain_ref, w_ref, live_ref, *refs
):
    yr_refs, out_ref, slices_ref = refs[:8], refs[8], refs[9]
    turn = order_matrix(False)
    for j in range(8):
        slices_ref[(place_ref[0] - j) & 7] = yr_refs[j][...]
    parts = []
    for k in range(8):
        first = jnp.dot(turn, slices_ref[k], preferred_element_type=F32)
        second = jnp.concatenate(
            [yc_ref[2 * k + h].astype(F32).reshape(8, 8, LANES) for h in range(2)], axis=1
        ).reshape(LANES, LANES)
        parts.append(first + second)
    combined = jnp.concatenate(join_slices(parts), axis=1)
    combined = combined + skip_ref[...] * act_ref[...].astype(F32)
    mean = jnp.mean(combined, axis=1, keepdims=True)
    centered = combined - mean
    variance = jnp.mean(centered * centered, axis=1, keepdims=True)
    normed = centered * lax.rsqrt(variance + 1e-05) * gain_ref[...]
    mixed = (normed * silu(gate_ref[...].astype(F32))).astype(BF16)
    out_ref[...] = (
        jnp.dot(mixed, w_ref[...], preferred_element_type=F32) * live_ref[...]
    ).astype(BF16)


def shifted(values, axis, step):
    count = lax.axis_size(axis)
    pairs = [(i, i + step) for i in range(count) if 0 <= i + step < count]
    return lax.ppermute(values, axis, pairs)


def around(values, axis):
    count = lax.axis_size(axis)
    return [
        v if j == 0 else lax.ppermute(v, axis, [(i, (i + j) % count) for i in range(count)])
        for j, v in enumerate(values)
    ]


def per_device(
    patches, tissue, in_weight, conv_weight, conv_bias, x_weight, dt_weight, dt_bias,
    decay_rate, skip_gain, norm_gain, out_weight,
):
    tile_rows, tile_cols, channels = patches.shape
    inner = out_weight.shape[0]
    tokens = tile_rows * tile_cols
    row = lax.axis_index("row").astype(jnp.int32)
    col = lax.axis_index("col").astype(jnp.int32)
    side = row % 2
    place_r = jnp.stack([col, col, row])
    place_c = jnp.stack([col, row // 2, col * 2 + side])
    top = shifted(patches[-1], "row", 1)
    bottom = shifted(patches[0], "row", -1)

    def edge(j):
        return jnp.concatenate([top[j : j + 1], patches[:, j], bottom[j : j + 1]], axis=0)

    left = shifted(edge(tile_cols - 1), "col", 1)
    right = shifted(edge(0), "col", -1)
    projected = jnp.dot(
        patches.reshape(tokens, channels), in_weight, preferred_element_type=F32
    ).astype(BF16)
    x_inner = projected[:, :inner]
    gate = projected[:, inner:]
    live = tissue.reshape(tokens, 1).astype(F32)
    rates = jnp.swapaxes(decay_rate, 1, 2)

    smem = [pl.BlockSpec(memory_space=pltpu.SMEM)]
    outs = call(
        local_kernel,
        (jax.ShapeDtypeStruct((tokens, inner), BF16),)
        + (jax.ShapeDtypeStruct((tokens, 2 * LANES), BF16),) * 8
        + (jax.ShapeDtypeStruct((16, tokens // 2, 2 * LANES), BF16),),
        smem + vmem(10),
        [
            pltpu.VMEM((10, 32, inner), F32),
            pltpu.VMEM((inner, 2 * LANES), BF16),
            pltpu.VMEM((8, tokens, LANES), BF16),
        ],
        name="local",
    )(
        place_r, x_inner, top, bottom, left, right, in_weight,
        conv_weight.reshape(9, inner), conv_bias.reshape(1, inner), x_weight, 1.0 - live,
    )
    act, rec_r, rec_c = outs[0], outs[1:9], outs[9]
    length = 8 * tokens
    wide = (length, LANES)

    def totals(place, recs, copies, first, turn, name):
        return call(
            functools.partial(totals_kernel, len(recs), copies, first, turn),
            (
                jax.ShapeDtypeStruct((2,) + wide, F32),
                jax.ShapeDtypeStruct(wide, BF16),
                jax.ShapeDtypeStruct(wide, BF16),
                jax.ShapeDtypeStruct((2, STATE + 1, 8, LANES), F32),
                jax.ShapeDtypeStruct((copies, 2 * TOT, LANES), F32),
                jax.ShapeDtypeStruct((2, STATE, LANES), F32),
            ),
            smem + vmem(len(recs) + 3),
            [
                pltpu.VMEM((2,) + wide, F32),
                pltpu.VMEM((2, LANES, LANES), F32),
                pltpu.VMEM((2, LANES, STATE * LANES), BF16),
                pltpu.VMEM((8 * BLOCK, STATE * LANES), F32),
            ],
            flops=10**9,
            name=name,
        )(place, *recs, dt_weight, dt_bias, rates)

    def outputs(place, dt, act, coef, excl, decay, tots, out, turn, name):
        pieces = len(tots)
        return call(
            functools.partial(outputs_kernel, pieces, len(out), turn),
            out,
            smem + vmem(pieces + 5),
            [
                pltpu.VMEM((2,) + wide, F32),
                pltpu.VMEM((2, LANES, 2 * STATE * LANES), BF16),
                pltpu.VMEM((8 * BLOCK, 2 * STATE * LANES), F32),
                pltpu.VMEM(wide, F32),
                pltpu.VMEM((16, 2 * TOT, LANES), F32),
            ],
            flops=10**9,
            name=name,
        )(place, dt, act, coef, excl, decay, *tots)

    rec_r = around(rec_r, "col")
    rec_c = lax.all_to_all(rec_c, "row", 0, 0).reshape(length, 2 * LANES)

    dt_r, act_r, coef_r, excl_r, tot_r, decay_r = totals(place_r, rec_r, 16, 0, 0, "totals_rows")
    dt_c, act_c, coef_c, excl_c, tot_c, decay_c = totals(place_c, [rec_c], 1, 2, TURN, "totals_cols")

    tot_r = lax.all_to_all(tot_r, "row", 0, 0)
    mate = lax.ppermute(tot_c, "row", [(i, i ^ 1) for i in range(16)])
    both = jnp.concatenate([jnp.where(side == 0, tot_c, mate), jnp.where(side == 0, mate, tot_c)])
    tot_c = around([both] * 8, "col")

    y_r = outputs(
        place_r, dt_r, act_r, coef_r, excl_r, decay_r, [tot_r],
        (jax.ShapeDtypeStruct((tokens, LANES), BF16),) * 8, 0, "outputs_rows",
    )
    (y_c,) = outputs(
        place_c, dt_c, act_c, coef_c, excl_c, decay_c, tot_c,
        (jax.ShapeDtypeStruct(wide, BF16),), TURN, "outputs_cols",
    )
    y_r = around(y_r, "col")
    y_c = lax.all_to_all(y_c.reshape(16, tokens // 2, LANES), "row", 0, 0)

    result = call(
        final_kernel,
        jax.ShapeDtypeStruct((tokens, channels), BF16),
        smem + vmem(15),
        [pltpu.VMEM((8, tokens, LANES), BF16)],
        name="final",
    )(
        place_r, y_c, act, gate, skip_gain.reshape(1, inner), norm_gain.reshape(1, inner),
        out_weight, live, *y_r,
    )
    return result.reshape(tile_rows, tile_cols, channels)


def solution(mesh):
    in_specs = (P("row", "col", None), P("row", "col")) + (P(),) * 10
    return jax.shard_map(
        per_device, mesh=mesh, in_specs=in_specs, out_specs=P("row", "col", None), check_vma=False
    )
```

time: 174 us -> 122 us (0.70)
  Pallas kernels: 87.5 us -> 38.4 us
  waiting for transfers between devices: 21.9 us -> 9.92 us
  starting transfers between devices: 52 us -> 60.7 us
    pallas_call x6, Pallas kernels: 87.5 us -> 38.4 us  [the longest x2 18.9 us: outputs(): call(functools.partial(outputs_kernel, pieces, len(out), turn), out, smem...]
    ppermute x0 -> x21, starting transfers between devices: none -> 26.3 us  [around(): lax.ppermute(v, axis, [(i, (i + j) % count) for i in range(count)])]
    all_to_all x3 -> x0, starting transfers between devices: 15.3 us -> none  [the longest x1 6.22 us: per_device(): lax.all_to_all(jnp.broadcast_to(both[None], (8,) + both.shape), 'col', 0, 0)]
    all_to_all x3 -> x0, waiting for transfers between devices: 9.23 us -> none  [the longest x1 9.22 us: per_device(): rec_r = lax.all_to_all(rec_r, 'col', 0, 0).reshape(length, 2 * LANES)]
    all_to_all x1, waiting for transfers between devices: 8.49 us -> 0.01 us  [per_device(): y_c = lax.all_to_all(y_c.reshape(16, tokens // 2, LANES), 'row', 0, 0)]
    ppermute x0 -> x21, waiting for transfers between devices: none -> 5.33 us  [around(): lax.ppermute(v, axis, [(i, (i + j) % count) for i in range(count)])]
    unnamed x30 -> x53, local copies, waits for them, and re-layouts: 5.04 us -> 8.59 us
    slice x8 -> x0, local copies, waits for them, and re-layouts: 1.79 us -> none  [the longest x1 0.93 us: slice_params(): dtw = lax.dynamic_slice_in_dim(dt_weight[first:first + 2], at, SLICE, 2)]
  transfers between devices with their start and end apart: 11 -> 29, of which waited for: 4 -> 10; matrix products, arithmetic and copies ran while one was open for 3% -> 3% of each run, Pallas kernels for 48% -> 28%
where the time goes in v2:
time: 122 us
  starting transfers between devices  60.7 us (50%)
  Pallas kernels  38.4 us (31%)
  local copies, waits for them, and re-layouts  10.4 us (9%)
  waiting for transfers between devices  9.92 us (8%)
  matrix products  1.74 us (1%)
    ppermute x21, starting transfers between devices, around(): lax.ppermute(v, axis, [(i, (i + j) % count) for i in range(count)])  26.3 us
    pallas_call x2, Pallas kernels, outputs(): call(functools.partial(outputs_kernel, pieces, len(out), turn), out, smem...  18.9 us
    pallas_call x2, Pallas kernels, totals(): call(functools.partial(totals_kernel, len(recs), copies, first, turn), (j...  14.8 us
    ppermute x4, starting transfers between devices, shifted(): return lax.ppermute(values, axis, pairs)  12.3 us
    all_to_all x1, starting transfers between devices, per_device(): rec_c = lax.all_to_all(rec_c, 'row', 0, 0).reshape(length, 2 * LANES)  9.25 us
    unnamed x53, local copies, waits for them, and re-layouts  8.59 us
    all_to_all x1, starting transfers between devices, per_device(): y_c = lax.all_to_all(y_c.reshape(16, tokens // 2, LANES), 'row', 0, 0)  6.94 us
    all_to_all x1, starting transfers between devices, per_device(): tot_r = lax.all_to_all(tot_r, 'row', 0, 0)  5.52 us
  transfers between devices with their start and end apart: 29, of which 10 were waited for; matrix products, arithmetic and copies ran while one was open for 3% of the time, Pallas kernels for 28%

profile of v2, /device:TPU:1, one launch (start us, length us, event | category | flops | bytes accessed | tf_op | source)
XLA Modules:
  0.0 121.8 jit_solution(3735334788193680516)
XLA Ops:
  0.7 4.0 %collective-permute-start = (bf16[16,384]{1,0:T(8,128)(2,1)S(1)}, bf16[16,384]{1,0:T(8,128)(2,1)S(1)}, u32[]{:S(2)}, u32[]{:S(2)}) collective-permute-start(bf16[16,384]{1,0:T(8,128)(2,1)S(1)} %get-tuple-element.70), channel_id=1, source_target_pairs={{0,8},{8,16},{16,24},{24,32},{32,40},{40,48},{48,56},{56,64},{64,7... | collective-permute-start | bytes 36872 | tf_op jit(solution)/shard_map/ppermute | solution.py:338
  6.1 1.7 %convolution_convert_fusion = bf16[128,1536]{1,0:T(8,128)(2,1)S(1)} fusion(bf16[128,384]{1,0:T(8,128)(2,1)} %bitcast.24, bf16[384,1536]{1,0:T(8,128)(2,1)} %w_ref.2), kind=kOutput, calls=%fused_computation | convolution fusion | flops 151191552 | bytes 1671168 | tf_op jit(solution)/shard_map/dot_general | solution.py:369
  9.2 5.1 %collective-permute-start.2 = (bf16[10,384]{1,0:T(8,128)(2,1)S(1)}, bf16[10,384]{1,0:T(8,128)(2,1)S(1)}, u32[]{:S(2)}, u32[]{:S(2)}) collective-permute-start(bf16[10,384]{1,0:T(8,128)(2,1)S(1)} %pad_maximum_fusion.1), channel_id=1, source_target_pairs={{0,1},{1,2},{2,3},{3,4},{4,5},{5,6},{6,7},{8,9},{9,10},{10,11},{11... | collective-permute-start | bytes 23048 | tf_op jit(solution)/shard_map/ppermute | solution.py:338
  14.4 1.9 %collective-permute-start.3 = (bf16[10,384]{1,0:T(8,128)(2,1)S(1)}, bf16[10,384]{1,0:T(8,128)(2,1)S(1)}, u32[]{:S(2)}, u32[]{:S(2)}) collective-permute-start(bf16[10,384]{1,0:T(8,128)(2,1)S(1)} %pad_maximum_fusion.2), channel_id=1, source_target_pairs={{1,0},{2,1},{3,2},{4,3},{5,4},{6,5},{7,6},{9,8},{10,9},{11,10},{12... | collective-permute-start | bytes 23048 | tf_op jit(solution)/shard_map/ppermute | solution.py:338
  16.6 2.8 %collective-permute-done.3.right_ref = bf16[10,384]{1,0:T(8,128)(2,1)S(1)} collective-permute-done((bf16[10,384]{1,0:T(8,128)(2,1)S(1)}, bf16[10,384]{1,0:T(8,128)(2,1)S(1)}, u32[]{:S(2)}, u32[]{:S(2)}) %collective-permute-start.3) | collective-permute-done | bytes 7712 | tf_op jit(solution)/shard_map/ppermute | solution.py:338
  19.4 2.7 %local.1 = (bf16[128,768]{1,0:T(8,128)(2,1)S(1)}, bf16[128,256]{1,0:T(8,128)(2,1)S(1)}, bf16[128,256]{1,0:T(8,128)(2,1)S(1)}, bf16[128,256]{1,0:T(8,128)(2,1)S(1...) custom-call(s32[3]{0:T(128)S(1)} %pad_add_fusion.place_ref, ...), custom_call_target="tpu_custom_call" | custom-call | flops 10000000 | bytes 4000000 | tf_op jit(solution)/shard_map/local/pallas_call | solution.py:378
  22.1 9.2 %all-to-all-start = ((bf16[16,64,256]{2,1,0:T(8,128)(2,1)}), bf16[16,64,256]{2,1,0:T(8,128)(2,1)S(1)}, u32[]{:S(2)}, u32[]{:S(2)}) async-start(bf16[16,64,256]{2,1,0:T(8,128)(2,1)} %get-tuple-element.35), calls=%async_computation | async-start | bytes 1048576 | tf_op jit(solution)/shard_map/all_to_all | solution.py:438
  33.0 1.6 %collective-permute-start.14 = (bf16[128,256]{1,0:T(8,128)(2,1)S(1)}, bf16[128,256]{1,0:T(8,128)(2,1)S(1)}, u32[]{:S(2)}, u32[]{:S(2)}) collective-permute-start(bf16[128,256]{1,0:T(8,128)(2,1)S(1)} %get-tuple-element.46), channel_id=1, source_target_pairs={{0,3},{1,4},{2,5},{3,6},{4,7},{5,0},{6,1},{7,2},{8,11},{9,12},{10,... | collective-permute-start | bytes 196616 | tf_op jit(solution)/shard_map/ppermute | solution.py:344
  34.6 1.7 %collective-permute-start.15 = (bf16[128,256]{1,0:T(8,128)(2,1)S(1)}, bf16[128,256]{1,0:T(8,128)(2,1)S(1)}, u32[]{:S(2)}, u32[]{:S(2)}) collective-permute-start(bf16[128,256]{1,0:T(8,128)(2,1)S(1)} %get-tuple-element.47), channel_id=1, source_target_pairs={{0,4},{1,5},{2,6},{3,7},{4,0},{5,1},{6,2},{7,3},{8,12},{9,13},{10,... | collective-permute-start | bytes 196616 | tf_op jit(solution)/shard_map/ppermute | solution.py:344
  37.8 2.5 %collective-permute-start.18 = (bf16[128,256]{1,0:T(8,128)(2,1)S(1)}, bf16[128,256]{1,0:T(8,128)(2,1)S(1)}, u32[]{:S(2)}, u32[]{:S(2)}) collective-permute-start(bf16[128,256]{1,0:T(8,128)(2,1)S(1)} %get-tuple-element.50), channel_id=1, source_target_pairs={{0,7},{1,0},{2,1},{3,2},{4,3},{5,4},{6,5},{7,6},{8,15},{9,8},{10,9... | collective-permute-start | bytes 196616 | tf_op jit(solution)/shard_map/ppermute | solution.py:344
  40.3 1.6 %all-to-all-done = bf16[16,64,256]{2,1,0:T(8,128)(2,1)S(1)} async-done(((bf16[16,64,256]{2,1,0:T(8,128)(2,1)}), bf16[16,64,256]{2,1,0:T(8,128)(2,1)S(1)}, u32[]{:S(2)}, u32[]{:S(2)}) %all-to-all-start) | async-done | bytes 524320 | tf_op jit(solution)/shard_map/all_to_all | solution.py:438
  42.0 7.0 %totals_cols.1 = (f32[2,1024,128]{2,1,0:T(8,128)S(1)}, bf16[1024,128]{1,0:T(8,128)(2,1)S(1)}, bf16[1024,128]{1,0:T(8,128)(2,1)S(1)}, f32[2,17,8,128]{3,2,1,0:T(8...) custom-call(s32[3]{0:T(128)S(1)} %pad_add_fusion.1.place_ref, bf16[1024,256]{1,0:T(8,128)(2,1)S(1)} %bitcast.21, ...), custom_call_target="tpu_custom_call" | custom-call | flops 1000000000 | bytes 4000000 | tf_op jit(solution)/shard_map/totals_cols/pallas_call | solution.py:399
  51.0 7.8 %totals_rows.1 = (f32[2,1024,128]{2,1,0:T(8,128)S(1)}, bf16[1024,128]{1,0:T(8,128)(2,1)S(1)}, bf16[1024,128]{1,0:T(8,128)(2,1)S(1)}, f32[2,17,8,128]{3,2,1,0:T(8...) custom-call(s32[3]{0:T(128)S(1)} %pad_add_fusion.place_ref, ...), custom_call_target="tpu_custom_call" | custom-call | flops 1000000000 | bytes 4000000 | tf_op jit(solution)/shard_map/totals_rows/pallas_call | solution.py:399
  60.5 5.5 %all-to-all-start.2 = ((f32[16,48,128]{2,1,0:T(8,128)}), f32[16,48,128]{2,1,0:T(8,128)S(1)}, u32[]{:S(2)}, u32[]{:S(2)}) async-start(f32[16,48,128]{2,1,0:T(8,128)} %get-tuple-element.56), calls=%async_computation.2 | async-start | bytes 786432 | tf_op jit(solution)/shard_map/all_to_all | solution.py:443
  67.0 1.7 %collective-permute-start.6 = (f32[2,48,128]{2,1,0:T(8,128)S(1)}, f32[2,48,128]{2,1,0:T(8,128)S(1)}, u32[]{:S(2)}, u32[]{:S(2)}) collective-permute-start(f32[2,48,128]{2,1,0:T(8,128)S(1)} %pad_maximum_fusion.refs_0_), channel_id=1, source_target_pairs={{0,2},{1,3},{2,4},{3,5},{4,6},{5,7},{6,0},{7,1},{8,10},{9,11},{10,... | collective-permute-start | bytes 147464 | tf_op jit(solution)/shard_map/ppermute | solution.py:344
  70.4 2.6 %collective-permute-start.9 = (f32[2,48,128]{2,1,0:T(8,128)S(1)}, f32[2,48,128]{2,1,0:T(8,128)S(1)}, u32[]{:S(2)}, u32[]{:S(2)}) collective-permute-start(f32[2,48,128]{2,1,0:T(8,128)S(1)} %pad_maximum_fusion.refs_0_), channel_id=1, source_target_pairs={{0,5},{1,6},{2,7},{3,0},{4,1},{5,2},{6,3},{7,4},{8,13},{9,14},{10,... | collective-permute-start | bytes 147464 | tf_op jit(solution)/shard_map/ppermute | solution.py:344
  73.1 2.1 %collective-permute-start.11 = (f32[2,48,128]{2,1,0:T(8,128)S(1)}, f32[2,48,128]{2,1,0:T(8,128)S(1)}, u32[]{:S(2)}, u32[]{:S(2)}) collective-permute-start(f32[2,48,128]{2,1,0:T(8,128)S(1)} %pad_maximum_fusion.refs_0_), channel_id=1, source_target_pairs={{0,7},{1,0},{2,1},{3,2},{4,3},{5,4},{6,5},{7,6},{8,15},{9,8},{10,9... | collective-permute-start | bytes 147464 | tf_op jit(solution)/shard_map/ppermute | solution.py:344
  79.2 9.8 %outputs_cols.1 = bf16[1024,128]{1,0:T(8,128)(2,1)} custom-call(s32[3]{0:T(128)S(1)} %pad_add_fusion.1.place_ref, f32[2,1024,128]{2,1,0:T(8,128)S(1)} %copy-done.6, bf16[1024,128]{1,0:T(8,128)(2,1)S(1)} %get-tuple-element.37.act_ref, bf16[1024,128]{1,0:T(8,128)(2,1)S(1)} %copy-done.10, f32[2,17,8,128]{3,2,1,0:T(8,128)S(1)} %copy-done.16, ...), custom_call_target="tpu_custom_call" | custom-call | flops 1000000000 | bytes 4000000 | tf_op jit(solution)/shard_map/outputs_cols/pallas_call | solution.py:422
  89.0 6.9 %all-to-all-start.1 = ((bf16[16,64,128]{2,1,0:T(8,128)(2,1)}), bf16[16,64,128]{2,1,0:T(8,128)(2,1)S(1)}, u32[]{:S(2)}, u32[]{:S(2)}) async-start(bf16[16,64,128]{2,1,0:T(8,128)(2,1)} %bitcast.11), calls=%async_computation.1 | async-start | bytes 524288 | tf_op jit(solution)/shard_map/all_to_all | solution.py:457
  98.8 9.2 %outputs_rows.1 = (bf16[128,128]{1,0:T(8,128)(2,1)S(1)}, bf16[128,128]{1,0:T(8,128)(2,1)S(1)}, bf16[128,128]{1,0:T(8,128)(2,1)S(1)}, bf16[128,128]{1,0:T(8,128)(...) custom-call(s32[3]{0:T(128)S(1)} %pad_add_fusion.place_ref, ...), custom_call_target="tpu_custom_call" | custom-call | flops 1000000000 | bytes 4000000 | tf_op jit(solution)/shard_map/outputs_rows/pallas_call | solution.py:422
  109.9 2.9 %collective-permute-start.21 = (bf16[128,128]{1,0:T(8,128)(2,1)S(1)}, bf16[128,128]{1,0:T(8,128)(2,1)S(1)}, u32[]{:S(2)}, u32[]{:S(2)}) collective-permute-start(bf16[128,128]{1,0:T(8,128)(2,1)S(1)} %get-tuple-element.60), channel_id=1, source_target_pairs={{0,3},{1,4},{2,5},{3,6},{4,7},{5,0},{6,1},{7,2},{8,11},{9,12},{10,... | collective-permute-start | bytes 98312 | tf_op jit(solution)/shard_map/ppermute | solution.py:344
  112.9 2.3 %collective-permute-start.23 = (bf16[128,128]{1,0:T(8,128)(2,1)S(1)}, bf16[128,128]{1,0:T(8,128)(2,1)S(1)}, u32[]{:S(2)}, u32[]{:S(2)}) collective-permute-start(bf16[128,128]{1,0:T(8,128)(2,1)S(1)} %get-tuple-element.62), channel_id=1, source_target_pairs={{0,5},{1,6},{2,7},{3,0},{4,1},{5,2},{6,3},{7,4},{8,13},{9,14},{10,... | collective-permute-start | bytes 98312 | tf_op jit(solution)/shard_map/ppermute | solution.py:344
  117.9 1.9 %collective-permute-done.25.refs_7_ = bf16[128,128]{1,0:T(8,128)(2,1)S(1)} collective-permute-done((bf16[128,128]{1,0:T(8,128)(2,1)S(1)}, bf16[128,128]{1,0:T(8,128)(2,1)S(1)}, u32[]{:S(2)}, u32[]{:S(2)}) %collective-permute-start.25) | collective-permute-done | bytes 32800 | tf_op jit(solution)/shard_map/ppermute | solution.py:344
  119.8 2.0 %final.1 = bf16[128,384]{1,0:T(8,128)(2,1)} custom-call(s32[3]{0:T(128)S(1)} %pad_add_fusion.place_ref, bf16[16,64,128]{2,1,0:T(8,128)(2,1)S(1)} %all-to-all-done.1.yc_ref, bf16[128,768]{1,0:T(8,128)(2,1)S(1)} %get-tuple-element.42.act_ref, bf16[128,768]{1,0:T(8,128)(2,1)S(1)} %get-tuple-element.65.gate_ref, f32[1,768]{1,0:T(1,128)S(1)} %reshape.51.skip_ref, ...), custom_call_target="tpu_custom_call" | custom-call | flops 10000000 | bytes 4000000 | tf_op jit(solution)/shard_map/final/pallas_call | solution.py:459
  (112 shorter events, 24.6 us)
Async XLA Ops:
  0.7 8.5 %collective-permute-start = (bf16[16,384]{1,0:T(8,128)(2,1)S(1)}, bf16[16,384]{1,0:T(8,128)(2,1)S(1)}, u32[]{:S(2)}, u32[]{:S(2)}) collective-permute-start(bf16[16,384]{1,0:T(8,128)(2,1)S(1)} %get-tuple-element.70), channel_id=1, source_target_pairs={{0,8},{8,16},{16,24},{24,32},{32,40},{40,48},{48,56},{56,64},{64,7... | collective-permute-start | bytes 36872 | tf_op jit(solution)/shard_map/ppermute | solution.py:338
  9.2 7.4 %collective-permute-start.2 = (bf16[10,384]{1,0:T(8,128)(2,1)S(1)}, bf16[10,384]{1,0:T(8,128)(2,1)S(1)}, u32[]{:S(2)}, u32[]{:S(2)}) collective-permute-start(bf16[10,384]{1,0:T(8,128)(2,1)S(1)} %pad_maximum_fusion.1), channel_id=1, source_target_pairs={{0,1},{1,2},{2,3},{3,4},{4,5},{5,6},{6,7},{8,9},{9,10},{10,11},{11... | collective-permute-start | bytes 23048 | tf_op jit(solution)/shard_map/ppermute | solution.py:338
  14.4 5.0 %collective-permute-start.3 = (bf16[10,384]{1,0:T(8,128)(2,1)S(1)}, bf16[10,384]{1,0:T(8,128)(2,1)S(1)}, u32[]{:S(2)}, u32[]{:S(2)}) collective-permute-start(bf16[10,384]{1,0:T(8,128)(2,1)S(1)} %pad_maximum_fusion.2), channel_id=1, source_target_pairs={{1,0},{2,1},{3,2},{4,3},{5,4},{6,5},{7,6},{9,8},{10,9},{11,10},{12... | collective-permute-start | bytes 23048 | tf_op jit(solution)/shard_map/ppermute | solution.py:338
  22.1 19.9 %all-to-all-start = ((bf16[16,64,256]{2,1,0:T(8,128)(2,1)}), bf16[16,64,256]{2,1,0:T(8,128)(2,1)S(1)}, u32[]{:S(2)}, u32[]{:S(2)}) async-start(bf16[16,64,256]{2,1,0:T(8,128)(2,1)} %get-tuple-element.35), calls=%async_computation | async-start | bytes 1048576 | tf_op jit(solution)/shard_map/all_to_all | solution.py:438
  31.4 5.7 %collective-permute-start.12 = (bf16[128,256]{1,0:T(8,128)(2,1)S(1)}, bf16[128,256]{1,0:T(8,128)(2,1)S(1)}, u32[]{:S(2)}, u32[]{:S(2)}) collective-permute-start(bf16[128,256]{1,0:T(8,128)(2,1)S(1)} %get-tuple-element.44), channel_id=1, source_target_pairs={{0,1},{1,2},{2,3},{3,4},{4,5},{5,6},{6,7},{7,0},{8,9},{9,10},{10,1... | collective-permute-start | bytes 196616 | tf_op jit(solution)/shard_map/ppermute | solution.py:344
  31.7 6.1 %collective-permute-start.13 = (bf16[128,256]{1,0:T(8,128)(2,1)S(1)}, bf16[128,256]{1,0:T(8,128)(2,1)S(1)}, u32[]{:S(2)}, u32[]{:S(2)}) collective-permute-start(bf16[128,256]{1,0:T(8,128)(2,1)S(1)} %get-tuple-element.45), channel_id=1, source_target_pairs={{0,2},{1,3},{2,4},{3,5},{4,6},{5,7},{6,0},{7,1},{8,10},{9,11},{10,... | collective-permute-start | bytes 196616 | tf_op jit(solution)/shard_map/ppermute | solution.py:344
  33.0 17.7 %collective-permute-start.14 = (bf16[128,256]{1,0:T(8,128)(2,1)S(1)}, bf16[128,256]{1,0:T(8,128)(2,1)S(1)}, u32[]{:S(2)}, u32[]{:S(2)}) collective-permute-start(bf16[128,256]{1,0:T(8,128)(2,1)S(1)} %get-tuple-element.46), channel_id=1, source_target_pairs={{0,3},{1,4},{2,5},{3,6},{4,7},{5,0},{6,1},{7,2},{8,11},{9,12},{10,... | collective-permute-start | bytes 196616 | tf_op jit(solution)/shard_map/ppermute | solution.py:344
  34.6 16.4 %collective-permute-start.15 = (bf16[128,256]{1,0:T(8,128)(2,1)S(1)}, bf16[128,256]{1,0:T(8,128)(2,1)S(1)}, u32[]{:S(2)}, u32[]{:S(2)}) collective-permute-start(bf16[128,256]{1,0:T(8,128)(2,1)S(1)} %get-tuple-element.47), channel_id=1, source_target_pairs={{0,4},{1,5},{2,6},{3,7},{4,0},{5,1},{6,2},{7,3},{8,12},{9,13},{10,... | collective-permute-start | bytes 196616 | tf_op jit(solution)/shard_map/ppermute | solution.py:344
  36.3 14.6 %collective-permute-start.16 = (bf16[128,256]{1,0:T(8,128)(2,1)S(1)}, bf16[128,256]{1,0:T(8,128)(2,1)S(1)}, u32[]{:S(2)}, u32[]{:S(2)}) collective-permute-start(bf16[128,256]{1,0:T(8,128)(2,1)S(1)} %get-tuple-element.48), channel_id=1, source_target_pairs={{0,5},{1,6},{2,7},{3,0},{4,1},{5,2},{6,3},{7,4},{8,13},{9,14},{10,... | collective-permute-start | bytes 196616 | tf_op jit(solution)/shard_map/ppermute | solution.py:344
  37.1 13.9 %collective-permute-start.17 = (bf16[128,256]{1,0:T(8,128)(2,1)S(1)}, bf16[128,256]{1,0:T(8,128)(2,1)S(1)}, u32[]{:S(2)}, u32[]{:S(2)}) collective-permute-start(bf16[128,256]{1,0:T(8,128)(2,1)S(1)} %get-tuple-element.49), channel_id=1, source_target_pairs={{0,6},{1,7},{2,0},{3,1},{4,2},{5,3},{6,4},{7,5},{8,14},{9,15},{10,... | collective-permute-start | bytes 196616 | tf_op jit(solution)/shard_map/ppermute | solution.py:344
  37.8 13.2 %collective-permute-start.18 = (bf16[128,256]{1,0:T(8,128)(2,1)S(1)}, bf16[128,256]{1,0:T(8,128)(2,1)S(1)}, u32[]{:S(2)}, u32[]{:S(2)}) collective-permute-start(bf16[128,256]{1,0:T(8,128)(2,1)S(1)} %get-tuple-element.50), channel_id=1, source_target_pairs={{0,7},{1,0},{2,1},{3,2},{4,3},{5,4},{6,5},{7,6},{8,15},{9,8},{10,9... | collective-permute-start | bytes 196616 | tf_op jit(solution)/shard_map/ppermute | solution.py:344
  50.7 15.4 %collective-permute-start.4 = (f32[1,48,128]{2,1,0:T(8,128)S(1)}, f32[1,48,128]{2,1,0:T(8,128)S(1)}, u32[]{:S(2)}, u32[]{:S(2)}) collective-permute-start(f32[1,48,128]{2,1,0:T(8,128)S(1)} %get-tuple-element.41), channel_id=1, source_target_pairs={{0,8},{8,0},{16,24},{24,16},{32,40},{40,32},{48,56},{56,48},{64,72... | collective-permute-start | bytes 73736 | tf_op jit(solution)/shard_map/ppermute | solution.py:444
  60.5 28.5 %all-to-all-start.2 = ((f32[16,48,128]{2,1,0:T(8,128)}), f32[16,48,128]{2,1,0:T(8,128)S(1)}, u32[]{:S(2)}, u32[]{:S(2)}) async-start(f32[16,48,128]{2,1,0:T(8,128)} %get-tuple-element.56), calls=%async_computation.2 | async-start | bytes 786432 | tf_op jit(solution)/shard_map/all_to_all | solution.py:443
  66.1 7.0 %collective-permute-start.5 = (f32[2,48,128]{2,1,0:T(8,128)S(1)}, f32[2,48,128]{2,1,0:T(8,128)S(1)}, u32[]{:S(2)}, u32[]{:S(2)}) collective-permute-start(f32[2,48,128]{2,1,0:T(8,128)S(1)} %pad_maximum_fusion.refs_0_), channel_id=1, source_target_pairs={{0,1},{1,2},{2,3},{3,4},{4,5},{5,6},{6,7},{7,0},{8,9},{9,10},{10,1... | collective-permute-start | bytes 147464 | tf_op jit(solution)/shard_map/ppermute | solution.py:344
  67.0 6.0 %collective-permute-start.6 = (f32[2,48,128]{2,1,0:T(8,128)S(1)}, f32[2,48,128]{2,1,0:T(8,128)S(1)}, u32[]{:S(2)}, u32[]{:S(2)}) collective-permute-start(f32[2,48,128]{2,1,0:T(8,128)S(1)} %pad_maximum_fusion.refs_0_), channel_id=1, source_target_pairs={{0,2},{1,3},{2,4},{3,5},{4,6},{5,7},{6,0},{7,1},{8,10},{9,11},{10,... | collective-permute-start | bytes 147464 | tf_op jit(solution)/shard_map/ppermute | solution.py:344
  68.8 6.4 %collective-permute-start.7 = (f32[2,48,128]{2,1,0:T(8,128)S(1)}, f32[2,48,128]{2,1,0:T(8,128)S(1)}, u32[]{:S(2)}, u32[]{:S(2)}) collective-permute-start(f32[2,48,128]{2,1,0:T(8,128)S(1)} %pad_maximum_fusion.refs_0_), channel_id=1, source_target_pairs={{0,3},{1,4},{2,5},{3,6},{4,7},{5,0},{6,1},{7,2},{8,11},{9,12},{10,... | collective-permute-start | bytes 147464 | tf_op jit(solution)/shard_map/ppermute | solution.py:344
  69.3 5.9 %collective-permute-start.8 = (f32[2,48,128]{2,1,0:T(8,128)S(1)}, f32[2,48,128]{2,1,0:T(8,128)S(1)}, u32[]{:S(2)}, u32[]{:S(2)}) collective-permute-start(f32[2,48,128]{2,1,0:T(8,128)S(1)} %pad_maximum_fusion.refs_0_), channel_id=1, source_target_pairs={{0,4},{1,5},{2,6},{3,7},{4,0},{5,1},{6,2},{7,3},{8,12},{9,13},{10,... | collective-permute-start | bytes 147464 | tf_op jit(solution)/shard_map/ppermute | solution.py:344
  70.4 5.3 %collective-permute-start.9 = (f32[2,48,128]{2,1,0:T(8,128)S(1)}, f32[2,48,128]{2,1,0:T(8,128)S(1)}, u32[]{:S(2)}, u32[]{:S(2)}) collective-permute-start(f32[2,48,128]{2,1,0:T(8,128)S(1)} %pad_maximum_fusion.refs_0_), channel_id=1, source_target_pairs={{0,5},{1,6},{2,7},{3,0},{4,1},{5,2},{6,3},{7,4},{8,13},{9,14},{10,... | collective-permute-start | bytes 147464 | tf_op jit(solution)/shard_map/ppermute | solution.py:344
  89.0 30.8 %all-to-all-start.1 = ((bf16[16,64,128]{2,1,0:T(8,128)(2,1)}), bf16[16,64,128]{2,1,0:T(8,128)(2,1)S(1)}, u32[]{:S(2)}, u32[]{:S(2)}) async-start(bf16[16,64,128]{2,1,0:T(8,128)(2,1)} %bitcast.11), calls=%async_computation.1 | async-start | bytes 524288 | tf_op jit(solution)/shard_map/all_to_all | solution.py:457
  108.0 7.2 %collective-permute-start.19 = (bf16[128,128]{1,0:T(8,128)(2,1)S(1)}, bf16[128,128]{1,0:T(8,128)(2,1)S(1)}, u32[]{:S(2)}, u32[]{:S(2)}) collective-permute-start(bf16[128,128]{1,0:T(8,128)(2,1)S(1)} %get-tuple-element.58), channel_id=1, source_target_pairs={{0,1},{1,2},{2,3},{3,4},{4,5},{5,6},{6,7},{7,0},{8,9},{9,10},{10,1... | collective-permute-start | bytes 98312 | tf_op jit(solution)/shard_map/ppermute | solution.py:344
  109.4 6.6 %collective-permute-start.20 = (bf16[128,128]{1,0:T(8,128)(2,1)S(1)}, bf16[128,128]{1,0:T(8,128)(2,1)S(1)}, u32[]{:S(2)}, u32[]{:S(2)}) collective-permute-start(bf16[128,128]{1,0:T(8,128)(2,1)S(1)} %get-tuple-element.59), channel_id=1, source_target_pairs={{0,2},{1,3},{2,4},{3,5},{4,6},{5,7},{6,0},{7,1},{8,10},{9,11},{10,... | collective-permute-start | bytes 98312 | tf_op jit(solution)/shard_map/ppermute | solution.py:344
  109.9 6.4 %collective-permute-start.21 = (bf16[128,128]{1,0:T(8,128)(2,1)S(1)}, bf16[128,128]{1,0:T(8,128)(2,1)S(1)}, u32[]{:S(2)}, u32[]{:S(2)}) collective-permute-start(bf16[128,128]{1,0:T(8,128)(2,1)S(1)} %get-tuple-element.60), channel_id=1, source_target_pairs={{0,3},{1,4},{2,5},{3,6},{4,7},{5,0},{6,1},{7,2},{8,11},{9,12},{10,... | collective-permute-start | bytes 98312 | tf_op jit(solution)/shard_map/ppermute | solution.py:344
  112.9 4.7 %collective-permute-start.22 = (bf16[128,128]{1,0:T(8,128)(2,1)S(1)}, bf16[128,128]{1,0:T(8,128)(2,1)S(1)}, u32[]{:S(2)}, u32[]{:S(2)}) collective-permute-start(bf16[128,128]{1,0:T(8,128)(2,1)S(1)} %get-tuple-element.61), channel_id=1, source_target_pairs={{0,4},{1,5},{2,6},{3,7},{4,0},{5,1},{6,2},{7,3},{8,12},{9,13},{10,... | collective-permute-start | bytes 98312 | tf_op jit(solution)/shard_map/ppermute | solution.py:344
  112.9 5.0 %collective-permute-start.23 = (bf16[128,128]{1,0:T(8,128)(2,1)S(1)}, bf16[128,128]{1,0:T(8,128)(2,1)S(1)}, u32[]{:S(2)}, u32[]{:S(2)}) collective-permute-start(bf16[128,128]{1,0:T(8,128)(2,1)S(1)} %get-tuple-element.62), channel_id=1, source_target_pairs={{0,5},{1,6},{2,7},{3,0},{4,1},{5,2},{6,3},{7,4},{8,13},{9,14},{10,... | collective-permute-start | bytes 98312 | tf_op jit(solution)/shard_map/ppermute | solution.py:344
  (30 other events, 279.3 us)

commit v3 on v2

--- a/solution.py
+++ b/solution.py
@@ -18,7 +18,7 @@
 OFF_LANE = 2 * EACH
 TOT = 24
 TURN = OFF_LANE
-BLOCK = 16
+BLOCK = 32
 LOG2E = math.log2(math.e)
 
 
@@ -26,14 +26,14 @@
     return [pl.BlockSpec(memory_space=pltpu.VMEM)] * count
 
 
-def call(kernel, out_shape, in_specs, scratch=(), flops=10**7, name=None):
+def call(kernel, out_shape, in_specs, scratch=(), flops=10**7, grant=16, name=None):
     return pl.pallas_call(
         kernel,
         out_shape=out_shape,
         in_specs=in_specs,
         out_specs=jax.tree.map(lambda _: pl.BlockSpec(memory_space=pltpu.VMEM), out_shape),
         scratch_shapes=list(scratch),
-        compiler_params=pltpu.CompilerParams(vmem_limit_bytes=48 << 20),
+        compiler_params=pltpu.CompilerParams(vmem_limit_bytes=grant << 20),
         cost_estimate=pl.CostEstimate(flops=flops, bytes_accessed=4 * 10**6, transcendentals=0),
         name=name,
     )
@@ -155,10 +155,23 @@
         spread_ref[o] = (source == wanted).astype(F32).astype(BF16)
 
 
-def drive(du_ref, dt_ref, act_ref):
-    act = act_ref[...].astype(F32)
-    for o in range(2):
-        du_ref[o] = dt_ref[o] * act
+def prepare(recs, place, rows_ref, bias, dt_ref, du_ref, coef_ref):
+    length = coef_ref.shape[0]
+    size = length // 8
+    for j in range(8):
+        if len(recs) == 1:
+            rec = recs[0].at[j * size : (j + 1) * size]
+            at = pl.ds(j * size, size)
+        else:
+            rec = recs[j]
+            at = pl.ds(pl.multiple_of(((place - j) & 7) * size, size), size)
+        coef = rec[:, LANES:]
+        act = rec[:, :LANES].astype(F32)
+        coef_ref[at, :] = coef
+        for o in range(2):
+            dt = softplus(jnp.dot(coef, rows_ref[o], preferred_element_type=F32) + bias[o])
+            dt_ref[o, at, :] = dt
+            du_ref[o, at, :] = dt * act
 
 
 def block_at(i, o, length):
@@ -169,35 +182,29 @@
 
 def totals_kernel(pieces, copies, first, turn, place_ref, *refs):
     recs, (dtw_ref, bias_ref, rates_ref) = refs[:pieces], refs[pieces : pieces + 3]
-    dt_ref, act_ref, coef_ref, excl_ref, tot_ref, decay_ref = refs[pieces + 3 : pieces + 9]
-    du_ref, rows_ref, spread_ref, bx_ref = refs[pieces + 9 :]
-    length = act_ref.shape[0]
-    step = length // pieces
-    for j in range(pieces):
-        at = pl.ds(pl.multiple_of(((place_ref[0] - j) & (pieces - 1)) * step, step), step)
-        act_ref[at, :] = recs[j][:, :LANES]
-        coef_ref[at, :] = recs[j][:, LANES:]
+    excl_ref, tot_ref, decay_ref, rows_ref = refs[pieces + 3 : pieces + 7]
+    dt_ref, du_ref, coef_ref, wide_ref, spread_ref, bx_ref = refs[pieces + 7 :]
+    length = coef_ref.shape[0]
     inner = dtw_ref.shape[2]
     shift = jnp.where(place_ref[1] == 0, 0, inner - SLICE * place_ref[1])
     used = lane_iota((1, LANES)) < SLICE
-    rows_ref[...] = jnp.zeros_like(rows_ref)
-    coef = coef_ref[...]
+    wide_ref[...] = jnp.zeros_like(wide_ref)
     for o in range(2):
         dtw = pltpu.roll(dtw_ref[first + o].astype(F32), shift, 1)[:, :LANES]
         base = (o * EACH + turn) % LANES
         head = min(RANK, LANES - base)
-        rows_ref[o, base : base + head, :] = dtw[:head]
+        wide_ref[o, base : base + head, :] = dtw[:head]
         if head < RANK:
-            rows_ref[o, : RANK - head, :] = dtw[head:]
+            wide_ref[o, : RANK - head, :] = dtw[head:]
         mark = (OFF_LANE + turn) % LANES
-        rows_ref[o, mark : mark + 1, :] = jnp.full((1, LANES), -1e30, F32)
+        wide_ref[o, mark : mark + 1, :] = jnp.full((1, LANES), -1e30, F32)
+        rows_ref[o] = wide_ref[o].astype(BF16)
         bias = pltpu.roll(bias_ref[...], shift, 1)[first + o : first + o + 1, :LANES]
-        bias = jnp.where(used, bias, -1e30)
         rates = pltpu.roll(rates_ref[first + o], shift, 1)[:, :LANES]
-        decay_ref[o] = jnp.where(used, rates * -LOG2E, 0.0)
-        z = jnp.dot(coef, rows_ref[o].astype(BF16), preferred_element_type=F32) + bias
-        dt_ref[o] = softplus(z)
-    drive(du_ref, dt_ref, act_ref)
+        decay_ref[o, :STATE] = jnp.where(used, rates * -LOG2E, 0.0)
+        decay_ref[o, STATE:] = jnp.broadcast_to(jnp.where(used, bias, -1e30), (TOT - STATE, LANES))
+    bias = [decay_ref[o, STATE : STATE + 1, :] for o in range(2)]
+    prepare(recs, place_ref[0], rows_ref, bias, dt_ref, du_ref, coef_ref)
     spread_matrix(spread_ref, turn, STATE)
     sub = lax.broadcasted_iota(jnp.int32, (8, LANES), 0)
     for o in range(2):
@@ -243,20 +250,17 @@
             )
 
 
-def outputs_kernel(pieces, parts_out, turn, place_ref, dt_ref, act_ref, coef_ref, excl_ref, decay_ref, *refs):
-    tots, outs = refs[:pieces], refs[pieces : pieces + parts_out]
-    du_ref, spread_ref, bx_ref, sum_ref, gathered_ref = refs[pieces + parts_out :]
-    length = act_ref.shape[0]
+def outputs_kernel(pieces, parts_out, turn, place_ref, gathered_ref, excl_ref, decay_ref, rows_ref, *refs):
+    recs, outs = refs[:pieces], refs[pieces : pieces + parts_out]
+    dt_ref, du_ref, coef_ref, spread_ref, bx_ref, sum_ref = refs[pieces + parts_out :]
+    length = coef_ref.shape[0]
     chunks = gathered_ref.shape[0]
+    bias = [decay_ref[o, STATE : STATE + 1, :] for o in range(2)]
+    prepare(recs, place_ref[0], rows_ref, bias, dt_ref, du_ref, coef_ref)
     place = place_ref[2]
-    per = chunks // pieces
-    for j in range(pieces):
-        at = pl.ds(((place_ref[0] - j) & (pieces - 1)) * per, per)
-        gathered_ref[at] = tots[j][...]
-    drive(du_ref, dt_ref, act_ref)
     spread_matrix(spread_ref, turn, 2 * STATE)
     for o in range(2):
-        rates = decay_ref[o]
+        rates = decay_ref[o, :STATE]
         entry = jnp.zeros((STATE, LANES), F32)
         for k in range(chunks) if o == 0 else range(chunks - 1, -1, -1):
             ahead = k < place if o == 0 else k > place
@@ -395,64 +399,70 @@
     length = 8 * tokens
     wide = (length, LANES)
 
+    scratch = [
+        pltpu.VMEM((2,) + wide, F32),
+        pltpu.VMEM((2,) + wide, F32),
+        pltpu.VMEM(wide, BF16),
+    ]
+
     def totals(place, recs, copies, first, turn, name):
         return call(
             functools.partial(totals_kernel, len(recs), copies, first, turn),
             (
-                jax.ShapeDtypeStruct((2,) + wide, F32),
-                jax.ShapeDtypeStruct(wide, BF16),
-                jax.ShapeDtypeStruct(wide, BF16),
                 jax.ShapeDtypeStruct((2, STATE + 1, 8, LANES), F32),
                 jax.ShapeDtypeStruct((copies, 2 * TOT, LANES), F32),
-                jax.ShapeDtypeStruct((2, STATE, LANES), F32),
+                jax.ShapeDtypeStruct((2, TOT, LANES), F32),
+                jax.ShapeDtypeStruct((2, LANES, LANES), BF16),
             ),
             smem + vmem(len(recs) + 3),
-            [
-                pltpu.VMEM((2,) + wide, F32),
+            scratch
+            + [
                 pltpu.VMEM((2, LANES, LANES), F32),
                 pltpu.VMEM((2, LANES, STATE * LANES), BF16),
                 pltpu.VMEM((8 * BLOCK, STATE * LANES), F32),
             ],
             flops=10**9,
+            grant=20,
             name=name,
         )(place, *recs, dt_weight, dt_bias, rates)
 
-    def outputs(place, dt, act, coef, excl, decay, tots, out, turn, name):
-        pieces = len(tots)
+    def outputs(place, tot, excl, decay, rows, recs, out, turn, name):
         return call(
-            functools.partial(outputs_kernel, pieces, len(out), turn),
+            functools.partial(outputs_kernel, len(recs), len(out), turn),
             out,
-            smem + vmem(pieces + 5),
-            [
-                pltpu.VMEM((2,) + wide, F32),
+            smem + vmem(len(recs) + 4),
+            scratch
+            + [
                 pltpu.VMEM((2, LANES, 2 * STATE * LANES), BF16),
                 pltpu.VMEM((8 * BLOCK, 2 * STATE * LANES), F32),
                 pltpu.VMEM(wide, F32),
-                pltpu.VMEM((16, 2 * TOT, LANES), F32),
             ],
             flops=10**9,
+            grant=24,
             name=name,
-        )(place, dt, act, coef, excl, decay, *tots)
+        )(place, tot, excl, decay, rows, *recs)
 
     rec_r = around(rec_r, "col")
     rec_c = lax.all_to_all(rec_c, "row", 0, 0).reshape(length, 2 * LANES)
 
-    dt_r, act_r, coef_r, excl_r, tot_r, decay_r = totals(place_r, rec_r, 16, 0, 0, "totals_rows")
-    dt_c, act_c, coef_c, excl_c, tot_c, decay_c = totals(place_c, [rec_c], 1, 2, TURN, "totals_cols")
+    excl_r, tot_r, decay_r, rows_r = totals(place_r, rec_r, 16, 0, 0, "totals_rows")
+    excl_c, tot_c, decay_c, rows_c = totals(place_c, [rec_c], 1, 2, TURN, "totals_cols")
 
     tot_r = lax.all_to_all(tot_r, "row", 0, 0)
     mate = lax.ppermute(tot_c, "row", [(i, i ^ 1) for i in range(16)])
     both = jnp.concatenate([jnp.where(side == 0, tot_c, mate), jnp.where(side == 0, mate, tot_c)])
-    tot_c = around([both] * 8, "col")
+    tot_c = lax.all_to_all(jnp.broadcast_to(both[None], (8,) + both.shape), "col", 0, 0)
+    tot_c = tot_c.reshape(16, 2 * TOT, LANES)
 
     y_r = outputs(
-        place_r, dt_r, act_r, coef_r, excl_r, decay_r, [tot_r],
+        place_r, tot_r, excl_r, decay_r, rows_r, rec_r,
         (jax.ShapeDtypeStruct((tokens, LANES), BF16),) * 8, 0, "outputs_rows",
     )
     (y_c,) = outputs(
-        place_c, dt_c, act_c, coef_c, excl_c, decay_c, tot_c,
+        place_c, tot_c, excl_c, decay_c, rows_c, [rec_c],
         (jax.ShapeDtypeStruct(wide, BF16),), TURN, "outputs_cols",
     )
+    y_c, *y_r = lax.optimization_barrier((y_c, *y_r))
     y_r = around(y_r, "col")
     y_c = lax.all_to_all(y_c.reshape(16, tokens // 2, LANES), "row", 0, 0)
 

time: 122 us -> 111 us (0.910)
  local copies, waits for them, and re-layouts: 10.4 us -> 2.83 us
  Pallas kernels: 38.4 us -> 35.4 us
    unnamed x53 -> x25, local copies, waits for them, and re-layouts: 8.59 us -> 0.24 us
    ppermute x21 -> x14, starting transfers between devices: 26.3 us -> 18.4 us  [around(): lax.ppermute(v, axis, [(i, (i + j) % count) for i in range(count)])]
    all_to_all x0 -> x1, starting transfers between devices: none -> 5.38 us  [per_device(): lax.all_to_all(jnp.broadcast_to(both[None], (8,) + both.shape), 'col', 0, 0)]
    all_to_all x1, waiting for transfers between devices: 1.61 us -> 0.01 us  [per_device(): rec_c = lax.all_to_all(rec_c, 'row', 0, 0).reshape(length, 2 * LANES)]
    ppermute x1, waiting for transfers between devices: 0.01 us -> 1.59 us  [per_device(): mate = lax.ppermute(tot_c, 'row', [(i, i ^ 1) for i in range(16)])]
    pallas_call x2, Pallas kernels: 14.8 us -> 13.3 us  [totals(): call(functools.partial(totals_kernel, len(recs), copies, first, turn), (j...]
    pallas_call x2, Pallas kernels: 18.9 us -> 17.5 us  [outputs(): call(functools.partial(outputs_kernel, len(recs), len(out), turn), out, s...]
    all_to_all x1, starting transfers between devices: 5.52 us -> 6.79 us  [per_device(): tot_r = lax.all_to_all(tot_r, 'row', 0, 0)]
  transfers between devices with their start and end apart: 29 -> 23, of which waited for: 10 -> 9; matrix products, arithmetic and copies ran while one was open for 3% -> 3% of each run, Pallas kernels for 28% -> 20%
where the time goes in v3:
time: 111 us; the launch traced here: 110 us
  starting transfers between devices  59.9 us (54%)
  Pallas kernels  35.4 us (32%)
  waiting for transfers between devices  9.51 us (9%)
  local copies, waits for them, and re-layouts  2.83 us (3%)
  matrix products  1.74 us (2%)
    ppermute x14, starting transfers between devices, around(): lax.ppermute(v, axis, [(i, (i + j) % count) for i in range(count)])  18.4 us
    pallas_call x2, Pallas kernels, outputs(): call(functools.partial(outputs_kernel, len(recs), len(out), turn), out, s...  17.5 us
    pallas_call x2, Pallas kernels, totals(): call(functools.partial(totals_kernel, len(recs), copies, first, turn), (j...  13.3 us
    ppermute x4, starting transfers between devices, shifted(): return lax.ppermute(values, axis, pairs)  12.3 us
    all_to_all x1, starting transfers between devices, per_device(): rec_c = lax.all_to_all(rec_c, 'row', 0, 0).reshape(length, 2 * LANES)  9.25 us
    all_to_all x1, starting transfers between devices, per_device(): tot_r = lax.all_to_all(tot_r, 'row', 0, 0)  6.79 us
    all_to_all x1, starting transfers between devices, per_device(): y_c = lax.all_to_all(y_c.reshape(16, tokens // 2, LANES), 'row', 0, 0)  6.31 us
    all_to_all x1, starting transfers between devices, per_device(): lax.all_to_all(jnp.broadcast_to(both[None], (8,) + both.shape), 'col', 0, 0)  5.38 us
  transfers between devices with their start and end apart: 23, of which 9 were waited for; matrix products, arithmetic and copies ran while one was open for 3% of the time, Pallas kernels for 20%

profile of v3, /device:TPU:1, one launch (start us, length us, event | category | flops | bytes accessed | tf_op | source)
XLA Modules:
  0.0 109.9 jit_solution(17066610302668681298)
XLA Ops:
  0.7 4.0 %collective-permute-start = (bf16[16,384]{1,0:T(8,128)(2,1)S(1)}, bf16[16,384]{1,0:T(8,128)(2,1)S(1)}, u32[]{:S(2)}, u32[]{:S(2)}) collective-permute-start(bf16[16,384]{1,0:T(8,128)(2,1)S(1)} %get-tuple-element.80), channel_id=1, source_target_pairs={{0,8},{8,16},{16,24},{24,32},{32,40},{40,48},{48,56},{56,64},{64,7... | collective-permute-start | bytes 36872 | tf_op jit(solution)/shard_map/ppermute | solution.py:342
  6.1 1.7 %convolution_convert_fusion = bf16[128,1536]{1,0:T(8,128)(2,1)S(1)} fusion(bf16[128,384]{1,0:T(8,128)(2,1)} %bitcast.27, bf16[384,1536]{1,0:T(8,128)(2,1)} %w_ref.2), kind=kOutput, calls=%fused_computation | convolution fusion | flops 151191552 | bytes 1671168 | tf_op jit(solution)/shard_map/dot_general | solution.py:373
  9.2 5.1 %collective-permute-start.2 = (bf16[10,384]{1,0:T(8,128)(2,1)S(1)}, bf16[10,384]{1,0:T(8,128)(2,1)S(1)}, u32[]{:S(2)}, u32[]{:S(2)}) collective-permute-start(bf16[10,384]{1,0:T(8,128)(2,1)S(1)} %pad_maximum_fusion.1), channel_id=1, source_target_pairs={{0,1},{1,2},{2,3},{3,4},{4,5},{5,6},{6,7},{8,9},{9,10},{10,11},{11... | collective-permute-start | bytes 23048 | tf_op jit(solution)/shard_map/ppermute | solution.py:342
  14.4 1.9 %collective-permute-start.3 = (bf16[10,384]{1,0:T(8,128)(2,1)S(1)}, bf16[10,384]{1,0:T(8,128)(2,1)S(1)}, u32[]{:S(2)}, u32[]{:S(2)}) collective-permute-start(bf16[10,384]{1,0:T(8,128)(2,1)S(1)} %pad_maximum_fusion.2), channel_id=1, source_target_pairs={{1,0},{2,1},{3,2},{4,3},{5,4},{6,5},{7,6},{9,8},{10,9},{11,10},{12... | collective-permute-start | bytes 23048 | tf_op jit(solution)/shard_map/ppermute | solution.py:342
  16.6 2.8 %collective-permute-done.3.right_ref = bf16[10,384]{1,0:T(8,128)(2,1)S(1)} collective-permute-done((bf16[10,384]{1,0:T(8,128)(2,1)S(1)}, bf16[10,384]{1,0:T(8,128)(2,1)S(1)}, u32[]{:S(2)}, u32[]{:S(2)}) %collective-permute-start.3) | collective-permute-done | bytes 7712 | tf_op jit(solution)/shard_map/ppermute | solution.py:342
  19.4 2.7 %local.1 = (bf16[128,768]{1,0:T(8,128)(2,1)S(1)}, bf16[128,256]{1,0:T(8,128)(2,1)S(1)}, bf16[128,256]{1,0:T(8,128)(2,1)S(1)}, bf16[128,256]{1,0:T(8,128)(2,1)S(1...) custom-call(s32[3]{0:T(128)S(1)} %pad_add_fusion.place_ref, ...), custom_call_target="tpu_custom_call" | custom-call | flops 10000000 | bytes 4000000 | tf_op jit(solution)/shard_map/local/pallas_call | solution.py:382
  22.1 9.2 %all-to-all-start = ((bf16[16,64,256]{2,1,0:T(8,128)(2,1)}), bf16[16,64,256]{2,1,0:T(8,128)(2,1)S(1)}, u32[]{:S(2)}, u32[]{:S(2)}) async-start(bf16[16,64,256]{2,1,0:T(8,128)(2,1)} %get-tuple-element.40), calls=%async_computation | async-start | bytes 1048576 | tf_op jit(solution)/shard_map/all_to_all | solution.py:446
  32.9 1.6 %collective-permute-start.7 = (bf16[128,256]{1,0:T(8,128)(2,1)S(1)}, bf16[128,256]{1,0:T(8,128)(2,1)S(1)}, u32[]{:S(2)}, u32[]{:S(2)}) collective-permute-start(bf16[128,256]{1,0:T(8,128)(2,1)S(1)} %get-tuple-element.48), channel_id=1, source_target_pairs={{0,3},{1,4},{2,5},{3,6},{4,7},{5,0},{6,1},{7,2},{8,11},{9,12},{10,... | collective-permute-start | bytes 196616 | tf_op jit(solution)/shard_map/ppermute | solution.py:348
  34.5 1.7 %collective-permute-start.8 = (bf16[128,256]{1,0:T(8,128)(2,1)S(1)}, bf16[128,256]{1,0:T(8,128)(2,1)S(1)}, u32[]{:S(2)}, u32[]{:S(2)}) collective-permute-start(bf16[128,256]{1,0:T(8,128)(2,1)S(1)} %get-tuple-element.49), channel_id=1, source_target_pairs={{0,4},{1,5},{2,6},{3,7},{4,0},{5,1},{6,2},{7,3},{8,12},{9,13},{10,... | collective-permute-start | bytes 196616 | tf_op jit(solution)/shard_map/ppermute | solution.py:348
  37.7 2.5 %collective-permute-start.11 = (bf16[128,256]{1,0:T(8,128)(2,1)S(1)}, bf16[128,256]{1,0:T(8,128)(2,1)S(1)}, u32[]{:S(2)}, u32[]{:S(2)}) collective-permute-start(bf16[128,256]{1,0:T(8,128)(2,1)S(1)} %get-tuple-element.52), channel_id=1, source_target_pairs={{0,7},{1,0},{2,1},{3,2},{4,3},{5,4},{6,5},{7,6},{8,15},{9,8},{10,9... | collective-permute-start | bytes 196616 | tf_op jit(solution)/shard_map/ppermute | solution.py:348
  42.9 7.0 %totals_rows.1 = (f32[2,17,8,128]{3,2,1,0:T(8,128)S(1)}, f32[16,48,128]{2,1,0:T(8,128)}, f32[2,24,128]{2,1,0:T(8,128)S(1)}, bf16[2,128,128]{2,1,0:T(8,128)(2,1)S(1)}) custom-call(s32[3]{0:T(128)S(1)} %pad_add_fusion.place_ref, bf16[128,256]{1,0:T(8,128)(2,1)S(1)} %get-tuple-element.45.refs_0_, bf16[128,256]{1,0:T(8,128)(2,1)S(1)} %collective-permute-done.5.refs_1_, ...), custom_call_target="tpu_custom_call" | custom-call | flops 1000000000 | bytes 4000000 | tf_op jit(solution)/shard_map/totals_rows/pallas_call | solution.py:409
  49.9 6.8 %all-to-all-start.2 = ((f32[16,48,128]{2,1,0:T(8,128)}), f32[16,48,128]{2,1,0:T(8,128)S(1)}, u32[]{:S(2)}, u32[]{:S(2)}) async-start(f32[16,48,128]{2,1,0:T(8,128)} %get-tuple-element.53), calls=%async_computation.2 | async-start | bytes 786432 | tf_op jit(solution)/shard_map/all_to_all | solution.py:451
  56.7 6.3 %totals_cols.1 = (f32[2,17,8,128]{3,2,1,0:T(8,128)S(1)}, f32[1,48,128]{2,1,0:T(8,128)S(1)}, f32[2,24,128]{2,1,0:T(8,128)S(1)}, bf16[2,128,128]{2,1,0:T(8,128)(2,1)S(1)}) custom-call(s32[3]{0:T(128)S(1)} %pad_add_fusion.1.place_ref, bf16[1024,256]{1,0:T(8,128)(2,1)S(1)} %bitcast.22, bf16[4,24,768]{2,1,0:T(8,128)(2,1)S(1)} %copy-done.3, ...), custom_call_target="tpu_custom_call" | custom-call | flops 1000000000 | bytes 4000000 | tf_op jit(solution)/shard_map/totals_cols/pallas_call | solution.py:409
  64.4 1.6 %collective-permute-done.4 = f32[1,48,128]{2,1,0:T(8,128)S(1)} collective-permute-done((f32[1,48,128]{2,1,0:T(8,128)S(1)}, f32[1,48,128]{2,1,0:T(8,128)S(1)}, u32[]{:S(2)}, u32[]{:S(2)}) %collective-permute-start.4) | collective-permute-done | bytes 24608 | tf_op jit(solution)/shard_map/ppermute | solution.py:452
  67.1 5.4 %all-to-all-start.1 = ((f32[8,2,48,128]{3,2,1,0:T(8,128)}), f32[8,2,48,128]{3,2,1,0:T(8,128)S(1)}, u32[]{:S(2)}, u32[]{:S(2)}) async-start(f32[8,2,48,128]{3,2,1,0:T(8,128)} %broadcast_in_dim.2), calls=%async_computation.1 | async-start | bytes 786432 | tf_op jit(solution)/shard_map/all_to_all | solution.py:454
  72.5 8.4 %outputs_rows.1 = (bf16[128,128]{1,0:T(8,128)(2,1)S(1)}, bf16[128,128]{1,0:T(8,128)(2,1)S(1)}, bf16[128,128]{1,0:T(8,128)(2,1)S(1)}, bf16[128,128]{1,0:T(8,128)(...) custom-call(s32[3]{0:T(128)S(1)} %pad_add_fusion.place_ref, ...), custom_call_target="tpu_custom_call" | custom-call | flops 1000000000 | bytes 4000000 | tf_op jit(solution)/shard_map/outputs_rows/pallas_call | solution.py:430
  80.9 9.1 %outputs_cols.1 = bf16[1024,128]{1,0:T(8,128)(2,1)} custom-call(s32[3]{0:T(128)S(1)} %pad_add_fusion.1.place_ref, f32[16,48,128]{2,1,0:T(8,128)S(1)} %bitcast.24, f32[2,17,8,128]{3,2,1,0:T(8,128)S(1)} %get-tuple-element.42.excl_ref, f32[2,24,128]{2,1,0:T(8,128)S(1)} %get-tuple-element.43.decay_ref, bf16[2,128,128]{2,1,0:T(8,128)(2,1)S(1)} %get-tuple-element.44.rows_ref, ...), custom_call_target="tpu_custom_call" | custom-call | flops 1000000000 | bytes 4000000 | tf_op jit(solution)/shard_map/outputs_cols/pallas_call | solution.py:430
  90.0 6.3 %all-to-all-start.3 = ((bf16[16,64,128]{2,1,0:T(8,128)(2,1)}), bf16[16,64,128]{2,1,0:T(8,128)(2,1)S(1)}, u32[]{:S(2)}, u32[]{:S(2)}) async-start(bf16[16,64,128]{2,1,0:T(8,128)(2,1)} %bitcast.12), calls=%async_computation.3 | async-start | bytes 524288 | tf_op jit(solution)/shard_map/all_to_all | solution.py:467
  96.3 1.9 %collective-permute-start.12 = (bf16[128,128]{1,0:T(8,128)(2,1)S(1)}, bf16[128,128]{1,0:T(8,128)(2,1)S(1)}, u32[]{:S(2)}, u32[]{:S(2)}) collective-permute-start(bf16[128,128]{1,0:T(8,128)(2,1)S(1)} %get-tuple-element.68), channel_id=1, source_target_pairs={{0,1},{1,2},{2,3},{3,4},{4,5},{5,6},{6,7},{7,0},{8,9},{9,10},{10,1... | collective-permute-start | bytes 98312 | tf_op jit(solution)/shard_map/ppermute | solution.py:348
  99.5 1.6 %collective-permute-start.14 = (bf16[128,128]{1,0:T(8,128)(2,1)S(1)}, bf16[128,128]{1,0:T(8,128)(2,1)S(1)}, u32[]{:S(2)}, u32[]{:S(2)}) collective-permute-start(bf16[128,128]{1,0:T(8,128)(2,1)S(1)} %get-tuple-element.70), channel_id=1, source_target_pairs={{0,3},{1,4},{2,5},{3,6},{4,7},{5,0},{6,1},{7,2},{8,11},{9,12},{10,... | collective-permute-start | bytes 98312 | tf_op jit(solution)/shard_map/ppermute | solution.py:348
  101.6 1.9 %collective-permute-start.16 = (bf16[128,128]{1,0:T(8,128)(2,1)S(1)}, bf16[128,128]{1,0:T(8,128)(2,1)S(1)}, u32[]{:S(2)}, u32[]{:S(2)}) collective-permute-start(bf16[128,128]{1,0:T(8,128)(2,1)S(1)} %get-tuple-element.72), channel_id=1, source_target_pairs={{0,5},{1,6},{2,7},{3,0},{4,1},{5,2},{6,3},{7,4},{8,13},{9,14},{10,... | collective-permute-start | bytes 98312 | tf_op jit(solution)/shard_map/ppermute | solution.py:348
  104.2 1.7 %collective-permute-start.18 = (bf16[128,128]{1,0:T(8,128)(2,1)S(1)}, bf16[128,128]{1,0:T(8,128)(2,1)S(1)}, u32[]{:S(2)}, u32[]{:S(2)}) collective-permute-start(bf16[128,128]{1,0:T(8,128)(2,1)S(1)} %get-tuple-element.74), channel_id=1, source_target_pairs={{0,7},{1,0},{2,1},{3,2},{4,3},{5,4},{6,5},{7,6},{8,15},{9,8},{10,9... | collective-permute-start | bytes 98312 | tf_op jit(solution)/shard_map/ppermute | solution.py:348
  106.5 1.5 %collective-permute-done.18.refs_7_ = bf16[128,128]{1,0:T(8,128)(2,1)S(1)} collective-permute-done((bf16[128,128]{1,0:T(8,128)(2,1)S(1)}, bf16[128,128]{1,0:T(8,128)(2,1)S(1)}, u32[]{:S(2)}, u32[]{:S(2)}) %collective-permute-start.18) | collective-permute-done | bytes 32800 | tf_op jit(solution)/shard_map/ppermute | solution.py:348
  108.0 2.0 %final.1 = bf16[128,384]{1,0:T(8,128)(2,1)} custom-call(s32[3]{0:T(128)S(1)} %pad_add_fusion.place_ref, bf16[16,64,128]{2,1,0:T(8,128)(2,1)S(1)} %all-to-all-done.3.yc_ref, bf16[128,768]{1,0:T(8,128)(2,1)S(1)} %get-tuple-element.66.act_ref, bf16[128,768]{1,0:T(8,128)(2,1)S(1)} %get-tuple-element.75.gate_ref, f32[1,768]{1,0:T(1,128)S(1)} %reshape.56.skip_ref, ...), custom_call_target="tpu_custom_call" | custom-call | flops 10000000 | bytes 4000000 | tf_op jit(solution)/shard_map/final/pallas_call | solution.py:469
  (73 shorter events, 14.8 us)
Async XLA Ops:
  0.7 8.5 %collective-permute-start = (bf16[16,384]{1,0:T(8,128)(2,1)S(1)}, bf16[16,384]{1,0:T(8,128)(2,1)S(1)}, u32[]{:S(2)}, u32[]{:S(2)}) collective-permute-start(bf16[16,384]{1,0:T(8,128)(2,1)S(1)} %get-tuple-element.80), channel_id=1, source_target_pairs={{0,8},{8,16},{16,24},{24,32},{32,40},{40,48},{48,56},{56,64},{64,7... | collective-permute-start | bytes 36872 | tf_op jit(solution)/shard_map/ppermute | solution.py:342
  4.8 4.4 %collective-permute-start.1 = (bf16[16,384]{1,0:T(8,128)(2,1)S(1)}, bf16[16,384]{1,0:T(8,128)(2,1)S(1)}, u32[]{:S(2)}, u32[]{:S(2)}) collective-permute-start(bf16[16,384]{1,0:T(8,128)(2,1)S(1)} %get-tuple-element.79), channel_id=1, source_target_pairs={{8,0},{16,8},{24,16},{32,24},{40,32},{48,40},{56,48},{64,56},{72,6... | collective-permute-start | bytes 36872 | tf_op jit(solution)/shard_map/ppermute | solution.py:342
  9.2 7.4 %collective-permute-start.2 = (bf16[10,384]{1,0:T(8,128)(2,1)S(1)}, bf16[10,384]{1,0:T(8,128)(2,1)S(1)}, u32[]{:S(2)}, u32[]{:S(2)}) collective-permute-start(bf16[10,384]{1,0:T(8,128)(2,1)S(1)} %pad_maximum_fusion.1), channel_id=1, source_target_pairs={{0,1},{1,2},{2,3},{3,4},{4,5},{5,6},{6,7},{8,9},{9,10},{10,11},{11... | collective-permute-start | bytes 23048 | tf_op jit(solution)/shard_map/ppermute | solution.py:342
  14.4 5.0 %collective-permute-start.3 = (bf16[10,384]{1,0:T(8,128)(2,1)S(1)}, bf16[10,384]{1,0:T(8,128)(2,1)S(1)}, u32[]{:S(2)}, u32[]{:S(2)}) collective-permute-start(bf16[10,384]{1,0:T(8,128)(2,1)S(1)} %pad_maximum_fusion.2), channel_id=1, source_target_pairs={{1,0},{2,1},{3,2},{4,3},{5,4},{6,5},{7,6},{9,8},{10,9},{11,10},{12... | collective-permute-start | bytes 23048 | tf_op jit(solution)/shard_map/ppermute | solution.py:342
  22.1 27.8 %all-to-all-start = ((bf16[16,64,256]{2,1,0:T(8,128)(2,1)}), bf16[16,64,256]{2,1,0:T(8,128)(2,1)S(1)}, u32[]{:S(2)}, u32[]{:S(2)}) async-start(bf16[16,64,256]{2,1,0:T(8,128)(2,1)} %get-tuple-element.40), calls=%async_computation | async-start | bytes 1048576 | tf_op jit(solution)/shard_map/all_to_all | solution.py:446
  31.4 5.5 %collective-permute-start.5 = (bf16[128,256]{1,0:T(8,128)(2,1)S(1)}, bf16[128,256]{1,0:T(8,128)(2,1)S(1)}, u32[]{:S(2)}, u32[]{:S(2)}) collective-permute-start(bf16[128,256]{1,0:T(8,128)(2,1)S(1)} %get-tuple-element.46), channel_id=1, source_target_pairs={{0,1},{1,2},{2,3},{3,4},{4,5},{5,6},{6,7},{7,0},{8,9},{9,10},{10,1... | collective-permute-start | bytes 196616 | tf_op jit(solution)/shard_map/ppermute | solution.py:348
  31.7 6.0 %collective-permute-start.6 = (bf16[128,256]{1,0:T(8,128)(2,1)S(1)}, bf16[128,256]{1,0:T(8,128)(2,1)S(1)}, u32[]{:S(2)}, u32[]{:S(2)}) collective-permute-start(bf16[128,256]{1,0:T(8,128)(2,1)S(1)} %get-tuple-element.47), channel_id=1, source_target_pairs={{0,2},{1,3},{2,4},{3,5},{4,6},{5,7},{6,0},{7,1},{8,10},{9,11},{10,... | collective-permute-start | bytes 196616 | tf_op jit(solution)/shard_map/ppermute | solution.py:348
  32.9 7.4 %collective-permute-start.7 = (bf16[128,256]{1,0:T(8,128)(2,1)S(1)}, bf16[128,256]{1,0:T(8,128)(2,1)S(1)}, u32[]{:S(2)}, u32[]{:S(2)}) collective-permute-start(bf16[128,256]{1,0:T(8,128)(2,1)S(1)} %get-tuple-element.48), channel_id=1, source_target_pairs={{0,3},{1,4},{2,5},{3,6},{4,7},{5,0},{6,1},{7,2},{8,11},{9,12},{10,... | collective-permute-start | bytes 196616 | tf_op jit(solution)/shard_map/ppermute | solution.py:348
  34.5 5.8 %collective-permute-start.8 = (bf16[128,256]{1,0:T(8,128)(2,1)S(1)}, bf16[128,256]{1,0:T(8,128)(2,1)S(1)}, u32[]{:S(2)}, u32[]{:S(2)}) collective-permute-start(bf16[128,256]{1,0:T(8,128)(2,1)S(1)} %get-tuple-element.49), channel_id=1, source_target_pairs={{0,4},{1,5},{2,6},{3,7},{4,0},{5,1},{6,2},{7,3},{8,12},{9,13},{10,... | collective-permute-start | bytes 196616 | tf_op jit(solution)/shard_map/ppermute | solution.py:348
  36.2 5.2 %collective-permute-start.9 = (bf16[128,256]{1,0:T(8,128)(2,1)S(1)}, bf16[128,256]{1,0:T(8,128)(2,1)S(1)}, u32[]{:S(2)}, u32[]{:S(2)}) collective-permute-start(bf16[128,256]{1,0:T(8,128)(2,1)S(1)} %get-tuple-element.50), channel_id=1, source_target_pairs={{0,5},{1,6},{2,7},{3,0},{4,1},{5,2},{6,3},{7,4},{8,13},{9,14},{10,... | collective-permute-start | bytes 196616 | tf_op jit(solution)/shard_map/ppermute | solution.py:348
  36.9 5.1 %collective-permute-start.10 = (bf16[128,256]{1,0:T(8,128)(2,1)S(1)}, bf16[128,256]{1,0:T(8,128)(2,1)S(1)}, u32[]{:S(2)}, u32[]{:S(2)}) collective-permute-start(bf16[128,256]{1,0:T(8,128)(2,1)S(1)} %get-tuple-element.51), channel_id=1, source_target_pairs={{0,6},{1,7},{2,0},{3,1},{4,2},{5,3},{6,4},{7,5},{8,14},{9,15},{10,... | collective-permute-start | bytes 196616 | tf_op jit(solution)/shard_map/ppermute | solution.py:348
  37.7 5.2 %collective-permute-start.11 = (bf16[128,256]{1,0:T(8,128)(2,1)S(1)}, bf16[128,256]{1,0:T(8,128)(2,1)S(1)}, u32[]{:S(2)}, u32[]{:S(2)}) collective-permute-start(bf16[128,256]{1,0:T(8,128)(2,1)S(1)} %get-tuple-element.52), channel_id=1, source_target_pairs={{0,7},{1,0},{2,1},{3,2},{4,3},{5,4},{6,5},{7,6},{8,15},{9,8},{10,9... | collective-permute-start | bytes 196616 | tf_op jit(solution)/shard_map/ppermute | solution.py:348
  49.9 16.4 %all-to-all-start.2 = ((f32[16,48,128]{2,1,0:T(8,128)}), f32[16,48,128]{2,1,0:T(8,128)S(1)}, u32[]{:S(2)}, u32[]{:S(2)}) async-start(f32[16,48,128]{2,1,0:T(8,128)} %get-tuple-element.53), calls=%async_computation.2 | async-start | bytes 786432 | tf_op jit(solution)/shard_map/all_to_all | solution.py:451
  62.9 3.1 %collective-permute-start.4 = (f32[1,48,128]{2,1,0:T(8,128)S(1)}, f32[1,48,128]{2,1,0:T(8,128)S(1)}, u32[]{:S(2)}, u32[]{:S(2)}) collective-permute-start(f32[1,48,128]{2,1,0:T(8,128)S(1)} %get-tuple-element.41), channel_id=1, source_target_pairs={{0,8},{8,0},{16,24},{24,16},{32,40},{40,32},{48,56},{56,48},{64,72... | collective-permute-start | bytes 73736 | tf_op jit(solution)/shard_map/ppermute | solution.py:452
  67.1 13.8 %all-to-all-start.1 = ((f32[8,2,48,128]{3,2,1,0:T(8,128)}), f32[8,2,48,128]{3,2,1,0:T(8,128)S(1)}, u32[]{:S(2)}, u32[]{:S(2)}) async-start(f32[8,2,48,128]{3,2,1,0:T(8,128)} %broadcast_in_dim.2), calls=%async_computation.1 | async-start | bytes 786432 | tf_op jit(solution)/shard_map/all_to_all | solution.py:454
  80.9 27.1 %copy-start.1 = (bf16[768,384]{1,0:T(8,128)(2,1)S(1)}, bf16[768,384]{1,0:T(8,128)(2,1)}, u32[]{:S(2)}) copy-start(bf16[768,384]{1,0:T(8,128)(2,1)} %w_ref.3) | copy-start | bytes 1769476
  90.0 18.0 %all-to-all-start.3 = ((bf16[16,64,128]{2,1,0:T(8,128)(2,1)}), bf16[16,64,128]{2,1,0:T(8,128)(2,1)S(1)}, u32[]{:S(2)}, u32[]{:S(2)}) async-start(bf16[16,64,128]{2,1,0:T(8,128)(2,1)} %bitcast.12), calls=%async_computation.3 | async-start | bytes 524288 | tf_op jit(solution)/shard_map/all_to_all | solution.py:467
  96.3 7.2 %collective-permute-start.12 = (bf16[128,128]{1,0:T(8,128)(2,1)S(1)}, bf16[128,128]{1,0:T(8,128)(2,1)S(1)}, u32[]{:S(2)}, u32[]{:S(2)}) collective-permute-start(bf16[128,128]{1,0:T(8,128)(2,1)S(1)} %get-tuple-element.68), channel_id=1, source_target_pairs={{0,1},{1,2},{2,3},{3,4},{4,5},{5,6},{6,7},{7,0},{8,9},{9,10},{10,1... | collective-permute-start | bytes 98312 | tf_op jit(solution)/shard_map/ppermute | solution.py:348
  98.3 5.9 %collective-permute-start.13 = (bf16[128,128]{1,0:T(8,128)(2,1)S(1)}, bf16[128,128]{1,0:T(8,128)(2,1)S(1)}, u32[]{:S(2)}, u32[]{:S(2)}) collective-permute-start(bf16[128,128]{1,0:T(8,128)(2,1)S(1)} %get-tuple-element.69), channel_id=1, source_target_pairs={{0,2},{1,3},{2,4},{3,5},{4,6},{5,7},{6,0},{7,1},{8,10},{9,11},{10,... | collective-permute-start | bytes 98312 | tf_op jit(solution)/shard_map/ppermute | solution.py:348
  99.5 6.4 %collective-permute-start.14 = (bf16[128,128]{1,0:T(8,128)(2,1)S(1)}, bf16[128,128]{1,0:T(8,128)(2,1)S(1)}, u32[]{:S(2)}, u32[]{:S(2)}) collective-permute-start(bf16[128,128]{1,0:T(8,128)(2,1)S(1)} %get-tuple-element.70), channel_id=1, source_target_pairs={{0,3},{1,4},{2,5},{3,6},{4,7},{5,0},{6,1},{7,2},{8,11},{9,12},{10,... | collective-permute-start | bytes 98312 | tf_op jit(solution)/shard_map/ppermute | solution.py:348
  101.0 4.9 %collective-permute-start.15 = (bf16[128,128]{1,0:T(8,128)(2,1)S(1)}, bf16[128,128]{1,0:T(8,128)(2,1)S(1)}, u32[]{:S(2)}, u32[]{:S(2)}) collective-permute-start(bf16[128,128]{1,0:T(8,128)(2,1)S(1)} %get-tuple-element.71), channel_id=1, source_target_pairs={{0,4},{1,5},{2,6},{3,7},{4,0},{5,1},{6,2},{7,3},{8,12},{9,13},{10,... | collective-permute-start | bytes 98312 | tf_op jit(solution)/shard_map/ppermute | solution.py:348
  101.6 4.8 %collective-permute-start.16 = (bf16[128,128]{1,0:T(8,128)(2,1)S(1)}, bf16[128,128]{1,0:T(8,128)(2,1)S(1)}, u32[]{:S(2)}, u32[]{:S(2)}) collective-permute-start(bf16[128,128]{1,0:T(8,128)(2,1)S(1)} %get-tuple-element.72), channel_id=1, source_target_pairs={{0,5},{1,6},{2,7},{3,0},{4,1},{5,2},{6,3},{7,4},{8,13},{9,14},{10,... | collective-permute-start | bytes 98312 | tf_op jit(solution)/shard_map/ppermute | solution.py:348
  103.5 2.9 %collective-permute-start.17 = (bf16[128,128]{1,0:T(8,128)(2,1)S(1)}, bf16[128,128]{1,0:T(8,128)(2,1)S(1)}, u32[]{:S(2)}, u32[]{:S(2)}) collective-permute-start(bf16[128,128]{1,0:T(8,128)(2,1)S(1)} %get-tuple-element.73), channel_id=1, source_target_pairs={{0,6},{1,7},{2,0},{3,1},{4,2},{5,3},{6,4},{7,5},{8,14},{9,15},{10,... | collective-permute-start | bytes 98312 | tf_op jit(solution)/shard_map/ppermute | solution.py:348
  104.2 3.8 %collective-permute-start.18 = (bf16[128,128]{1,0:T(8,128)(2,1)S(1)}, bf16[128,128]{1,0:T(8,128)(2,1)S(1)}, u32[]{:S(2)}, u32[]{:S(2)}) collective-permute-start(bf16[128,128]{1,0:T(8,128)(2,1)S(1)} %get-tuple-element.74), channel_id=1, source_target_pairs={{0,7},{1,0},{2,1},{3,2},{4,3},{5,4},{6,5},{7,6},{8,15},{9,8},{10,9... | collective-permute-start | bytes 98312 | tf_op jit(solution)/shard_map/ppermute | solution.py:348
  (10 other events, 164.8 us)

commit v4 on v3

v4 whole, which is shorter than its diff:
```python
import functools
import math

import jax
import jax.numpy as jnp
from jax import lax
from jax.experimental import pallas as pl
from jax.experimental.pallas import tpu as pltpu
from jax.sharding import PartitionSpec as P

F32 = jnp.float32
BF16 = jnp.bfloat16
LANES = 128
SLICE = 96
STATE = 16
RANK = 24
EACH = RANK + 2 * STATE
OFF_LANE = 2 * EACH
TOT = 24
BLOCK = 64
LOG2E = math.log2(math.e)
HALF = 64


def vmem(count):
    return [pl.BlockSpec(memory_space=pltpu.VMEM)] * count


def call(kernel, out_shape, in_specs, scratch=(), flops=10**7, grant=16, name=None):
    return pl.pallas_call(
        kernel,
        out_shape=out_shape,
        in_specs=in_specs,
        out_specs=jax.tree.map(lambda _: pl.BlockSpec(memory_space=pltpu.VMEM), out_shape),
        scratch_shapes=list(scratch),
        compiler_params=pltpu.CompilerParams(vmem_limit_bytes=grant << 20),
        cost_estimate=pl.CostEstimate(flops=flops, bytes_accessed=4 * 10**6, transcendentals=0),
        name=name,
    )


def lane_iota(shape):
    return lax.broadcasted_iota(jnp.int32, shape, len(shape) - 1)


def softplus(x):
    u = jnp.exp2(jnp.abs(x) * -LOG2E)
    series = u * (1.0 - u * (0.5 - u * (1.0 / 3.0 - u * 0.25)))
    return jnp.maximum(x, 0.0) + jnp.where(u < 0.03, series, jnp.log(1.0 + u))


def silu(x):
    return x * jax.nn.sigmoid(x)


def cut_slice(values, k):
    j0, off = divmod(SLICE * k, LANES)
    first = values[:, j0 * LANES : (j0 + 1) * LANES]
    if off == 0:
        return first
    shift = LANES - off
    head = pltpu.roll(first, shift, 1)
    if shift >= SLICE:
        return head
    second = values[:, (j0 + 1) * LANES : (j0 + 2) * LANES]
    tail = pltpu.roll(second, shift, 1)
    return jnp.where(lane_iota(head.shape) < shift, head, tail)


def join_slices(parts):
    tiles = []
    lane = lane_iota(parts[0].shape)
    for m in range(2):
        y0, y1, y2, y3 = parts[4 * m : 4 * m + 4]
        r1 = pltpu.roll(y1, 96, 1)
        r2 = pltpu.roll(y2, 64, 1)
        r3 = pltpu.roll(y3, 32, 1)
        tiles.append(jnp.where(lane < 96, y0, r1))
        tiles.append(jnp.where(lane < 64, r1, r2))
        tiles.append(jnp.where(lane < 32, r2, r3))
    return tiles


def cut_narrow(values, k, start):
    j0, off = divmod(SLICE // 2 * k, LANES)
    shift = (start - off) % LANES
    first = values[:, j0 * LANES : (j0 + 1) * LANES]
    head = first if shift == 0 else pltpu.roll(first, shift, 1)
    if off + SLICE // 2 <= LANES:
        return head
    second = values[:, (j0 + 1) * LANES : (j0 + 2) * LANES]
    tail = pltpu.roll(second, shift, 1)
    return jnp.where(lane_iota(head.shape) < start + LANES - off, head, tail)


def join_narrow(parts, start):
    lane = lane_iota(parts[0].shape)

    def pick(chosen, bounds):
        out = chosen[-1]
        for value, bound in zip(chosen[-2::-1], bounds[::-1]):
            out = jnp.where(lane < bound, value, out)
        return out

    tiles = []
    for m in range(2):
        r = []
        for k in range(8):
            shift = (48 * k - start) % LANES
            y = parts[8 * m + k]
            r.append(y if shift == 0 else pltpu.roll(y, shift, 1))
        tiles.append(pick(r[0:3], (48, 96)))
        tiles.append(pick(r[2:6], (16, 64, 112)))
        tiles.append(pick(r[5:8], (32, 80)))
    return tiles


def order_matrix(to_columns):
    q = lax.broadcasted_iota(jnp.int32, (LANES, LANES), 0 if to_columns else 1)
    p = lax.broadcasted_iota(jnp.int32, (LANES, LANES), 1 if to_columns else 0)
    return (p == (q % 8) * 16 + q // 8).astype(F32).astype(BF16)


def column(col, chips, flip):
    return ((col + 2 * chips) & 7) ^ flip


def merge_kernel(near_ref, far_ref, *out_refs):
    for j, out_ref in enumerate(out_refs):
        out_ref[0] = near_ref[j]
        out_ref[1] = far_ref[j]


def local_kernel(
    place_ref, x_ref, top_ref, bottom_ref, left_ref, right_ref, w_ref, cw_ref, cb_ref, xw_ref, off_ref,
    *rest,
):
    act_ref, near_ref, far_ref, recc_ref, frame_ref, xwide_ref, slices_ref = rest
    inner = x_ref.shape[1]
    weight = w_ref[:, :inner]

    def project(v):
        return jnp.dot(v, weight, preferred_element_type=F32).astype(BF16).astype(F32)

    frame_ref[1:9, 8:24, :] = x_ref[...].astype(F32).reshape(8, 16, inner)
    frame_ref[0:1, 8:24, :] = project(top_ref[...]).reshape(1, 16, inner)
    frame_ref[9:10, 8:24, :] = project(bottom_ref[...]).reshape(1, 16, inner)
    left = project(left_ref[...])
    right = project(right_ref[...])
    for i in range(10):
        frame_ref[i, 7:8, :] = left[i : i + 1]
        frame_ref[i, 24:25, :] = right[i : i + 1]
    total = jnp.zeros((8, 16, inner), F32) + cb_ref[...].reshape(1, 1, inner)
    for dc in range(3):
        for dr in range(3):
            k = dr * 3 + dc
            total = total + frame_ref[dr : dr + 8, 7 + dc : 23 + dc, :] * cw_ref[
                k : k + 1, :
            ].reshape(1, 1, inner)
    act = silu(total).reshape(LANES, inner).astype(BF16)
    act_ref[...] = act
    xwide_ref[:, LANES:] = jnp.zeros((inner, LANES), BF16)
    xwide_ref[:, : xw_ref.shape[1]] = xw_ref[...]
    coef = jnp.dot(act, xwide_ref[...], preferred_element_type=F32)
    lane = lane_iota((LANES, LANES))
    off = jnp.broadcast_to(off_ref[...], (LANES, LANES))
    coef_r = jnp.where(lane == OFF_LANE, off, jnp.where(lane < OFF_LANE, coef[:, :LANES], 0.0)).astype(BF16)
    coef_c = pltpu.roll(jnp.where(lane >= OFF_LANE, coef[:, :LANES], coef[:, LANES:]), 16, 1)
    coef_c = jnp.where(lane == OFF_LANE, off, jnp.where(lane < OFF_LANE, coef_c, 0.0))
    turn = order_matrix(True)
    act_r = jnp.dot(turn, act, preferred_element_type=F32)
    coef_r = jnp.dot(turn, coef_r, preferred_element_type=F32).astype(BF16)
    wide = act.astype(F32).reshape(8, 16, inner)
    half = coef_c.reshape(8, 16, LANES)
    sides = [wide[:, 8 * h : 8 * h + 8, :].reshape(HALF, inner) for h in range(2)]
    coefs = [half[:, 8 * h : 8 * h + 8, :].reshape(HALF, LANES).astype(BF16) for h in range(2)]
    for k in range(8):
        slices_ref[k] = cut_slice(act_r, k).astype(BF16)
    for k in range(16):
        pair = [cut_narrow(sides[h], k, HALF * h) for h in range(2)]
        recc_ref[k, :, :LANES] = jnp.where(
            lane_iota(pair[0].shape) < HALF, pair[0], pair[1]
        ).astype(BF16)
        for h in range(2):
            recc_ref[k, :, (1 + h) * LANES : (2 + h) * LANES] = coefs[h]
    for ref, flip in ((near_ref, 0), (far_ref, 1)):
        for j in range(4):
            ref[j, :, :LANES] = slices_ref[column(place_ref[0], j, flip)]
            ref[j, :, LANES:] = coef_r


def spread_matrix(spread_ref):
    halves = spread_ref.shape[0] // LANES
    low, high = 16, 64
    spread_ref[...] = jnp.zeros_like(spread_ref)
    shape = (high - low, spread_ref.shape[1])
    source = lax.broadcasted_iota(jnp.int32, shape, 0) + low
    place = lax.broadcasted_iota(jnp.int32, shape, 1)
    hit = source == RANK + place // LANES
    for h in range(halves):
        side = hit if halves == 1 else jnp.logical_and(hit, ((place // HALF) & 1) == h)
        spread_ref[h * LANES + low : h * LANES + high, :] = side.astype(F32).astype(BF16)


def prepare(recs, place, rows_ref, bias, dt_ref, du_ref, coef_ref):
    length = dt_ref.shape[1]
    halves = coef_ref.shape[2] // LANES
    size = length // 8
    for j in range(8):
        if len(recs) == 1:
            rec = recs[0].at[j * size : (j + 1) * size]
            at = pl.ds(j * size, size)
        else:
            rec = recs[j // 2].at[j % 2]
            at = pl.ds(pl.multiple_of(column(place, -(j // 2), j % 2) * size, size), size)
        act = rec[:, :LANES].astype(F32)
        for o in range(2):
            z = bias[o]
            for h in range(halves):
                coef = rec[:, (1 + h) * LANES : (2 + h) * LANES]
                if o == 1:
                    coef = pltpu.roll(coef.astype(F32), LANES - EACH, 1).astype(BF16)
                coef_ref[o, at, h * LANES : (h + 1) * LANES] = coef
                z = z + jnp.dot(
                    coef, rows_ref[o, h * LANES : (h + 1) * LANES, :], preferred_element_type=F32
                )
            dt = softplus(z)
            dt_ref[o, at, :] = dt
            du_ref[o, at, :] = dt * act


def block_at(i, o, length):
    size = BLOCK * 8
    i = length // size - 1 - i if o == 1 else i
    return pl.multiple_of(i * size, size)


def totals_kernel(pieces, copies, first, place_ref, *refs):
    recs, (dtw_ref, bias_ref, rates_ref) = refs[:pieces], refs[pieces : pieces + 3]
    excl_ref, tot_ref, decay_ref, rows_ref = refs[pieces + 3 : pieces + 7]
    dt_ref, du_ref, coef_ref, wide_ref, spread_ref, bx_ref = refs[pieces + 7 :]
    length = dt_ref.shape[1]
    halves = coef_ref.shape[2] // LANES
    inner = dtw_ref.shape[2]
    slice_width = SLICE // halves
    shift = jnp.where(place_ref[1] == 0, 0, inner - slice_width * place_ref[1])
    lane = lane_iota((1, LANES))
    used = lane < SLICE if halves == 1 else (lane & (HALF - 1)) < slice_width

    def cut(values):
        return pltpu.roll(values, shift, 1)[:, :LANES]

    def paired(values):
        return values if halves == 1 else jnp.where(lane < HALF, values, pltpu.roll(values, HALF, 1))

    wide_ref[...] = jnp.zeros_like(wide_ref)
    for o in range(2):
        dtw = cut(dtw_ref[first + o].astype(F32))
        mark = OFF_LANE - o * EACH
        for h in range(halves):
            base = h * LANES
            mine = lane < HALF if h == 0 else lane >= HALF
            if halves == 1:
                wide_ref[o, :RANK, :] = dtw
                off = jnp.full((1, LANES), -1e30, F32)
            else:
                moved = dtw if h == 0 else pltpu.roll(dtw, HALF, 1)
                wide_ref[o, base : base + RANK, :] = jnp.where(mine, moved, 0.0)
                off = jnp.where(mine, -1e30, 0.0)
            wide_ref[o, base + mark : base + mark + 1, :] = off
        rows_ref[o] = wide_ref[o].astype(BF16)
        bias = cut(bias_ref[...])[first + o : first + o + 1]
        rates = cut(rates_ref[first + o])
        decay_ref[o, :STATE] = jnp.where(used, paired(rates) * -LOG2E, 0.0)
        decay_ref[o, STATE:] = jnp.broadcast_to(
            jnp.where(used, paired(bias), -1e30), (TOT - STATE, LANES)
        )
    bias = [decay_ref[o, STATE : STATE + 1, :] for o in range(2)]
    prepare(recs, place_ref[0], rows_ref, bias, dt_ref, du_ref, coef_ref)
    spread_matrix(spread_ref)
    sub = lax.broadcasted_iota(jnp.int32, (8, LANES), 0)
    spans = []
    for o in range(2):
        decay = [jnp.broadcast_to(decay_ref[o, n : n + 1, :], (8, LANES)) for n in range(STATE)]

        def advance(i, carry):
            span, states = carry
            states = list(states)
            base = block_at(i, o, length)
            bx_ref[...] = jnp.dot(
                coef_ref[o, pl.ds(base, BLOCK * 8), :], spread_ref[...], preferred_element_type=F32
            )
            for t in range(BLOCK) if o == 0 else range(BLOCK - 1, -1, -1):
                dt = dt_ref[o, pl.ds(base + t * 8, 8), :]
                du = du_ref[o, pl.ds(base + t * 8, 8), :]
                for n in range(STATE):
                    b = bx_ref[t * 8 : t * 8 + 8, n * LANES : (n + 1) * LANES]
                    states[n] = jnp.exp2(decay[n] * dt) * states[n] + du * b
                span = span + dt
            return span, tuple(states)

        zero = jnp.zeros((8, LANES), F32)
        span, states = lax.fori_loop(0, length // (8 * BLOCK), advance, (zero, (zero,) * STATE))
        states = list(states)
        for k in (1, 2, 4):
            shift_k = k if o == 0 else 8 - k
            keep = sub >= k if o == 0 else sub < 8 - k
            for n in range(STATE):
                moved = jnp.where(keep, pltpu.roll(states[n], shift_k, 0), 0.0)
                states[n] = jnp.exp2(decay[n] * span) * moved + states[n]
            span = span + jnp.where(keep, pltpu.roll(span, shift_k, 0), 0.0)
        shift_k = 1 if o == 0 else 7
        keep = sub >= 1 if o == 0 else sub < 7
        last = 7 if o == 0 else 0
        ends = jnp.concatenate([s[last : last + 1] for s in states], axis=0)
        end = span[last : last + 1]
        states = [jnp.where(keep, pltpu.roll(s, shift_k, 0), 0.0) for s in states]
        span = jnp.where(keep, pltpu.roll(span, shift_k, 0), 0.0)
        if halves == 2:
            second = lane >= HALF if o == 0 else lane < HALF
            before = pltpu.roll(ends, HALF, 1)
            for n in range(STATE):
                lifted = jnp.exp2(decay[n] * span) * before[n : n + 1] + states[n]
                states[n] = jnp.where(second, lifted, states[n])
            ends = jnp.exp2(decay_ref[o, :STATE] * end) * before + ends
            ends = jnp.where(second, ends, pltpu.roll(ends, HALF, 1))
            span = span + jnp.where(second, pltpu.roll(end, HALF, 1), 0.0)
            end = end + pltpu.roll(end, HALF, 1)
        for n in range(STATE):
            excl_ref[o, n] = states[n]
        excl_ref[o, STATE] = span
        high = end.astype(BF16).astype(F32)
        row = lax.broadcasted_iota(jnp.int32, (STATE, LANES), 0)
        spans.append(jnp.where(row == 2 * o, high, jnp.where(row == 2 * o + 1, end - high, 0.0)))
        for k in range(copies):
            tot_ref[k, o * STATE : (o + 1) * STATE, :] = ends.astype(BF16)
    for k in range(copies):
        tot_ref[k, 2 * STATE :, :] = (spans[0] + spans[1]).astype(BF16)


def outputs_kernel(pieces, parts_out, place_ref, gathered_ref, excl_ref, decay_ref, rows_ref, *refs):
    recs, outs = refs[:pieces], refs[pieces : pieces + parts_out]
    dt_ref, du_ref, coef_ref, spread_ref, bx_ref, sum_ref = refs[pieces + parts_out :]
    length = dt_ref.shape[1]
    chunks = gathered_ref.shape[0]
    bias = [decay_ref[o, STATE : STATE + 1, :] for o in range(2)]
    prepare(recs, place_ref[0], rows_ref, bias, dt_ref, du_ref, coef_ref)
    place = place_ref[2]
    spread_matrix(spread_ref)
    for o in range(2):
        rates = decay_ref[o, :STATE]
        entry = jnp.zeros((STATE, LANES), F32)
        for k in range(chunks) if o == 0 else range(chunks - 1, -1, -1):
            ahead = k < place if o == 0 else k > place
            tail = gathered_ref[k, 2 * STATE :, :].astype(F32)
            span = tail[2 * o : 2 * o + 1] + tail[2 * o + 1 : 2 * o + 2]
            ends = gathered_ref[k, o * STATE : (o + 1) * STATE, :].astype(F32)
            following = jnp.exp2(rates * span) * entry + ends
            entry = jnp.where(ahead, following, entry)
        decay = [jnp.broadcast_to(decay_ref[o, n : n + 1, :], (8, LANES)) for n in range(STATE)]
        states = tuple(
            jnp.exp2(decay[n] * excl_ref[o, STATE]) * entry[n : n + 1] + excl_ref[o, n]
            for n in range(STATE)
        )

        def advance(i, states):
            states = list(states)
            base = block_at(i, o, length)
            bx_ref[...] = jnp.dot(
                coef_ref[o, pl.ds(base, BLOCK * 8), :], spread_ref[...], preferred_element_type=F32
            )
            for t in range(BLOCK) if o == 0 else range(BLOCK - 1, -1, -1):
                at = pl.ds(base + t * 8, 8)
                dt = dt_ref[o, at, :]
                du = du_ref[o, at, :]
                parts = []
                for n in range(STATE):
                    b = bx_ref[t * 8 : t * 8 + 8, n * LANES : (n + 1) * LANES]
                    c = bx_ref[t * 8 : t * 8 + 8, (STATE + n) * LANES : (STATE + n + 1) * LANES]
                    states[n] = jnp.exp2(decay[n] * dt) * states[n] + du * b
                    parts.append(states[n] * c)
                while len(parts) > 1:
                    parts = [a + b for a, b in zip(parts[::2], parts[1::2])]
                if o == 0:
                    sum_ref[at, :] = parts[0]
                else:
                    sum_ref[at, :] = sum_ref[at, :] + parts[0]
            return tuple(states)

        lax.fori_loop(0, length // (8 * BLOCK), advance, states)
    if parts_out == 1:
        outs[0][...] = sum_ref[...].astype(BF16)
    else:
        step = length // 8
        for flip in range(2):
            for j in range(4):
                at = pl.multiple_of(column(place_ref[0], j, flip) * step, step)
                outs[flip][j] = sum_ref[pl.ds(at, step), :].astype(BF16)


def final_kernel(
    place_ref, yc_ref, act_ref, gate_ref, skip_ref, gain_ref, w_ref, live_ref, *refs
):
    yr_refs, out_ref, slices_ref = refs[:4], refs[4], refs[5]
    turn = order_matrix(False)
    for j in range(4):
        for flip in range(2):
            slices_ref[column(place_ref[0], -j, flip)] = yr_refs[j][flip]
    parts = [jnp.dot(turn, slices_ref[k], preferred_element_type=F32) for k in range(8)]
    narrow = [yc_ref[k].astype(F32) for k in range(16)]
    sides = [
        jnp.concatenate(join_narrow(narrow, HALF * h), axis=1).reshape(8, 8, -1) for h in range(2)
    ]
    combined = jnp.concatenate(join_slices(parts), axis=1)
    combined = combined + jnp.concatenate(sides, axis=1).reshape(combined.shape)
    combined = combined + skip_ref[...] * act_ref[...].astype(F32)
    mean = jnp.mean(combined, axis=1, keepdims=True)
    centered = combined - mean
    variance = jnp.mean(centered * centered, axis=1, keepdims=True)
    normed = centered * lax.rsqrt(variance + 1e-05) * gain_ref[...]
    mixed = (normed * silu(gate_ref[...].astype(F32))).astype(BF16)
    out_ref[...] = (
        jnp.dot(mixed, w_ref[...], preferred_element_type=F32) * live_ref[...]
    ).astype(BF16)


def shifted(values, axis, step):
    count = lax.axis_size(axis)
    pairs = [(i, i + step) for i in range(count) if 0 <= i + step < count]
    return lax.ppermute(values, axis, pairs)


def exchange(near, far):
    count = lax.axis_size("col")
    merged = call(
        merge_kernel,
        (jax.ShapeDtypeStruct((2,) + near.shape[1:], near.dtype),) * 4,
        vmem(2),
        flops=10**6,
        name="merge",
    )(near, far)
    return [
        m if j == 0 else lax.ppermute(m, "col", [(c, (c + 2 * j) % count) for c in range(count)])
        for j, m in enumerate(merged)
    ]


def crossed(far):
    return lax.ppermute(far, "col", [(c, c ^ 1) for c in range(lax.axis_size("col"))])


def per_device(
    patches, tissue, in_weight, conv_weight, conv_bias, x_weight, dt_weight, dt_bias,
    decay_rate, skip_gain, norm_gain, out_weight,
):
    tile_rows, tile_cols, channels = patches.shape
    inner = out_weight.shape[0]
    tokens = tile_rows * tile_cols
    row = lax.axis_index("row").astype(jnp.int32)
    col = lax.axis_index("col").astype(jnp.int32)
    place_r = jnp.stack([col, col, row])
    place_c = jnp.stack([col, row, col])
    top = shifted(patches[-1], "row", 1)
    bottom = shifted(patches[0], "row", -1)

    def edge(j):
        return jnp.concatenate([top[j : j + 1], patches[:, j], bottom[j : j + 1]], axis=0)

    left = shifted(edge(tile_cols - 1), "col", 1)
    right = shifted(edge(0), "col", -1)
    projected = jnp.dot(
        patches.reshape(tokens, channels), in_weight, preferred_element_type=F32
    ).astype(BF16)
    x_inner = projected[:, :inner]
    gate = projected[:, inner:]
    live = tissue.reshape(tokens, 1).astype(F32)
    rates = jnp.swapaxes(decay_rate, 1, 2)

    smem = [pl.BlockSpec(memory_space=pltpu.SMEM)]
    outs = call(
        local_kernel,
        (jax.ShapeDtypeStruct((tokens, inner), BF16),)
        + (jax.ShapeDtypeStruct((4, tokens, 2 * LANES), BF16),) * 2
        + (jax.ShapeDtypeStruct((16, tokens // 2, 3 * LANES), BF16),),
        smem + vmem(10),
        [
            pltpu.VMEM((10, 32, inner), F32),
            pltpu.VMEM((inner, 2 * LANES), BF16),
            pltpu.VMEM((8, tokens, LANES), BF16),
        ],
        name="local",
    )(
        place_r, x_inner, top, bottom, left, right, in_weight,
        conv_weight.reshape(9, inner), conv_bias.reshape(1, inner), x_weight, 1.0 - live,
    )
    act, near_r, far_r, rec_c = outs
    length = 8 * tokens
    wide = (length, LANES)


    def scratch(halves):
        return [
            pltpu.VMEM((2,) + wide, F32),
            pltpu.VMEM((2,) + wide, F32),
            pltpu.VMEM((2, length, halves * LANES), BF16),
        ]

    def totals(place, recs, copies, first, halves, name):
        return call(
            functools.partial(totals_kernel, len(recs), copies, first),
            (
                jax.ShapeDtypeStruct((2, STATE + 1, 8, LANES), F32),
                jax.ShapeDtypeStruct((copies, 3 * STATE, LANES), BF16),
                jax.ShapeDtypeStruct((2, TOT, LANES), F32),
                jax.ShapeDtypeStruct((2, halves * LANES, LANES), BF16),
            ),
            smem + vmem(len(recs) + 3),
            scratch(halves)
            + [
                pltpu.VMEM((2, halves * LANES, LANES), F32),
                pltpu.VMEM((halves * LANES, STATE * LANES), BF16),
                pltpu.VMEM((8 * BLOCK, STATE * LANES), F32),
            ],
            flops=10**9,
            grant=20,
            name=name,
        )(place, *recs, dt_weight, dt_bias, rates)

    def outputs(place, tot, excl, decay, rows, recs, out, halves, name):
        return call(
            functools.partial(outputs_kernel, len(recs), len(out)),
            out,
            smem + vmem(len(recs) + 4),
            scratch(halves)
            + [
                pltpu.VMEM((halves * LANES, 2 * STATE * LANES), BF16),
                pltpu.VMEM((8 * BLOCK, 2 * STATE * LANES), F32),
                pltpu.VMEM(wide, F32),
            ],
            flops=10**9,
            grant=24,
            name=name,
        )(place, tot, excl, decay, rows, *recs)

    rec_r = exchange(near_r, crossed(far_r))
    rec_c = lax.all_to_all(rec_c, "row", 0, 0).reshape(length, 3 * LANES)

    excl_r, tot_r, decay_r, rows_r = totals(place_r, rec_r, 16, 0, 1, "totals_rows")
    excl_c, tot_c, decay_c, rows_c = totals(place_c, [rec_c], 8, 2, 2, "totals_cols")

    tot_r = lax.all_to_all(tot_r, "row", 0, 0)
    tot_c = lax.all_to_all(tot_c, "col", 0, 0)

    near_y, far_y = outputs(
        place_r, tot_r, excl_r, decay_r, rows_r, rec_r,
        (jax.ShapeDtypeStruct((4, tokens, LANES), BF16),) * 2, 1, "outputs_rows",
    )
    (y_c,) = outputs(
        place_c, tot_c, excl_c, decay_c, rows_c, [rec_c],
        (jax.ShapeDtypeStruct(wide, BF16),), 2, "outputs_cols",
    )
    y_c, far_y = lax.optimization_barrier((y_c, crossed(far_y)))
    y_r = exchange(near_y, far_y)
    y_c = lax.all_to_all(y_c.reshape(16, tokens // 2, LANES), "row", 0, 0)

    result = call(
        final_kernel,
        jax.ShapeDtypeStruct((tokens, channels), BF16),
        smem + vmem(11),
        [pltpu.VMEM((8, tokens, LANES), BF16)],
        name="final",
    )(
        place_r, y_c, act, gate, skip_gain.reshape(1, inner), norm_gain.reshape(1, inner),
        out_weight, live, *y_r,
    )
    return result.reshape(tile_rows, tile_cols, channels)


def solution(mesh):
    in_specs = (P("row", "col", None), P("row", "col")) + (P(),) * 10
    return jax.shard_map(
        per_device, mesh=mesh, in_specs=in_specs, out_specs=P("row", "col", None), check_vma=False
    )
```

time: 111 us -> 104 us (0.937)
  starting transfers between devices: 59.9 us -> 50.2 us
  waiting for transfers between devices: 9.51 us -> 13.5 us
    ppermute x15 -> x8, starting transfers between devices: 19.8 us -> 9.52 us  [the longest x6 9.35 us: exchange(): lax.ppermute(m, 'col', [(c, (c + 2 * j) % count) for c in range(count)])]
    ppermute x15 -> x8, waiting for transfers between devices: 6.23 us -> 10.3 us  [the longest x6 8.73 us: exchange(): lax.ppermute(m, 'col', [(c, (c + 2 * j) % count) for c in range(count)])]
    all_to_all x2, starting transfers between devices: 14.6 us -> 16 us  [the longest x1 9.38 us: per_device(): rec_c = lax.all_to_all(rec_c, 'row', 0, 0).reshape(length, 3 * LANES)]
    pallas_call x4 -> x6, Pallas kernels: 30.8 us -> 29.5 us  [the longest x2 16.3 us: outputs(): call(functools.partial(outputs_kernel, len(recs), len(out)), out, smem +...]
  transfers between devices with their start and end apart: 23 -> 16, of which waited for: 9 -> 10; matrix products, arithmetic and copies ran while one was open for 3% -> 3% of each run, Pallas kernels for 20% -> 29%
where the time goes in v4:
time: 104 us; the launch traced here: 102 us
  starting transfers between devices  50.2 us (48%)
  Pallas kernels  34.3 us (33%)
  waiting for transfers between devices  13.5 us (13%)
  local copies, waits for them, and re-layouts  2.06 us (2%)
  matrix products  1.74 us (2%)
    pallas_call x2, Pallas kernels, outputs(): call(functools.partial(outputs_kernel, len(recs), len(out)), out, smem +...  16.3 us
    pallas_call x2, Pallas kernels, totals(): call(functools.partial(totals_kernel, len(recs), copies, first), (jax.Sha...  13.1 us
    ppermute x4, starting transfers between devices, shifted(): return lax.ppermute(values, axis, pairs)  12.3 us
    all_to_all x1, starting transfers between devices, per_device(): rec_c = lax.all_to_all(rec_c, 'row', 0, 0).reshape(length, 3 * LANES)  9.38 us
    ppermute x6, starting transfers between devices, exchange(): lax.ppermute(m, 'col', [(c, (c + 2 * j) % count) for c in range(count)])  9.35 us
    ppermute x6, waiting for transfers between devices, exchange(): lax.ppermute(m, 'col', [(c, (c + 2 * j) % count) for c in range(count)])  8.73 us
    all_to_all x1, starting transfers between devices, per_device(): tot_c = lax.all_to_all(tot_c, 'col', 0, 0)  6.65 us
    all_to_all x1, starting transfers between devices, per_device(): tot_r = lax.all_to_all(tot_r, 'row', 0, 0)  6.61 us
  transfers between devices with their start and end apart: 16, of which 10 were waited for; matrix products, arithmetic and copies ran while one was open for 3% of the time, Pallas kernels for 29%

profile of v4, /device:TPU:1, one launch (start us, length us, event | category | flops | bytes accessed | tf_op | source)
XLA Modules:
  0.0 102.3 jit_solution(16022837268041353352)
XLA Ops:
  0.7 4.0 %collective-permute-start = (bf16[16,384]{1,0:T(8,128)(2,1)S(1)}, bf16[16,384]{1,0:T(8,128)(2,1)S(1)}, u32[]{:S(2)}, u32[]{:S(2)}) collective-permute-start(bf16[16,384]{1,0:T(8,128)(2,1)S(1)} %get-tuple-element.58), channel_id=1, source_target_pairs={{0,8},{8,16},{16,24},{24,32},{32,40},{40,48},{48,56},{56,64},{64,7... | collective-permute-start | bytes 36872 | tf_op jit(solution)/shard_map/ppermute | solution.py:430
  4.8 1.3 %collective-permute-start.1 = (bf16[16,384]{1,0:T(8,128)(2,1)S(1)}, bf16[16,384]{1,0:T(8,128)(2,1)S(1)}, u32[]{:S(2)}, u32[]{:S(2)}) collective-permute-start(bf16[16,384]{1,0:T(8,128)(2,1)S(1)} %get-tuple-element.57), channel_id=1, source_target_pairs={{8,0},{16,8},{24,16},{32,24},{40,32},{48,40},{56,48},{64,56},{72,6... | collective-permute-start | bytes 36872 | tf_op jit(solution)/shard_map/ppermute | solution.py:430
  6.1 1.7 %convolution_convert_fusion = bf16[128,1536]{1,0:T(8,128)(2,1)S(1)} fusion(bf16[128,384]{1,0:T(8,128)(2,1)} %bitcast.23, bf16[384,1536]{1,0:T(8,128)(2,1)} %w_ref.2), kind=kOutput, calls=%fused_computation | convolution fusion | flops 151191552 | bytes 1671168 | tf_op jit(solution)/shard_map/dot_general | solution.py:471
  9.2 5.1 %collective-permute-start.2 = (bf16[10,384]{1,0:T(8,128)(2,1)S(1)}, bf16[10,384]{1,0:T(8,128)(2,1)S(1)}, u32[]{:S(2)}, u32[]{:S(2)}) collective-permute-start(bf16[10,384]{1,0:T(8,128)(2,1)S(1)} %pad_maximum_fusion), channel_id=1, source_target_pairs={{0,1},{1,2},{2,3},{3,4},{4,5},{5,6},{6,7},{8,9},{9,10},{10,11},{11... | collective-permute-start | bytes 23048 | tf_op jit(solution)/shard_map/ppermute | solution.py:430
  14.4 1.9 %collective-permute-start.3 = (bf16[10,384]{1,0:T(8,128)(2,1)S(1)}, bf16[10,384]{1,0:T(8,128)(2,1)S(1)}, u32[]{:S(2)}, u32[]{:S(2)}) collective-permute-start(bf16[10,384]{1,0:T(8,128)(2,1)S(1)} %pad_maximum_fusion.1), channel_id=1, source_target_pairs={{1,0},{2,1},{3,2},{4,3},{5,4},{6,5},{7,6},{9,8},{10,9},{11,10},{12... | collective-permute-start | bytes 23048 | tf_op jit(solution)/shard_map/ppermute | solution.py:430
  16.6 2.8 %collective-permute-done.3.right_ref = bf16[10,384]{1,0:T(8,128)(2,1)S(1)} collective-permute-done((bf16[10,384]{1,0:T(8,128)(2,1)S(1)}, bf16[10,384]{1,0:T(8,128)(2,1)S(1)}, u32[]{:S(2)}, u32[]{:S(2)}) %collective-permute-start.3) | collective-permute-done | bytes 7712 | tf_op jit(solution)/shard_map/ppermute | solution.py:430
  19.4 2.8 %local.1 = (bf16[128,768]{1,0:T(8,128)(2,1)S(1)}, bf16[4,128,256]{2,1,0:T(8,128)(2,1)S(1)}, bf16[4,128,256]{2,1,0:T(8,128)(2,1)S(1)}, bf16[16,64,384]{2,1,0:T(8,128)(2,1)}) custom-call(s32[3]{0:T(128)S(1)} %pad_add_fusion.place_ref, bf16[128,768]{1,0:T(8,128)(2,1)S(1)} %get-tuple-element.54.x_ref, bf16[16,384]{1,0:T(8,128)(2,1)S(1)} %collective-permute-done.top_ref, ...), custom_call_target="tpu_custom_call" | custom-call | flops 10000000 | bytes 4000000 | tf_op jit(solution)/shard_map/local/pallas_call | solution.py:480
  22.2 9.4 %all-to-all-start = ((bf16[16,64,384]{2,1,0:T(8,128)(2,1)}), bf16[16,64,384]{2,1,0:T(8,128)(2,1)S(1)}, u32[]{:S(2)}, u32[]{:S(2)}) async-start(bf16[16,64,384]{2,1,0:T(8,128)(2,1)} %get-tuple-element.29), calls=%async_computation | async-start | bytes 1572864 | tf_op jit(solution)/shard_map/all_to_all | solution.py:546
  31.7 1.5 %collective-permute-done.4.far_ref = bf16[4,128,256]{2,1,0:T(8,128)(2,1)S(1)} collective-permute-done((bf16[4,128,256]{2,1,0:T(8,128)(2,1)S(1)}, bf16[4,128,256]{2,1,0:T(8,128)(2,1)S(1)}, u32[]{:S(2)}, u32[]{:S(2)}) %collective-permute-start.4) | collective-permute-done | bytes 262176 | tf_op jit(solution)/shard_map/ppermute | solution.py:449
  34.5 1.3 %collective-permute-start.6 = (bf16[2,128,256]{2,1,0:T(8,128)(2,1)S(1)}, bf16[2,128,256]{2,1,0:T(8,128)(2,1)S(1)}, u32[]{:S(2)}, u32[]{:S(2)}) collective-permute-start(bf16[2,128,256]{2,1,0:T(8,128)(2,1)S(1)} %get-tuple-element.38), channel_id=1, source_target_pairs={{0,4},{1,5},{2,6},{3,7},{4,0},{5,1},{6,2},{7,3},{8,12},{9,13},{10,... | collective-permute-start | bytes 393224 | tf_op jit(solution)/shard_map/ppermute | solution.py:443
  35.9 2.0 %collective-permute-start.7 = (bf16[2,128,256]{2,1,0:T(8,128)(2,1)S(1)}, bf16[2,128,256]{2,1,0:T(8,128)(2,1)S(1)}, u32[]{:S(2)}, u32[]{:S(2)}) collective-permute-start(bf16[2,128,256]{2,1,0:T(8,128)(2,1)S(1)} %get-tuple-element.39), channel_id=1, source_target_pairs={{0,6},{1,7},{2,0},{3,1},{4,2},{5,3},{6,4},{7,5},{8,14},{9,15},{10,... | collective-permute-start | bytes 393224 | tf_op jit(solution)/shard_map/ppermute | solution.py:443
  37.9 2.1 %collective-permute-done.5.refs_1_ = bf16[2,128,256]{2,1,0:T(8,128)(2,1)S(1)} collective-permute-done((bf16[2,128,256]{2,1,0:T(8,128)(2,1)S(1)}, bf16[2,128,256]{2,1,0:T(8,128)(2,1)S(1)}, u32[]{:S(2)}, u32[]{:S(2)}) %collective-permute-start.5) | collective-permute-done | bytes 131104 | tf_op jit(solution)/shard_map/ppermute | solution.py:443
  39.9 2.0 %collective-permute-done.6.refs_2_ = bf16[2,128,256]{2,1,0:T(8,128)(2,1)S(1)} collective-permute-done((bf16[2,128,256]{2,1,0:T(8,128)(2,1)S(1)}, bf16[2,128,256]{2,1,0:T(8,128)(2,1)S(1)}, u32[]{:S(2)}, u32[]{:S(2)}) %collective-permute-start.6) | collective-permute-done | bytes 131104 | tf_op jit(solution)/shard_map/ppermute | solution.py:443
  42.6 6.2 %totals_rows.1 = (f32[2,17,8,128]{3,2,1,0:T(8,128)S(1)}, bf16[16,48,128]{2,1,0:T(8,128)(2,1)}, f32[2,24,128]{2,1,0:T(8,128)S(1)}, bf16[2,128,128]{2,1,0:T(8,128)(2,1)S(1)}) custom-call(s32[3]{0:T(128)S(1)} %pad_add_fusion.place_ref, bf16[2,128,256]{2,1,0:T(8,128)(2,1)S(1)} %get-tuple-element.36.refs_0_, ...), custom_call_target="tpu_custom_call" | custom-call | flops 1000000000 | bytes 4000000 | tf_op jit(solution)/shard_map/totals_rows/pallas_call | solution.py:509
  48.8 6.6 %all-to-all-start.2 = ((bf16[16,48,128]{2,1,0:T(8,128)(2,1)}), bf16[16,48,128]{2,1,0:T(8,128)(2,1)S(1)}, u32[]{:S(2)}, u32[]{:S(2)}) async-start(bf16[16,48,128]{2,1,0:T(8,128)(2,1)} %get-tuple-element.40), calls=%async_computation.2 | async-start | bytes 393216 | tf_op jit(solution)/shard_map/all_to_all | solution.py:551
  55.5 6.9 %totals_cols.1 = (f32[2,17,8,128]{3,2,1,0:T(8,128)S(1)}, bf16[8,48,128]{2,1,0:T(8,128)(2,1)}, f32[2,24,128]{2,1,0:T(8,128)S(1)}, bf16[2,256,128]{2,1,0:T(8,128)(2,1)S(1)}) custom-call(s32[3]{0:T(128)S(1)} %pad_add_fusion.1.place_ref, bf16[1024,384]{1,0:T(8,128)(2,1)S(1)} %bitcast.19, bf16[4,24,768]{2,1,0:T(8,128)(2,1)S(1)} %copy-done.3, ...), custom_call_target="tpu_custom_call" | custom-call | flops 1000000000 | bytes 4000000 | tf_op jit(solution)/shard_map/totals_cols/pallas_call | solution.py:509
  62.7 6.7 %all-to-all-start.1 = ((bf16[8,48,128]{2,1,0:T(8,128)(2,1)}), bf16[8,48,128]{2,1,0:T(8,128)(2,1)S(1)}, u32[]{:S(2)}, u32[]{:S(2)}) async-start(bf16[8,48,128]{2,1,0:T(8,128)(2,1)} %get-tuple-element.30), calls=%async_computation.1 | async-start | bytes 196608 | tf_op jit(solution)/shard_map/all_to_all | solution.py:552
  69.3 7.6 %outputs_rows.1 = (bf16[4,128,128]{2,1,0:T(8,128)(2,1)S(1)}, bf16[4,128,128]{2,1,0:T(8,128)(2,1)S(1)}) custom-call(s32[3]{0:T(128)S(1)} %pad_add_fusion.place_ref, bf16[16,48,128]{2,1,0:T(8,128)(2,1)S(1)} %all-to-all-done.2.gathered_ref, f32[2,17,8,128]{3,2,1,0:T(8,128)S(1)} %get-tuple-element.41.excl_ref, f32[2,24,128]{2,1,0:T(8,128)S(1)} %get-tuple-element.42.decay_ref, ...), custom_call_target="tpu_custom_call" | custom-call | flops 1000000000 | bytes 4000000 | tf_op jit(solution)/shard_map/outputs_rows/pallas_call | solution.py:530
  77.0 8.8 %outputs_cols.1 = bf16[1024,128]{1,0:T(8,128)(2,1)} custom-call(s32[3]{0:T(128)S(1)} %pad_add_fusion.1.place_ref, bf16[8,48,128]{2,1,0:T(8,128)(2,1)S(1)} %all-to-all-done.1.gathered_ref, f32[2,17,8,128]{3,2,1,0:T(8,128)S(1)} %get-tuple-element.31.excl_ref, f32[2,24,128]{2,1,0:T(8,128)S(1)} %get-tuple-element.32.decay_ref, ...), custom_call_target="tpu_custom_call" | custom-call | flops 1000000000 | bytes 4000000 | tf_op jit(solution)/shard_map/outputs_cols/pallas_call | solution.py:530
  85.8 5.7 %all-to-all-start.3 = ((bf16[16,64,128]{2,1,0:T(8,128)(2,1)}), bf16[16,64,128]{2,1,0:T(8,128)(2,1)S(1)}, u32[]{:S(2)}, u32[]{:S(2)}) async-start(bf16[16,64,128]{2,1,0:T(8,128)(2,1)} %bitcast.9), calls=%async_computation.3 | async-start | bytes 524288 | tf_op jit(solution)/shard_map/all_to_all | solution.py:564
  91.5 3.3 %collective-permute-start.10 = (bf16[2,128,128]{2,1,0:T(8,128)(2,1)S(1)}, bf16[2,128,128]{2,1,0:T(8,128)(2,1)S(1)}, u32[]{:S(2)}, u32[]{:S(2)}) collective-permute-start(bf16[2,128,128]{2,1,0:T(8,128)(2,1)S(1)} %get-tuple-element.51), channel_id=1, source_target_pairs={{0,4},{1,5},{2,6},{3,7},{4,0},{5,1},{6,2},{7,3},{8,12},{9,13},{10,... | collective-permute-start | bytes 196616 | tf_op jit(solution)/shard_map/ppermute | solution.py:443
  96.5 2.2 %collective-permute-done.11.refs_3_ = bf16[2,128,128]{2,1,0:T(8,128)(2,1)S(1)} collective-permute-done((bf16[2,128,128]{2,1,0:T(8,128)(2,1)S(1)}, bf16[2,128,128]{2,1,0:T(8,128)(2,1)S(1)}, u32[]{:S(2)}, u32[]{:S(2)}) %collective-permute-start.11) | collective-permute-done | bytes 65568 | tf_op jit(solution)/shard_map/ppermute | solution.py:443
  98.7 1.7 %collective-permute-done.9.refs_1_ = bf16[2,128,128]{2,1,0:T(8,128)(2,1)S(1)} collective-permute-done((bf16[2,128,128]{2,1,0:T(8,128)(2,1)S(1)}, bf16[2,128,128]{2,1,0:T(8,128)(2,1)S(1)}, u32[]{:S(2)}, u32[]{:S(2)}) %collective-permute-start.9) | collective-permute-done | bytes 65568 | tf_op jit(solution)/shard_map/ppermute | solution.py:443
  100.3 2.0 %final.1 = bf16[128,384]{1,0:T(8,128)(2,1)} custom-call(s32[3]{0:T(128)S(1)} %pad_add_fusion.place_ref, bf16[16,64,128]{2,1,0:T(8,128)(2,1)S(1)} %all-to-all-done.3.yc_ref, bf16[128,768]{1,0:T(8,128)(2,1)S(1)} %get-tuple-element.46.act_ref, bf16[128,768]{1,0:T(8,128)(2,1)S(1)} %get-tuple-element.53.gate_ref, f32[1,768]{1,0:T(1,128)S(1)} %reshape.51.skip_ref, ...), custom_call_target="tpu_custom_call" | custom-call | flops 10000000 | bytes 4000000 | tf_op jit(solution)/shard_map/final/pallas_call | solution.py:566
  (58 shorter events, 6.5 us)
Async XLA Ops:
  0.7 8.3 %collective-permute-start = (bf16[16,384]{1,0:T(8,128)(2,1)S(1)}, bf16[16,384]{1,0:T(8,128)(2,1)S(1)}, u32[]{:S(2)}, u32[]{:S(2)}) collective-permute-start(bf16[16,384]{1,0:T(8,128)(2,1)S(1)} %get-tuple-element.58), channel_id=1, source_target_pairs={{0,8},{8,16},{16,24},{24,32},{32,40},{40,48},{48,56},{56,64},{64,7... | collective-permute-start | bytes 36872 | tf_op jit(solution)/shard_map/ppermute | solution.py:430
  4.8 4.4 %collective-permute-start.1 = (bf16[16,384]{1,0:T(8,128)(2,1)S(1)}, bf16[16,384]{1,0:T(8,128)(2,1)S(1)}, u32[]{:S(2)}, u32[]{:S(2)}) collective-permute-start(bf16[16,384]{1,0:T(8,128)(2,1)S(1)} %get-tuple-element.57), channel_id=1, source_target_pairs={{8,0},{16,8},{24,16},{32,24},{40,32},{48,40},{56,48},{64,56},{72,6... | collective-permute-start | bytes 36872 | tf_op jit(solution)/shard_map/ppermute | solution.py:430
  6.1 10.3 %copy-start.5 = (bf16[768,224]{0,1:T(8,128)(2,1)S(1)}, bf16[768,224]{0,1:T(8,128)(2,1)}, u32[]{:S(2)}) copy-start(bf16[768,224]{0,1:T(8,128)(2,1)} %param.17) | copy-start | bytes 1032196
  7.8 11.5 %copy-start = (bf16[384,1536]{1,0:T(8,128)(2,1)S(1)}, bf16[384,1536]{1,0:T(8,128)(2,1)}, u32[]{:S(2)}) copy-start(bf16[384,1536]{1,0:T(8,128)(2,1)} %w_ref.2) | copy-start | bytes 3538948
  9.2 7.4 %collective-permute-start.2 = (bf16[10,384]{1,0:T(8,128)(2,1)S(1)}, bf16[10,384]{1,0:T(8,128)(2,1)S(1)}, u32[]{:S(2)}, u32[]{:S(2)}) collective-permute-start(bf16[10,384]{1,0:T(8,128)(2,1)S(1)} %pad_maximum_fusion), channel_id=1, source_target_pairs={{0,1},{1,2},{2,3},{3,4},{4,5},{5,6},{6,7},{8,9},{9,10},{10,11},{11... | collective-permute-start | bytes 23048 | tf_op jit(solution)/shard_map/ppermute | solution.py:430
  14.4 5.0 %collective-permute-start.3 = (bf16[10,384]{1,0:T(8,128)(2,1)S(1)}, bf16[10,384]{1,0:T(8,128)(2,1)S(1)}, u32[]{:S(2)}, u32[]{:S(2)}) collective-permute-start(bf16[10,384]{1,0:T(8,128)(2,1)S(1)} %pad_maximum_fusion.1), channel_id=1, source_target_pairs={{1,0},{2,1},{3,2},{4,3},{5,4},{6,5},{7,6},{9,8},{10,9},{11,10},{12... | collective-permute-start | bytes 23048 | tf_op jit(solution)/shard_map/ppermute | solution.py:430
  22.2 20.4 %copy-start.2 = (f32[4,768,16]{1,2,0:T(8,128)S(1)}, f32[4,768,16]{1,2,0:T(8,128)}, u32[]{:S(2)}) copy-start(f32[4,768,16]{1,2,0:T(8,128)} %param.20) | copy-start | bytes 589828
  22.2 20.4 %copy-start.3 = (bf16[4,24,768]{2,1,0:T(8,128)(2,1)S(1)}, bf16[4,24,768]{2,1,0:T(8,128)(2,1)}, u32[]{:S(2)}) copy-start(bf16[4,24,768]{2,1,0:T(8,128)(2,1)} %refs_4_.1) | copy-start | bytes 442372
  22.2 20.4 %copy-start.4 = (f32[4,768]{1,0:T(4,128)S(1)}, f32[4,768]{1,0:T(4,128)}, u32[]{:S(2)}) copy-start(f32[4,768]{1,0:T(4,128)} %refs_5_.1) | copy-start | bytes 36868
  22.2 26.5 %all-to-all-start = ((bf16[16,64,384]{2,1,0:T(8,128)(2,1)}), bf16[16,64,384]{2,1,0:T(8,128)(2,1)S(1)}, u32[]{:S(2)}, u32[]{:S(2)}) async-start(bf16[16,64,384]{2,1,0:T(8,128)(2,1)} %get-tuple-element.29), calls=%async_computation | async-start | bytes 1572864 | tf_op jit(solution)/shard_map/all_to_all | solution.py:546
  31.6 1.6 %collective-permute-start.4 = (bf16[4,128,256]{2,1,0:T(8,128)(2,1)S(1)}, bf16[4,128,256]{2,1,0:T(8,128)(2,1)S(1)}, u32[]{:S(2)}, u32[]{:S(2)}) collective-permute-start(bf16[4,128,256]{2,1,0:T(8,128)(2,1)S(1)} %get-tuple-element.35), channel_id=1, source_target_pairs={{0,1},{1,0},{2,3},{3,2},{4,5},{5,4},{6,7},{7,6},{8,9},{9,8},{10,11... | collective-permute-start | bytes 786440 | tf_op jit(solution)/shard_map/ppermute | solution.py:449
  33.3 6.6 %collective-permute-start.5 = (bf16[2,128,256]{2,1,0:T(8,128)(2,1)S(1)}, bf16[2,128,256]{2,1,0:T(8,128)(2,1)S(1)}, u32[]{:S(2)}, u32[]{:S(2)}) collective-permute-start(bf16[2,128,256]{2,1,0:T(8,128)(2,1)S(1)} %get-tuple-element.37), channel_id=1, source_target_pairs={{0,2},{1,3},{2,4},{3,5},{4,6},{5,7},{6,0},{7,1},{8,10},{9,11},{10,... | collective-permute-start | bytes 393224 | tf_op jit(solution)/shard_map/ppermute | solution.py:443
  34.5 7.4 %collective-permute-start.6 = (bf16[2,128,256]{2,1,0:T(8,128)(2,1)S(1)}, bf16[2,128,256]{2,1,0:T(8,128)(2,1)S(1)}, u32[]{:S(2)}, u32[]{:S(2)}) collective-permute-start(bf16[2,128,256]{2,1,0:T(8,128)(2,1)S(1)} %get-tuple-element.38), channel_id=1, source_target_pairs={{0,4},{1,5},{2,6},{3,7},{4,0},{5,1},{6,2},{7,3},{8,12},{9,13},{10,... | collective-permute-start | bytes 393224 | tf_op jit(solution)/shard_map/ppermute | solution.py:443
  35.9 6.7 %collective-permute-start.7 = (bf16[2,128,256]{2,1,0:T(8,128)(2,1)S(1)}, bf16[2,128,256]{2,1,0:T(8,128)(2,1)S(1)}, u32[]{:S(2)}, u32[]{:S(2)}) collective-permute-start(bf16[2,128,256]{2,1,0:T(8,128)(2,1)S(1)} %get-tuple-element.39), channel_id=1, source_target_pairs={{0,6},{1,7},{2,0},{3,1},{4,2},{5,3},{6,4},{7,5},{8,14},{9,15},{10,... | collective-permute-start | bytes 393224 | tf_op jit(solution)/shard_map/ppermute | solution.py:443
  48.8 13.9 %all-to-all-start.2 = ((bf16[16,48,128]{2,1,0:T(8,128)(2,1)}), bf16[16,48,128]{2,1,0:T(8,128)(2,1)S(1)}, u32[]{:S(2)}, u32[]{:S(2)}) async-start(bf16[16,48,128]{2,1,0:T(8,128)(2,1)} %get-tuple-element.40), calls=%async_computation.2 | async-start | bytes 393216 | tf_op jit(solution)/shard_map/all_to_all | solution.py:551
  62.7 14.3 %all-to-all-start.1 = ((bf16[8,48,128]{2,1,0:T(8,128)(2,1)}), bf16[8,48,128]{2,1,0:T(8,128)(2,1)S(1)}, u32[]{:S(2)}, u32[]{:S(2)}) async-start(bf16[8,48,128]{2,1,0:T(8,128)(2,1)} %get-tuple-element.30), calls=%async_computation.1 | async-start | bytes 196608 | tf_op jit(solution)/shard_map/all_to_all | solution.py:552
  76.9 8.9 %collective-permute-start.8 = (bf16[4,128,128]{2,1,0:T(8,128)(2,1)S(1)}, bf16[4,128,128]{2,1,0:T(8,128)(2,1)S(1)}, u32[]{:S(2)}, u32[]{:S(2)}) collective-permute-start(bf16[4,128,128]{2,1,0:T(8,128)(2,1)S(1)} %get-tuple-element.44), channel_id=1, source_target_pairs={{0,1},{1,0},{2,3},{3,2},{4,5},{5,4},{6,7},{7,6},{8,9},{9,8},{10,11... | collective-permute-start | bytes 393224 | tf_op jit(solution)/shard_map/ppermute | solution.py:449
  77.0 19.3 %copy-start.8 = (f32[768]{0:T(1024)S(1)}, f32[768]{0:T(1024)}, u32[]{:S(2)}) copy-start(f32[768]{0:T(1024)} %param.21) | copy-start | bytes 9220
  77.0 19.3 %copy-start.9 = (f32[768]{0:T(1024)S(1)}, f32[768]{0:T(1024)}, u32[]{:S(2)}) copy-start(f32[768]{0:T(1024)} %param.22) | copy-start | bytes 9220
  85.8 14.6 %copy-start.1 = (bf16[768,384]{1,0:T(8,128)(2,1)S(1)}, bf16[768,384]{1,0:T(8,128)(2,1)}, u32[]{:S(2)}) copy-start(bf16[768,384]{1,0:T(8,128)(2,1)} %w_ref.3) | copy-start | bytes 1769476
  85.8 14.6 %all-to-all-start.3 = ((bf16[16,64,128]{2,1,0:T(8,128)(2,1)}), bf16[16,64,128]{2,1,0:T(8,128)(2,1)S(1)}, u32[]{:S(2)}, u32[]{:S(2)}) async-start(bf16[16,64,128]{2,1,0:T(8,128)(2,1)} %bitcast.9), calls=%async_computation.3 | async-start | bytes 524288 | tf_op jit(solution)/shard_map/all_to_all | solution.py:564
  91.5 4.9 %collective-permute-start.10 = (bf16[2,128,128]{2,1,0:T(8,128)(2,1)S(1)}, bf16[2,128,128]{2,1,0:T(8,128)(2,1)S(1)}, u32[]{:S(2)}, u32[]{:S(2)}) collective-permute-start(bf16[2,128,128]{2,1,0:T(8,128)(2,1)S(1)} %get-tuple-element.51), channel_id=1, source_target_pairs={{0,4},{1,5},{2,6},{3,7},{4,0},{5,1},{6,2},{7,3},{8,12},{9,13},{10,... | collective-permute-start | bytes 196616 | tf_op jit(solution)/shard_map/ppermute | solution.py:443
  94.8 3.8 %collective-permute-start.11 = (bf16[2,128,128]{2,1,0:T(8,128)(2,1)S(1)}, bf16[2,128,128]{2,1,0:T(8,128)(2,1)S(1)}, u32[]{:S(2)}, u32[]{:S(2)}) collective-permute-start(bf16[2,128,128]{2,1,0:T(8,128)(2,1)S(1)} %get-tuple-element.52), channel_id=1, source_target_pairs={{0,6},{1,7},{2,0},{3,1},{4,2},{5,3},{6,4},{7,5},{8,14},{9,15},{10,... | collective-permute-start | bytes 196616 | tf_op jit(solution)/shard_map/ppermute | solution.py:443
  95.7 4.6 %collective-permute-start.9 = (bf16[2,128,128]{2,1,0:T(8,128)(2,1)S(1)}, bf16[2,128,128]{2,1,0:T(8,128)(2,1)S(1)}, u32[]{:S(2)}, u32[]{:S(2)}) collective-permute-start(bf16[2,128,128]{2,1,0:T(8,128)(2,1)S(1)} %get-tuple-element.50), channel_id=1, source_target_pairs={{0,2},{1,3},{2,4},{3,5},{4,6},{5,7},{6,0},{7,1},{8,10},{9,11},{10,... | collective-permute-start | bytes 196616 | tf_op jit(solution)/shard_map/ppermute | solution.py:443
  (3 other events, 19.3 us)

commit v5 on v4

--- a/solution.py
+++ b/solution.py
@@ -132,7 +132,7 @@
 
 
 def local_kernel(
-    place_ref, x_ref, top_ref, bottom_ref, left_ref, right_ref, w_ref, cw_ref, cb_ref, xw_ref, off_ref,
+    place_ref, x_ref, row_near_ref, row_away_ref, col_near_ref, col_away_ref, w_ref, cw_ref, cb_ref, xw_ref, off_ref,
     *rest,
 ):
     act_ref, near_ref, far_ref, recc_ref, frame_ref, xwide_ref, slices_ref = rest
@@ -143,10 +143,12 @@
         return jnp.dot(v, weight, preferred_element_type=F32).astype(BF16).astype(F32)
 
     frame_ref[1:9, 8:24, :] = x_ref[...].astype(F32).reshape(8, 16, inner)
-    frame_ref[0:1, 8:24, :] = project(top_ref[...]).reshape(1, 16, inner)
-    frame_ref[9:10, 8:24, :] = project(bottom_ref[...]).reshape(1, 16, inner)
-    left = project(left_ref[...])
-    right = project(right_ref[...])
+    rows = (project(row_near_ref[...]), project(row_away_ref[...]))
+    top, bottom = before_after(rows, (place_ref[2] & 1) == 0)
+    frame_ref[0:1, 8:24, :] = top.reshape(1, 16, inner)
+    frame_ref[9:10, 8:24, :] = bottom.reshape(1, 16, inner)
+    cols = (project(col_near_ref[...]), project(col_away_ref[...]))
+    left, right = before_after(cols, (place_ref[0] & 1) == 0)
     for i in range(10):
         frame_ref[i, 7:8, :] = left[i : i + 1]
         frame_ref[i, 24:25, :] = right[i : i + 1]
@@ -424,10 +426,19 @@
     ).astype(BF16)
 
 
-def shifted(values, axis, step):
+def swapped(low, high, axis):
     count = lax.axis_size(axis)
-    pairs = [(i, i + step) for i in range(count) if 0 <= i + step < count]
-    return lax.ppermute(values, axis, pairs)
+    even = lax.axis_index(axis) % 2 == 0
+    inner = [(i, i ^ 1) for i in range(count)]
+    outer = [(i + d, i + 1 - d) for i in range(1, count - 1, 2) for d in range(2)]
+    near = lax.ppermute(jnp.where(even, high, low), axis, inner)
+    away = lax.ppermute(jnp.where(even, low, high), axis, outer)
+    return near, away
+
+
+def before_after(pair, even):
+    near, away = pair
+    return jnp.where(even, away, near), jnp.where(even, near, away)
 
 
 def exchange(near, far):
@@ -460,14 +471,13 @@
     col = lax.axis_index("col").astype(jnp.int32)
     place_r = jnp.stack([col, col, row])
     place_c = jnp.stack([col, row, col])
-    top = shifted(patches[-1], "row", 1)
-    bottom = shifted(patches[0], "row", -1)
+    row_pair = swapped(patches[0], patches[-1], "row")
+    top, bottom = before_after(row_pair, row % 2 == 0)
 
     def edge(j):
         return jnp.concatenate([top[j : j + 1], patches[:, j], bottom[j : j + 1]], axis=0)
 
-    left = shifted(edge(tile_cols - 1), "col", 1)
-    right = shifted(edge(0), "col", -1)
+    col_pair = swapped(edge(0), edge(tile_cols - 1), "col")
     projected = jnp.dot(
         patches.reshape(tokens, channels), in_weight, preferred_element_type=F32
     ).astype(BF16)
@@ -490,7 +500,7 @@
         ],
         name="local",
     )(
-        place_r, x_inner, top, bottom, left, right, in_weight,
+        place_r, x_inner, *row_pair, *col_pair, in_weight,
         conv_weight.reshape(9, inner), conv_bias.reshape(1, inner), x_weight, 1.0 - live,
     )
     act, near_r, far_r, rec_c = outs

time: 104 us -> 98.9 us (0.951)
  starting transfers between devices: 50.2 us -> 46.7 us
  waiting for transfers between devices: 13.5 us -> 12.2 us
    ppermute x4, starting transfers between devices: 12.3 us -> 6.83 us  [the longest x2 3.67 us: swapped(): away = lax.ppermute(jnp.where(even, low, high), axis, outer)]
    all_to_all x1, starting transfers between devices: 9.38 us -> 10.9 us  [per_device(): rec_c = lax.all_to_all(rec_c, 'row', 0, 0).reshape(length, 3 * LANES)]
    ppermute x4, waiting for transfers between devices: 2.93 us -> 1.66 us  [the longest x2 1.65 us: swapped(): away = lax.ppermute(jnp.where(even, low, high), axis, outer)]
  transfers between devices with their start and end apart: 16 -> 16, of which waited for: 10 -> 8; matrix products, arithmetic and copies ran while one was open for 3% -> 3% of each run, Pallas kernels for 29% -> 30%
where the time goes in v5:
time: 98.9 us; the launch traced here: 97.5 us
  starting transfers between devices  46.7 us (47%)
  Pallas kernels  34.3 us (35%)
  waiting for transfers between devices  12.2 us (12%)
  matrix products  1.74 us (2%)
  local copies, waits for them, and re-layouts  1.23 us (1%)
    pallas_call x2, Pallas kernels, outputs(): call(functools.partial(outputs_kernel, len(recs), len(out)), out, smem +...  16.3 us
    pallas_call x2, Pallas kernels, totals(): call(functools.partial(totals_kernel, len(recs), copies, first), (jax.Sha...  13.1 us
    all_to_all x1, starting transfers between devices, per_device(): rec_c = lax.all_to_all(rec_c, 'row', 0, 0).reshape(length, 3 * LANES)  10.9 us
    ppermute x6, starting transfers between devices, exchange(): lax.ppermute(m, 'col', [(c, (c + 2 * j) % count) for c in range(count)])  9.64 us
    ppermute x6, waiting for transfers between devices, exchange(): lax.ppermute(m, 'col', [(c, (c + 2 * j) % count) for c in range(count)])  8.85 us
    all_to_all x1, starting transfers between devices, per_device(): tot_r = lax.all_to_all(tot_r, 'row', 0, 0)  6.89 us
    all_to_all x1, starting transfers between devices, per_device(): tot_c = lax.all_to_all(tot_c, 'col', 0, 0)  6.54 us
    all_to_all x1, starting transfers between devices, per_device(): y_c = lax.all_to_all(y_c.reshape(16, tokens // 2, LANES), 'row', 0, 0)  5.72 us
  transfers between devices with their start and end apart: 16, of which 8 were waited for; matrix products, arithmetic and copies ran while one was open for 3% of the time, Pallas kernels for 30%

profile of v5, /device:TPU:1, one launch (start us, length us, event | category | flops | bytes accessed | tf_op | source)
XLA Modules:
  0.0 97.5 jit_solution(2943223480419214673)
XLA Ops:
  0.7 2.1 %collective-permute-start = (bf16[16,384]{1,0:T(8,128)(2,1)S(1)}, bf16[16,384]{1,0:T(8,128)(2,1)S(1)}, u32[]{:S(2)}, u32[]{:S(2)}) collective-permute-start(bf16[16,384]{1,0:T(8,128)(2,1)S(1)} %get-tuple-element.58), channel_id=1, source_target_pairs={{0,8},{8,0},{16,24},{24,16},{32,40},{40,32},{48,56},{56,48},{64,72... | collective-permute-start | bytes 36872 | tf_op jit(solution)/shard_map/ppermute | solution.py:434
  4.4 1.7 %convolution_convert_fusion = bf16[128,1536]{1,0:T(8,128)(2,1)S(1)} fusion(bf16[128,384]{1,0:T(8,128)(2,1)} %bitcast.21, bf16[384,1536]{1,0:T(8,128)(2,1)} %w_ref.2), kind=kOutput, calls=%fused_computation | convolution fusion | flops 151191552 | bytes 1671168 | tf_op jit(solution)/shard_map/dot_general | solution.py:481
  6.4 1.0 %collective-permute-start.2 = (bf16[10,384]{1,0:T(8,128)(2,1)S(1)}, bf16[10,384]{1,0:T(8,128)(2,1)S(1)}, u32[]{:S(2)}, u32[]{:S(2)}) collective-permute-start(bf16[10,384]{1,0:T(8,128)(2,1)S(1)} %get-tuple-element.62), channel_id=1, source_target_pairs={{0,1},{1,0},{2,3},{3,2},{4,5},{5,4},{6,7},{7,6},{8,9},{9,8},{10,11... | collective-permute-start | bytes 23048 | tf_op jit(solution)/shard_map/ppermute | solution.py:434
  7.5 3.0 %collective-permute-start.3 = (bf16[10,384]{1,0:T(8,128)(2,1)S(1)}, bf16[10,384]{1,0:T(8,128)(2,1)S(1)}, u32[]{:S(2)}, u32[]{:S(2)}) collective-permute-start(bf16[10,384]{1,0:T(8,128)(2,1)S(1)} %get-tuple-element.61), channel_id=1, source_target_pairs={{1,2},{2,1},{3,4},{4,3},{5,6},{6,5},{9,10},{10,9},{11,12},{12,11},... | collective-permute-start | bytes 23048 | tf_op jit(solution)/shard_map/ppermute | solution.py:435
  10.8 1.7 %collective-permute-done.3.col_away_ref = bf16[10,384]{1,0:T(8,128)(2,1)S(1)} collective-permute-done((bf16[10,384]{1,0:T(8,128)(2,1)S(1)}, bf16[10,384]{1,0:T(8,128)(2,1)S(1)}, u32[]{:S(2)}, u32[]{:S(2)}) %collective-permute-start.3) | collective-permute-done | bytes 7712 | tf_op jit(solution)/shard_map/ppermute | solution.py:435
  12.5 2.9 %local.1 = (bf16[128,768]{1,0:T(8,128)(2,1)S(1)}, bf16[4,128,256]{2,1,0:T(8,128)(2,1)S(1)}, bf16[4,128,256]{2,1,0:T(8,128)(2,1)S(1)}, bf16[16,64,384]{2,1,0:T(8,128)(2,1)}) custom-call(s32[3]{0:T(128)S(1)} %pad_add_fusion.place_ref, bf16[128,768]{1,0:T(8,128)(2,1)S(1)} %get-tuple-element.54.x_ref, bf16[16,384]{1,0:T(8,128)(2,1)S(1)} %collective-permute-done.row_near_ref, ...), custom_call_target="tpu_custom_call" | custom-call | flops 10000000 | bytes 4000000 | tf_op jit(solution)/shard_map/local/pallas_call | solution.py:490
  15.4 10.9 %all-to-all-start = ((bf16[16,64,384]{2,1,0:T(8,128)(2,1)}), bf16[16,64,384]{2,1,0:T(8,128)(2,1)S(1)}, u32[]{:S(2)}, u32[]{:S(2)}) async-start(bf16[16,64,384]{2,1,0:T(8,128)(2,1)} %get-tuple-element.29), calls=%async_computation | async-start | bytes 1572864 | tf_op jit(solution)/shard_map/all_to_all | solution.py:556
  26.4 1.5 %collective-permute-done.4.far_ref = bf16[4,128,256]{2,1,0:T(8,128)(2,1)S(1)} collective-permute-done((bf16[4,128,256]{2,1,0:T(8,128)(2,1)S(1)}, bf16[4,128,256]{2,1,0:T(8,128)(2,1)S(1)}, u32[]{:S(2)}, u32[]{:S(2)}) %collective-permute-start.4) | collective-permute-done | bytes 262176 | tf_op jit(solution)/shard_map/ppermute | solution.py:460
  27.9 1.3 %collective-permute-start.5 = (bf16[2,128,256]{2,1,0:T(8,128)(2,1)S(1)}, bf16[2,128,256]{2,1,0:T(8,128)(2,1)S(1)}, u32[]{:S(2)}, u32[]{:S(2)}) collective-permute-start(bf16[2,128,256]{2,1,0:T(8,128)(2,1)S(1)} %get-tuple-element.37), channel_id=1, source_target_pairs={{0,2},{1,3},{2,4},{3,5},{4,6},{5,7},{6,0},{7,1},{8,10},{9,11},{10,... | collective-permute-start | bytes 393224 | tf_op jit(solution)/shard_map/ppermute | solution.py:454
  29.2 2.4 %collective-permute-start.6 = (bf16[2,128,256]{2,1,0:T(8,128)(2,1)S(1)}, bf16[2,128,256]{2,1,0:T(8,128)(2,1)S(1)}, u32[]{:S(2)}, u32[]{:S(2)}) collective-permute-start(bf16[2,128,256]{2,1,0:T(8,128)(2,1)S(1)} %get-tuple-element.38), channel_id=1, source_target_pairs={{0,4},{1,5},{2,6},{3,7},{4,0},{5,1},{6,2},{7,3},{8,12},{9,13},{10,... | collective-permute-start | bytes 393224 | tf_op jit(solution)/shard_map/ppermute | solution.py:454
  31.6 1.2 %collective-permute-start.7 = (bf16[2,128,256]{2,1,0:T(8,128)(2,1)S(1)}, bf16[2,128,256]{2,1,0:T(8,128)(2,1)S(1)}, u32[]{:S(2)}, u32[]{:S(2)}) collective-permute-start(bf16[2,128,256]{2,1,0:T(8,128)(2,1)S(1)} %get-tuple-element.39), channel_id=1, source_target_pairs={{0,6},{1,7},{2,0},{3,1},{4,2},{5,3},{6,4},{7,5},{8,14},{9,15},{10,... | collective-permute-start | bytes 393224 | tf_op jit(solution)/shard_map/ppermute | solution.py:454
  32.8 1.3 %collective-permute-done.5.refs_1_ = bf16[2,128,256]{2,1,0:T(8,128)(2,1)S(1)} collective-permute-done((bf16[2,128,256]{2,1,0:T(8,128)(2,1)S(1)}, bf16[2,128,256]{2,1,0:T(8,128)(2,1)S(1)}, u32[]{:S(2)}, u32[]{:S(2)}) %collective-permute-start.5) | collective-permute-done | bytes 131104 | tf_op jit(solution)/shard_map/ppermute | solution.py:454
  34.2 3.5 %collective-permute-done.6.refs_2_ = bf16[2,128,256]{2,1,0:T(8,128)(2,1)S(1)} collective-permute-done((bf16[2,128,256]{2,1,0:T(8,128)(2,1)S(1)}, bf16[2,128,256]{2,1,0:T(8,128)(2,1)S(1)}, u32[]{:S(2)}, u32[]{:S(2)}) %collective-permute-start.6) | collective-permute-done | bytes 131104 | tf_op jit(solution)/shard_map/ppermute | solution.py:454
  37.7 6.2 %totals_rows.1 = (f32[2,17,8,128]{3,2,1,0:T(8,128)S(1)}, bf16[16,48,128]{2,1,0:T(8,128)(2,1)}, f32[2,24,128]{2,1,0:T(8,128)S(1)}, bf16[2,128,128]{2,1,0:T(8,128)(2,1)S(1)}) custom-call(s32[3]{0:T(128)S(1)} %pad_add_fusion.place_ref, bf16[2,128,256]{2,1,0:T(8,128)(2,1)S(1)} %get-tuple-element.36.refs_0_, ...), custom_call_target="tpu_custom_call" | custom-call | flops 1000000000 | bytes 4000000 | tf_op jit(solution)/shard_map/totals_rows/pallas_call | solution.py:519
  43.9 6.9 %all-to-all-start.2 = ((bf16[16,48,128]{2,1,0:T(8,128)(2,1)}), bf16[16,48,128]{2,1,0:T(8,128)(2,1)S(1)}, u32[]{:S(2)}, u32[]{:S(2)}) async-start(bf16[16,48,128]{2,1,0:T(8,128)(2,1)} %get-tuple-element.40), calls=%async_computation.2 | async-start | bytes 393216 | tf_op jit(solution)/shard_map/all_to_all | solution.py:561
  50.8 6.9 %totals_cols.1 = (f32[2,17,8,128]{3,2,1,0:T(8,128)S(1)}, bf16[8,48,128]{2,1,0:T(8,128)(2,1)}, f32[2,24,128]{2,1,0:T(8,128)S(1)}, bf16[2,256,128]{2,1,0:T(8,128)(2,1)S(1)}) custom-call(s32[3]{0:T(128)S(1)} %pad_add_fusion.1.place_ref, bf16[1024,384]{1,0:T(8,128)(2,1)S(1)} %bitcast.17, bf16[4,24,768]{2,1,0:T(8,128)(2,1)S(1)} %copy-done.3, ...), custom_call_target="tpu_custom_call" | custom-call | flops 1000000000 | bytes 4000000 | tf_op jit(solution)/shard_map/totals_cols/pallas_call | solution.py:519
  57.9 6.5 %all-to-all-start.1 = ((bf16[8,48,128]{2,1,0:T(8,128)(2,1)}), bf16[8,48,128]{2,1,0:T(8,128)(2,1)S(1)}, u32[]{:S(2)}, u32[]{:S(2)}) async-start(bf16[8,48,128]{2,1,0:T(8,128)(2,1)} %get-tuple-element.30), calls=%async_computation.1 | async-start | bytes 196608 | tf_op jit(solution)/shard_map/all_to_all | solution.py:562
  64.5 7.6 %outputs_rows.1 = (bf16[4,128,128]{2,1,0:T(8,128)(2,1)S(1)}, bf16[4,128,128]{2,1,0:T(8,128)(2,1)S(1)}) custom-call(s32[3]{0:T(128)S(1)} %pad_add_fusion.place_ref, bf16[16,48,128]{2,1,0:T(8,128)(2,1)S(1)} %all-to-all-done.2.gathered_ref, f32[2,17,8,128]{3,2,1,0:T(8,128)S(1)} %get-tuple-element.41.excl_ref, f32[2,24,128]{2,1,0:T(8,128)S(1)} %get-tuple-element.42.decay_ref, ...), custom_call_target="tpu_custom_call" | custom-call | flops 1000000000 | bytes 4000000 | tf_op jit(solution)/shard_map/outputs_rows/pallas_call | solution.py:540
  72.2 8.8 %outputs_cols.1 = bf16[1024,128]{1,0:T(8,128)(2,1)} custom-call(s32[3]{0:T(128)S(1)} %pad_add_fusion.1.place_ref, bf16[8,48,128]{2,1,0:T(8,128)(2,1)S(1)} %all-to-all-done.1.gathered_ref, f32[2,17,8,128]{3,2,1,0:T(8,128)S(1)} %get-tuple-element.31.excl_ref, f32[2,24,128]{2,1,0:T(8,128)S(1)} %get-tuple-element.32.decay_ref, ...), custom_call_target="tpu_custom_call" | custom-call | flops 1000000000 | bytes 4000000 | tf_op jit(solution)/shard_map/outputs_cols/pallas_call | solution.py:540
  80.9 5.7 %all-to-all-start.3 = ((bf16[16,64,128]{2,1,0:T(8,128)(2,1)}), bf16[16,64,128]{2,1,0:T(8,128)(2,1)S(1)}, u32[]{:S(2)}, u32[]{:S(2)}) async-start(bf16[16,64,128]{2,1,0:T(8,128)(2,1)} %bitcast.9), calls=%async_computation.3 | async-start | bytes 524288 | tf_op jit(solution)/shard_map/all_to_all | solution.py:574
  86.7 3.3 %collective-permute-start.10 = (bf16[2,128,128]{2,1,0:T(8,128)(2,1)S(1)}, bf16[2,128,128]{2,1,0:T(8,128)(2,1)S(1)}, u32[]{:S(2)}, u32[]{:S(2)}) collective-permute-start(bf16[2,128,128]{2,1,0:T(8,128)(2,1)S(1)} %get-tuple-element.51), channel_id=1, source_target_pairs={{0,4},{1,5},{2,6},{3,7},{4,0},{5,1},{6,2},{7,3},{8,12},{9,13},{10,... | collective-permute-start | bytes 196616 | tf_op jit(solution)/shard_map/ppermute | solution.py:454
  91.7 2.2 %collective-permute-done.11.refs_3_ = bf16[2,128,128]{2,1,0:T(8,128)(2,1)S(1)} collective-permute-done((bf16[2,128,128]{2,1,0:T(8,128)(2,1)S(1)}, bf16[2,128,128]{2,1,0:T(8,128)(2,1)S(1)}, u32[]{:S(2)}, u32[]{:S(2)}) %collective-permute-start.11) | collective-permute-done | bytes 65568 | tf_op jit(solution)/shard_map/ppermute | solution.py:454
  93.8 1.7 %collective-permute-done.9.refs_1_ = bf16[2,128,128]{2,1,0:T(8,128)(2,1)S(1)} collective-permute-done((bf16[2,128,128]{2,1,0:T(8,128)(2,1)S(1)}, bf16[2,128,128]{2,1,0:T(8,128)(2,1)S(1)}, u32[]{:S(2)}, u32[]{:S(2)}) %collective-permute-start.9) | collective-permute-done | bytes 65568 | tf_op jit(solution)/shard_map/ppermute | solution.py:454
  95.5 2.0 %final.1 = bf16[128,384]{1,0:T(8,128)(2,1)} custom-call(s32[3]{0:T(128)S(1)} %pad_add_fusion.place_ref, bf16[16,64,128]{2,1,0:T(8,128)(2,1)S(1)} %all-to-all-done.3.yc_ref, bf16[128,768]{1,0:T(8,128)(2,1)S(1)} %get-tuple-element.46.act_ref, bf16[128,768]{1,0:T(8,128)(2,1)S(1)} %get-tuple-element.53.gate_ref, f32[1,768]{1,0:T(1,128)S(1)} %reshape.55.skip_ref, ...), custom_call_target="tpu_custom_call" | custom-call | flops 10000000 | bytes 4000000 | tf_op jit(solution)/shard_map/final/pallas_call | solution.py:576
  (56 shorter events, 4.9 us)
Async XLA Ops:
  0.7 5.6 %collective-permute-start = (bf16[16,384]{1,0:T(8,128)(2,1)S(1)}, bf16[16,384]{1,0:T(8,128)(2,1)S(1)}, u32[]{:S(2)}, u32[]{:S(2)}) collective-permute-start(bf16[16,384]{1,0:T(8,128)(2,1)S(1)} %get-tuple-element.58), channel_id=1, source_target_pairs={{0,8},{8,0},{16,24},{24,16},{32,40},{40,32},{48,56},{56,48},{64,72... | collective-permute-start | bytes 36872 | tf_op jit(solution)/shard_map/ppermute | solution.py:434
  2.9 3.5 %collective-permute-start.1 = (bf16[16,384]{1,0:T(8,128)(2,1)S(1)}, bf16[16,384]{1,0:T(8,128)(2,1)S(1)}, u32[]{:S(2)}, u32[]{:S(2)}) collective-permute-start(bf16[16,384]{1,0:T(8,128)(2,1)S(1)} %get-tuple-element.57), channel_id=1, source_target_pairs={{8,16},{16,8},{24,32},{32,24},{40,48},{48,40},{56,64},{64,56},{72,... | collective-permute-start | bytes 36872 | tf_op jit(solution)/shard_map/ppermute | solution.py:435
  4.4 6.2 %copy-start.5 = (bf16[768,224]{0,1:T(8,128)(2,1)S(1)}, bf16[768,224]{0,1:T(8,128)(2,1)}, u32[]{:S(2)}) copy-start(bf16[768,224]{0,1:T(8,128)(2,1)} %param.17) | copy-start | bytes 1032196
  6.2 6.3 %copy-start = (bf16[384,1536]{1,0:T(8,128)(2,1)S(1)}, bf16[384,1536]{1,0:T(8,128)(2,1)}, u32[]{:S(2)}) copy-start(bf16[384,1536]{1,0:T(8,128)(2,1)} %w_ref.2) | copy-start | bytes 3538948
  6.4 4.4 %collective-permute-start.2 = (bf16[10,384]{1,0:T(8,128)(2,1)S(1)}, bf16[10,384]{1,0:T(8,128)(2,1)S(1)}, u32[]{:S(2)}, u32[]{:S(2)}) collective-permute-start(bf16[10,384]{1,0:T(8,128)(2,1)S(1)} %get-tuple-element.62), channel_id=1, source_target_pairs={{0,1},{1,0},{2,3},{3,2},{4,5},{5,4},{6,7},{7,6},{8,9},{9,8},{10,11... | collective-permute-start | bytes 23048 | tf_op jit(solution)/shard_map/ppermute | solution.py:434
  7.5 5.0 %collective-permute-start.3 = (bf16[10,384]{1,0:T(8,128)(2,1)S(1)}, bf16[10,384]{1,0:T(8,128)(2,1)S(1)}, u32[]{:S(2)}, u32[]{:S(2)}) collective-permute-start(bf16[10,384]{1,0:T(8,128)(2,1)S(1)} %get-tuple-element.61), channel_id=1, source_target_pairs={{1,2},{2,1},{3,4},{4,3},{5,6},{6,5},{9,10},{10,9},{11,12},{12,11},... | collective-permute-start | bytes 23048 | tf_op jit(solution)/shard_map/ppermute | solution.py:435
  15.4 22.3 %copy-start.2 = (f32[4,768,16]{1,2,0:T(8,128)S(1)}, f32[4,768,16]{1,2,0:T(8,128)}, u32[]{:S(2)}) copy-start(f32[4,768,16]{1,2,0:T(8,128)} %param.20) | copy-start | bytes 589828
  15.4 22.3 %copy-start.3 = (bf16[4,24,768]{2,1,0:T(8,128)(2,1)S(1)}, bf16[4,24,768]{2,1,0:T(8,128)(2,1)}, u32[]{:S(2)}) copy-start(bf16[4,24,768]{2,1,0:T(8,128)(2,1)} %refs_4_.1) | copy-start | bytes 442372
  15.4 22.3 %copy-start.4 = (f32[4,768]{1,0:T(4,128)S(1)}, f32[4,768]{1,0:T(4,128)}, u32[]{:S(2)}) copy-start(f32[4,768]{1,0:T(4,128)} %refs_5_.1) | copy-start | bytes 36868
  15.4 28.5 %all-to-all-start = ((bf16[16,64,384]{2,1,0:T(8,128)(2,1)}), bf16[16,64,384]{2,1,0:T(8,128)(2,1)S(1)}, u32[]{:S(2)}, u32[]{:S(2)}) async-start(bf16[16,64,384]{2,1,0:T(8,128)(2,1)} %get-tuple-element.29), calls=%async_computation | async-start | bytes 1572864 | tf_op jit(solution)/shard_map/all_to_all | solution.py:556
  26.3 1.6 %collective-permute-start.4 = (bf16[4,128,256]{2,1,0:T(8,128)(2,1)S(1)}, bf16[4,128,256]{2,1,0:T(8,128)(2,1)S(1)}, u32[]{:S(2)}, u32[]{:S(2)}) collective-permute-start(bf16[4,128,256]{2,1,0:T(8,128)(2,1)S(1)} %get-tuple-element.35), channel_id=1, source_target_pairs={{0,1},{1,0},{2,3},{3,2},{4,5},{5,4},{6,7},{7,6},{8,9},{9,8},{10,11... | collective-permute-start | bytes 786440 | tf_op jit(solution)/shard_map/ppermute | solution.py:460
  27.9 6.2 %collective-permute-start.5 = (bf16[2,128,256]{2,1,0:T(8,128)(2,1)S(1)}, bf16[2,128,256]{2,1,0:T(8,128)(2,1)S(1)}, u32[]{:S(2)}, u32[]{:S(2)}) collective-permute-start(bf16[2,128,256]{2,1,0:T(8,128)(2,1)S(1)} %get-tuple-element.37), channel_id=1, source_target_pairs={{0,2},{1,3},{2,4},{3,5},{4,6},{5,7},{6,0},{7,1},{8,10},{9,11},{10,... | collective-permute-start | bytes 393224 | tf_op jit(solution)/shard_map/ppermute | solution.py:454
  29.2 8.4 %collective-permute-start.6 = (bf16[2,128,256]{2,1,0:T(8,128)(2,1)S(1)}, bf16[2,128,256]{2,1,0:T(8,128)(2,1)S(1)}, u32[]{:S(2)}, u32[]{:S(2)}) collective-permute-start(bf16[2,128,256]{2,1,0:T(8,128)(2,1)S(1)} %get-tuple-element.38), channel_id=1, source_target_pairs={{0,4},{1,5},{2,6},{3,7},{4,0},{5,1},{6,2},{7,3},{8,12},{9,13},{10,... | collective-permute-start | bytes 393224 | tf_op jit(solution)/shard_map/ppermute | solution.py:454
  31.6 6.1 %collective-permute-start.7 = (bf16[2,128,256]{2,1,0:T(8,128)(2,1)S(1)}, bf16[2,128,256]{2,1,0:T(8,128)(2,1)S(1)}, u32[]{:S(2)}, u32[]{:S(2)}) collective-permute-start(bf16[2,128,256]{2,1,0:T(8,128)(2,1)S(1)} %get-tuple-element.39), channel_id=1, source_target_pairs={{0,6},{1,7},{2,0},{3,1},{4,2},{5,3},{6,4},{7,5},{8,14},{9,15},{10,... | collective-permute-start | bytes 393224 | tf_op jit(solution)/shard_map/ppermute | solution.py:454
  43.9 14.1 %all-to-all-start.2 = ((bf16[16,48,128]{2,1,0:T(8,128)(2,1)}), bf16[16,48,128]{2,1,0:T(8,128)(2,1)S(1)}, u32[]{:S(2)}, u32[]{:S(2)}) async-start(bf16[16,48,128]{2,1,0:T(8,128)(2,1)} %get-tuple-element.40), calls=%async_computation.2 | async-start | bytes 393216 | tf_op jit(solution)/shard_map/all_to_all | solution.py:561
  57.9 14.2 %all-to-all-start.1 = ((bf16[8,48,128]{2,1,0:T(8,128)(2,1)}), bf16[8,48,128]{2,1,0:T(8,128)(2,1)S(1)}, u32[]{:S(2)}, u32[]{:S(2)}) async-start(bf16[8,48,128]{2,1,0:T(8,128)(2,1)} %get-tuple-element.30), calls=%async_computation.1 | async-start | bytes 196608 | tf_op jit(solution)/shard_map/all_to_all | solution.py:562
  72.1 8.9 %collective-permute-start.8 = (bf16[4,128,128]{2,1,0:T(8,128)(2,1)S(1)}, bf16[4,128,128]{2,1,0:T(8,128)(2,1)S(1)}, u32[]{:S(2)}, u32[]{:S(2)}) collective-permute-start(bf16[4,128,128]{2,1,0:T(8,128)(2,1)S(1)} %get-tuple-element.44), channel_id=1, source_target_pairs={{0,1},{1,0},{2,3},{3,2},{4,5},{5,4},{6,7},{7,6},{8,9},{9,8},{10,11... | collective-permute-start | bytes 393224 | tf_op jit(solution)/shard_map/ppermute | solution.py:460
  72.2 19.3 %copy-start.8 = (f32[768]{0:T(1024)S(1)}, f32[768]{0:T(1024)}, u32[]{:S(2)}) copy-start(f32[768]{0:T(1024)} %param.21) | copy-start | bytes 9220
  72.2 19.3 %copy-start.9 = (f32[768]{0:T(1024)S(1)}, f32[768]{0:T(1024)}, u32[]{:S(2)}) copy-start(f32[768]{0:T(1024)} %param.22) | copy-start | bytes 9220
  80.9 14.6 %copy-start.1 = (bf16[768,384]{1,0:T(8,128)(2,1)S(1)}, bf16[768,384]{1,0:T(8,128)(2,1)}, u32[]{:S(2)}) copy-start(bf16[768,384]{1,0:T(8,128)(2,1)} %w_ref.3) | copy-start | bytes 1769476
  80.9 14.6 %all-to-all-start.3 = ((bf16[16,64,128]{2,1,0:T(8,128)(2,1)}), bf16[16,64,128]{2,1,0:T(8,128)(2,1)S(1)}, u32[]{:S(2)}, u32[]{:S(2)}) async-start(bf16[16,64,128]{2,1,0:T(8,128)(2,1)} %bitcast.9), calls=%async_computation.3 | async-start | bytes 524288 | tf_op jit(solution)/shard_map/all_to_all | solution.py:574
  86.7 4.9 %collective-permute-start.10 = (bf16[2,128,128]{2,1,0:T(8,128)(2,1)S(1)}, bf16[2,128,128]{2,1,0:T(8,128)(2,1)S(1)}, u32[]{:S(2)}, u32[]{:S(2)}) collective-permute-start(bf16[2,128,128]{2,1,0:T(8,128)(2,1)S(1)} %get-tuple-element.51), channel_id=1, source_target_pairs={{0,4},{1,5},{2,6},{3,7},{4,0},{5,1},{6,2},{7,3},{8,12},{9,13},{10,... | collective-permute-start | bytes 196616 | tf_op jit(solution)/shard_map/ppermute | solution.py:454
  90.0 3.8 %collective-permute-start.11 = (bf16[2,128,128]{2,1,0:T(8,128)(2,1)S(1)}, bf16[2,128,128]{2,1,0:T(8,128)(2,1)S(1)}, u32[]{:S(2)}, u32[]{:S(2)}) collective-permute-start(bf16[2,128,128]{2,1,0:T(8,128)(2,1)S(1)} %get-tuple-element.52), channel_id=1, source_target_pairs={{0,6},{1,7},{2,0},{3,1},{4,2},{5,3},{6,4},{7,5},{8,14},{9,15},{10,... | collective-permute-start | bytes 196616 | tf_op jit(solution)/shard_map/ppermute | solution.py:454
  90.9 4.6 %collective-permute-start.9 = (bf16[2,128,128]{2,1,0:T(8,128)(2,1)S(1)}, bf16[2,128,128]{2,1,0:T(8,128)(2,1)S(1)}, u32[]{:S(2)}, u32[]{:S(2)}) collective-permute-start(bf16[2,128,128]{2,1,0:T(8,128)(2,1)S(1)} %get-tuple-element.50), channel_id=1, source_target_pairs={{0,2},{1,3},{2,4},{3,5},{4,6},{5,7},{6,0},{7,1},{8,10},{9,11},{10,... | collective-permute-start | bytes 196616 | tf_op jit(solution)/shard_map/ppermute | solution.py:454
  (3 other events, 11.1 us)
